TPU v7x, 32 devices: a whole 2x2x4 slice. The times are simulated.
32 devices in a mesh: ctx: 8 (over z, x), head: 4 (over y, core).
Axes of the slice: x: 2, y: 2, z: 4, core: 2. Of those that a mesh axis runs over, the one named last changes fastest.
Arguments:
- inputs: bfloat16 [2048, 8192], P('ctx', 'head'), may hold values from -6 to 6
- grad_out: bfloat16 [2048, 8192], P('ctx', 'head'), may hold values from -18 to 18
- b_proj: bfloat16 [2048, 128], P('ctx'), may hold values from -0.25 to 0.25
- c_proj: bfloat16 [2048, 128], P('ctx'), may hold values from -0.25 to 0.25
- log_decay: float32 [128, 2048], P('head', 'ctx'), may hold values from -1 to 0, as said below
Outputs:
- grad_x: bfloat16 [2048, 8192], P('ctx', 'head')
- grad_b: float32 [2048, 128], P(('ctx', 'head'))
- grad_c: float32 [2048, 128], P(('ctx', 'head'))
- grad_decay: float32 [128, 2048], P('head', 'ctx')
Inputs may be any that keep to these rules, and one draw needn't show every extreme that they name: `log_decay`: log of a decay factor, negative.
All inputs are finite; a program needn't handle non-finite values.
Results may differ from a plain program's by a relative error of at most 0.0057.
Values sent between devices are 32-bit elements; how exact they have to be, the bound alone decides.
No kernel may reach another device: no remote copies, remote signals or barrier semaphores. Data moves between devices by JAX's collectives and lax.ppermute only.
A program may use at most 384 MiB of HBM per device.

v0:
```python
import jax
import jax.numpy as jnp
from jax import lax
from jax.sharding import PartitionSpec as P

HEAD_DIM = 64
STATE = 128
SPAN = 128


HIGHEST = lax.Precision.HIGHEST


def entering(value, axis, join, neutral, backward):
    count, mine = (lax.axis_size(axis), lax.axis_index(axis))
    pieces = jax.tree.map(lambda part: lax.all_gather(part, axis), value)
    if backward:
        pieces = jax.tree.map(lambda part: part[::-1], pieces)
        mine = count - 1 - mine
    subtotal = jax.tree.map(
        lambda part, zero: jnp.full_like(part, 0) + jnp.asarray(zero, part.dtype), value, neutral
    )

    def hop(position, subtotal):
        longer = join(subtotal, jax.tree.map(lambda part: part[position], pieces))
        return jax.tree.map(lambda new, old: jnp.where(position < mine, new, old), longer, subtotal)

    return lax.fori_loop(0, count - 1, hop, subtotal)


def decay_factors(decay_rows, b_rows, c_rows):
    running = jnp.cumsum(decay_rows, axis=1)
    totals = running[:, -1]
    into_end = jnp.exp(totals[:, None] - running)
    from_start = jnp.exp(running)
    b_decayed = (into_end[:, :, None] * b_rows.astype(jnp.float32)[None]).astype(jnp.bfloat16)
    c_decayed = (from_start[:, :, None] * c_rows.astype(jnp.float32)[None]).astype(jnp.bfloat16)
    return (totals, running, into_end, from_start, b_decayed, c_decayed)


def mask_table(running):
    length = running.shape[1]
    lower_mask = (jnp.arange(length)[:, None] >= jnp.arange(length)[None, :])[None]
    spread = jnp.where(lower_mask, running[:, :, None] - running[:, None, :], 0.0)
    return jnp.where(lower_mask, jnp.exp(spread), 0.0)


def combine_links(earlier, later):
    return (earlier[0] * later[0], later[0][:, None, None] * earlier[1] + later[1])


def shards(inputs, grad_out, b_proj, c_proj, log_decay):
    tok_rows = inputs.shape[0]
    head_count = log_decay.shape[0]
    x_view = inputs.reshape(tok_rows, head_count, HEAD_DIM)
    dy_view = grad_out.reshape(tok_rows, head_count, HEAD_DIM)
    blocks = tok_rows // SPAN
    saved = []
    intra_b = []
    intra_c = []
    for number in range(blocks):
        first_row = number * SPAN
        x_block = x_view[first_row : first_row + SPAN]
        dy_block = dy_view[first_row : first_row + SPAN]
        b_block = b_proj[first_row : first_row + SPAN]
        c_block = c_proj[first_row : first_row + SPAN]
        decay_rows = log_decay[:, first_row : first_row + SPAN]
        totals, running, into_end, from_start, b_decayed, c_decayed = decay_factors(
            decay_rows, b_block, c_block
        )
        mask_decay = mask_table(running)
        scores = jnp.dot(c_block, b_block.T, preferred_element_type=jnp.float32)
        forward_w = (mask_decay * scores[None]).astype(jnp.bfloat16)
        y_intra = jnp.einsum("hij,jhp->ihp", forward_w, x_block, preferred_element_type=jnp.float32)
        dx_intra = jnp.einsum(
            "hij,ihp->jhp", forward_w, dy_block, preferred_element_type=jnp.float32
        )
        pair_grad = jnp.einsum(
            "ihp,jhp->hij", dy_block, x_block, preferred_element_type=jnp.float32
        )
        weight_grad = (mask_decay * pair_grad).astype(jnp.bfloat16)
        summed = jnp.sum(weight_grad, axis=0, dtype=jnp.float32)
        intra_c.append(jnp.dot(summed, b_block.astype(jnp.float32), precision=HIGHEST))
        intra_b.append(jnp.dot(summed.T, c_block.astype(jnp.float32), precision=HIGHEST))
        state_local = jnp.einsum(
            "jhp,hjn->hpn", x_block, b_decayed, preferred_element_type=jnp.float32
        )
        adjoint_local = jnp.einsum(
            "ihp,hin->hpn", dy_block, c_decayed, preferred_element_type=jnp.float32
        )
        saved.append(
            (
                totals,
                into_end,
                from_start,
                b_decayed,
                c_decayed,
                y_intra,
                dx_intra,
                state_local,
                adjoint_local,
                x_block,
                dy_block,
            )
        )
    zero_state = jnp.zeros((head_count, HEAD_DIM, STATE), jnp.float32)
    forward_run = zero_state
    decay_run = jnp.ones((head_count,), jnp.float32)
    start_local = []
    before_decay = []
    for number in range(blocks):
        start_local.append(forward_run)
        before_decay.append(decay_run)
        block_decay = jnp.exp(saved[number][0])
        forward_run = block_decay[:, None, None] * forward_run + saved[number][7]
        decay_run = decay_run * block_decay
    backward_run = zero_state
    decay_back = jnp.ones((head_count,), jnp.float32)
    end_local = [zero_state] * blocks
    after_decay = [decay_back] * blocks
    for number in reversed(range(blocks)):
        end_local[number] = backward_run
        after_decay[number] = decay_back
        block_decay = jnp.exp(saved[number][0])
        backward_run = block_decay[:, None, None] * backward_run + saved[number][8]
        decay_back = decay_back * block_decay
    identity = (jnp.ones((head_count,), jnp.float32), zero_state)
    prior_decay, state_in = entering(
        (decay_run, forward_run), "ctx", combine_links, identity, False
    )
    later_decay, adjoint_out = entering(
        (decay_run, backward_run), "ctx", combine_links, identity, True
    )
    dx_parts = []
    changes = []
    inter_b = []
    inter_c = []
    for number in range(blocks):
        (
            totals,
            into_end,
            from_start,
            b_decayed,
            c_decayed,
            y_intra,
            dx_intra,
            state_local,
            adjoint_local,
            x_block,
            dy_block,
        ) = saved[number]
        start = start_local[number] + before_decay[number][:, None, None] * state_in
        finish = end_local[number] + after_decay[number][:, None, None] * adjoint_out
        x_wide = x_block.astype(jnp.float32)
        dy_wide = dy_block.astype(jnp.float32)
        outputs_y = y_intra + jnp.einsum(
            "hin,hpn->ihp", c_decayed.astype(jnp.float32), start, precision=HIGHEST
        )
        grad_full = dx_intra + jnp.einsum(
            "hjn,hpn->jhp", b_decayed.astype(jnp.float32), finish, precision=HIGHEST
        )
        dy_scaled = dy_wide * from_start.T[:, :, None]
        x_scaled = x_wide * into_end.T[:, :, None]
        inter_c.append(jnp.einsum("ihp,hpn->in", dy_scaled, start, precision=HIGHEST))
        inter_b.append(jnp.einsum("jhp,hpn->jn", x_scaled, finish, precision=HIGHEST))
        changes.append(
            jnp.einsum("ihp,ihp->hi", dy_wide, outputs_y)
            - jnp.einsum("jhp,jhp->hj", x_wide, grad_full)
        )
        dx_parts.append(grad_full)
    grad_x = (
        jnp.concatenate(dx_parts, axis=0)
        .reshape(tok_rows, head_count * HEAD_DIM)
        .astype(jnp.bfloat16)
    )
    change_all = jnp.concatenate(changes, axis=1)
    local_suffix = jnp.flip(jnp.cumsum(jnp.flip(change_all, 1), axis=1), 1)
    state_end = decay_run[:, None, None] * state_in + forward_run
    later_sum = jnp.sum(state_end * adjoint_out, axis=(1, 2))
    grad_decay = local_suffix + later_sum[:, None]
    total_b = jnp.concatenate(intra_b, axis=0) + jnp.concatenate(inter_b, axis=0)
    total_c = jnp.concatenate(intra_c, axis=0) + jnp.concatenate(inter_c, axis=0)
    grad_b, grad_c = (
        lax.psum_scatter(total_b, "head", scatter_dimension=0, tiled=True),
        lax.psum_scatter(total_c, "head", scatter_dimension=0, tiled=True),
    )
    return (grad_x, grad_b, grad_c, grad_decay)


def solution(mesh):
    placed = (P("ctx", "head"), P("ctx", "head"), P("ctx", None), P("ctx", None), P("head", "ctx"))
    return jax.shard_map(
        shards,
        mesh=mesh,
        in_specs=placed,
        out_specs=(
            P("ctx", "head"),
            P(("ctx", "head"), None),
            P(("ctx", "head"), None),
            P("head", "ctx"),
        ),
        check_vma=False,
    )
```

profile of v0, /device:TPU:0, one launch (start us, length us, event | category | flops | bytes accessed | tf_op | source)
XLA Modules:
  0.0 347.9 jit_solution(5633826469627760647)
XLA Ops:
  13.3 1.9 fusion.19
  16.1 1.6 fusion.17
  17.7 2.6 fusion.13
  23.9 24.5 %all-reduce = f32[256]{0:T(256)} all-reduce(f32[256]{0:T(256)} %dynamic-update-slice), channel_id=2, replica_groups=mesh['ctx'=8,'head'=4] {'ctx'}, use_global_device_ids=true, to_apply=%add | all-reduce | flops 256 | bytes 2048
  51.2 2.2 convert_reduce_fusion
  57.9 1.9 convolution_bitcast_fusion.1
  59.9 1.9 convolution_bitcast_fusion.3
  61.8 1.9 convolution_bitcast_fusion
  63.7 1.9 convolution_bitcast_fusion.2
  65.6 78.1 %all-gather.6.cloned.1.call-done = f32[256,64,128]{2,1,0:T(8,128)} async-done(((f32[32,64,128]{2,1,0:T(8,128)}), f32[256,64,128]{2,1,0:T(8,128)}) %all-gather.6.cloned.1.call-update) | async-done | bytes 8388624 | tf_op jit(solution)/shard_map/all_gather | solution.py:16
  143.7 8.4 %rev.14 = f32[8,32,64,128]{3,2,1,0:T(8,128)} reverse(f32[8,32,64,128]{3,2,1,0:T(8,128)} %bitcast.154), dimensions={0} | reverse | bytes 16777216 | tf_op jit(solution)/shard_map/rev | solution.py:18
  152.1 15.2 %while.28 = (s32[]{:T(128)}, f32[32,64,128]{2,1,0:T(8,128)S(1)}, s32[]{:T(128)}, f32[8,32]{1,0:T(8,128)}, f32[8,32,64,128]{3,2,1,0:T(8,128)}, /*index=5*/s32[]{:T(128)}, s32[]{:T(128)}) while((s32[]{:T(128)}, f32[32,64,128]{2,1,0:T(8,128)S(1)}, s32[]{:T(128)}, f32[8,32]{1,0:T(8,128)}, f32[8,32,64,128]{3,2,1,0:T(8,128)}, ...), condition=%wide.region_3.4_spmd.clone, body=%wide.region_2.3_spmd.clone.sunk | while | flops 1048580 | bytes 3146217 | solution.py:28
  167.3 4.2 %fusion.82 = (bf16[128,32,64]{0,2,1:T(8,128)(2,1)}, f32[128,32,64]{0,2,1:T(8,128)S(1)}) fusion(f32[128,32,64]{0,2,1:T(8,128)} %convolution_bitcast_fusion.1, f32[128,128]{1,0:T(8,128)S(1)} %get-tuple-element.269, f32[32,128]{1,0:T(8,128)S(1)} %copy-done.22, f32[32,64,128]{2,1,0:T(8,128)S(1)} %fusion.25, f32[32,64,128]{2,1,0:T(8,128)S(1)} %get-tuple-element.192, ...), kind=kOutput, calls=%fused_computation.135 | convolution fusion | flops 404750336 | bytes 4800640 | tf_op jit(solution)/shard_map/hjn,hpn->jhp/dot_general | solution.py:159
  171.7 97.2 %all-gather.8.cloned.1.call-done = f32[256,64,128]{2,1,0:T(8,128)} async-done(((f32[32,64,128]{2,1,0:T(8,128)}), f32[256,64,128]{2,1,0:T(8,128)}) %all-gather.8.cloned.1.call-update) | async-done | bytes 8388624 | tf_op jit(solution)/shard_map/all_gather | solution.py:16
  268.9 15.1 %while.29 = (s32[]{:T(128)}, f32[32,64,128]{2,1,0:T(8,128)S(1)}, s32[]{:T(128)}, f32[8,32]{1,0:T(8,128)}, f32[8,32,64,128]{3,2,1,0:T(8,128)}, /*index=5*/s32[]{:T(128)}, s32[]{:T(128)}) while((s32[]{:T(128)}, f32[32,64,128]{2,1,0:T(8,128)S(1)}, s32[]{:T(128)}, f32[8,32]{1,0:T(8,128)}, f32[8,32,64,128]{3,2,1,0:T(8,128)}, ...), condition=%wide.region_8.9_spmd.clone, body=%wide.region_7.8_spmd.clone.sunk | while | flops 1048580 | bytes 3146217 | solution.py:28
  284.1 4.4 %fusion.81 = (bf16[128,32,64]{0,2,1:T(8,128)(2,1)}, f32[128,32,64]{0,2,1:T(8,128)S(1)}) fusion(f32[128,32,64]{0,2,1:T(8,128)} %convolution_bitcast_fusion, f32[32,64,128]{2,1,0:T(8,128)S(1)} %get-tuple-element.192, f32[128,128]{1,0:T(8,128)S(1)} %get-tuple-element.270, f32[32,128]{1,0:T(8,128)S(1)} %get-tuple-element.291), kind=kOutput, calls=%fused_computation.134 | convolution fusion | flops 404226048 | bytes 3751936 | tf_op jit(solution)/shard_map/hjn,hpn->jhp/dot_general | solution.py:159
  288.8 2.4 fusion.31
  291.2 2.3 fusion.30
  294.8 3.4 convolution_bitcast_fusion.4
  298.3 1.8 convolution_bitcast_fusion.5
  300.9 3.1 convolution_bitcast_fusion.7
  304.0 1.8 convolution_bitcast_fusion.6
  310.7 8.0 %reduce-scatter.5.cloned.1.call-done = f32[64,128]{1,0:T(8,128)} async-done(((f32[256,128]{1,0:T(8,128)}), f32[64,128]{1,0:T(8,128)}) %reduce-scatter.5.cloned.1.call-update) | async-done | bytes 32784 | tf_op jit(solution)/shard_map/reduce_scatter | solution.py:185
  318.7 22.6 %reduce-scatter.3.cloned.1.call-done = f32[64,128]{1,0:T(8,128)} async-done(((f32[256,128]{1,0:T(8,128)}), f32[64,128]{1,0:T(8,128)}) %reduce-scatter.3.cloned.1.call-update) | async-done | bytes 32784 | tf_op jit(solution)/shard_map/reduce_scatter | solution.py:184
  (169 shorter events, 54.5 us)
Async XLA Ops:
  7.2 4.9 %copy-start.21 = (bf16[256,128]{1,0:T(8,128)(2,1)S(1)}, bf16[256,128]{1,0:T(8,128)(2,1)}, u32[]{:S(2)}) copy-start(bf16[256,128]{1,0:T(8,128)(2,1)} %param.12) | copy-start | bytes 196612
  7.2 136.5 %all-gather.6.cloned.1.call-start = ((), (), s32[]{:S(2)}) async-start(), calls=%async_computation.4 | async-start | bytes 9437184 | tf_op jit(solution)/shard_map/all_gather | solution.py:16
  8.2 4.1 %copy-start.33 = (f32[32,128]{1,0:T(8,128)}, f32[32,128]{1,0:T(8,128)S(1)}, u32[]{:S(2)}) copy-start(f32[32,128]{1,0:T(8,128)S(1)} %reduce_window_sum.32) | copy-start | bytes 49156
  15.2 253.7 %all-gather.8.cloned.1.call-start = ((), (), s32[]{:S(2)}) async-start(), calls=%async_computation.5 | async-start | bytes 9437184 | tf_op jit(solution)/shard_map/all_gather | solution.py:16
  15.7 4.6 %copy-start.7 = (bf16[128,2048]{0,1:T(8,128)(2,1)}, bf16[128,2048]{0,1:T(8,128)(2,1)S(1)}, u32[]{:S(2)}) copy-start(bf16[128,2048]{0,1:T(8,128)(2,1)S(1)} %copy.23) | copy-start | bytes 1572868
  16.1 4.2 %copy-start.3 = (bf16[128,2048]{0,1:T(8,128)(2,1)}, bf16[128,2048]{0,1:T(8,128)(2,1)S(1)}, u32[]{:S(2)}) copy-start(bf16[128,2048]{0,1:T(8,128)(2,1)S(1)} %copy.24) | copy-start | bytes 1572868
  20.3 298.5 %reduce-scatter.5.cloned.1.call-start = ((), (), s32[]{:S(2)}) async-start(), calls=%async_computation.3 | async-start | bytes 163840 | tf_op jit(solution)/shard_map/reduce_scatter | solution.py:185
  51.2 4.0 %copy-start.8 = (bf16[128,2048]{0,1:T(8,128)(2,1)S(1)}, bf16[128,2048]{0,1:T(8,128)(2,1)}, u32[]{:S(2)}) copy-start(bf16[128,2048]{0,1:T(8,128)(2,1)} %copy-done.7) | copy-start | bytes 1572868
  51.2 4.0 %copy-start.11 = (bf16[128,2048]{0,1:T(8,128)(2,1)S(1)}, bf16[128,2048]{0,1:T(8,128)(2,1)}, u32[]{:S(2)}) copy-start(bf16[128,2048]{0,1:T(8,128)(2,1)} %copy-done.10) | copy-start | bytes 1572868
  152.1 15.2 %copy-start.22 = (f32[32,128]{1,0:T(8,128)S(1)}, f32[32,128]{1,0:T(8,128)}, u32[]{:S(2)}) copy-start(f32[32,128]{1,0:T(8,128)} %get-tuple-element.276) | copy-start | bytes 49156
  152.1 15.2 %copy-start.37 = (f32[32]{0:T(128)S(1)}, f32[32]{0:T(128)}, u32[]{:S(2)}) copy-start(f32[32]{0:T(128)} %get-tuple-element.283) | copy-start | bytes 388
  167.3 4.2 %copy-start.9 = (bf16[128,2048]{0,1:T(8,128)(2,1)S(1)}, bf16[128,2048]{0,1:T(8,128)(2,1)}, u32[]{:S(2)}) copy-start(bf16[128,2048]{0,1:T(8,128)(2,1)} %copy-done.7) | copy-start | bytes 1572868
  284.0 4.5 %copy-start.5 = (bf16[128,2048]{0,1:T(8,128)(2,1)S(1)}, bf16[128,2048]{0,1:T(8,128)(2,1)}, u32[]{:S(2)}) copy-start(bf16[128,2048]{0,1:T(8,128)(2,1)} %copy-done.3) | copy-start | bytes 1572868
  284.0 4.7 %copy-start.12 = (bf16[128,2048]{0,1:T(8,128)(2,1)S(1)}, bf16[128,2048]{0,1:T(8,128)(2,1)}, u32[]{:S(2)}) copy-start(bf16[128,2048]{0,1:T(8,128)(2,1)} %copy-done.10) | copy-start | bytes 1572868
  284.0 4.7 %copy-start.19 = (f32[128,32,64]{0,2,1:T(8,128)S(1)}, f32[128,32,64]{0,2,1:T(8,128)}, u32[]{:S(2)}) copy-start(f32[128,32,64]{0,2,1:T(8,128)} %convolution_bitcast_fusion.3) | copy-start | bytes 3145732
  284.1 4.7 %copy-start.30 = (f32[32,128]{1,0:T(8,128)S(1)}, f32[32,128]{1,0:T(8,128)}, u32[]{:S(2)}) copy-start(f32[32,128]{1,0:T(8,128)} %copy-done.29) | copy-start | bytes 49156
  293.5 4.7 %copy-start.35 = (f32[128,32]{0,1:T(8,128)S(1)}, f32[128,32]{0,1:T(8,128)}, u32[]{:S(2)}) copy-start(f32[128,32]{0,1:T(8,128)} %get-tuple-element.275) | copy-start | bytes 49156
  294.8 5.3 %copy-start.25 = (f32[128,128]{1,0:T(8,128)S(1)}, f32[128,128]{1,0:T(8,128)}, u32[]{:S(2)}) copy-start(f32[128,128]{1,0:T(8,128)} %fusion.60) | copy-start | bytes 196612
  294.8 5.3 %copy-start.26 = (f32[128,128]{1,0:T(8,128)S(1)}, f32[128,128]{1,0:T(8,128)}, u32[]{:S(2)}) copy-start(f32[128,128]{1,0:T(8,128)} %fusion.67) | copy-start | bytes 196612
  294.8 6.1 %copy-start.38 = (f32[32]{0:T(128)S(1)}, f32[32]{0:T(128)}, u32[]{:S(2)}) copy-start(f32[32]{0:T(128)} %get-tuple-element.283) | copy-start | bytes 388
  300.8 40.5 %reduce-scatter.3.cloned.1.call-start = ((), (), s32[]{:S(2)}) async-start(), calls=%async_computation.2 | async-start | bytes 163840 | tf_op jit(solution)/shard_map/reduce_scatter | solution.py:184
  300.9 5.0 %copy-start.23 = (f32[128,128]{1,0:T(8,128)S(1)}, f32[128,128]{1,0:T(8,128)}, u32[]{:S(2)}) copy-start(f32[128,128]{1,0:T(8,128)} %fusion.64) | copy-start | bytes 196612
  300.9 5.0 %copy-start.24 = (f32[128,128]{1,0:T(8,128)S(1)}, f32[128,128]{1,0:T(8,128)}, u32[]{:S(2)}) copy-start(f32[128,128]{1,0:T(8,128)} %fusion.71) | copy-start | bytes 196612
  300.9 5.6 %copy-start.41 = (f32[32]{0:T(128)S(1)}, f32[32]{0:T(128)}, u32[]{:S(2)}) copy-start(f32[32]{0:T(128)} %get-tuple-element.281) | copy-start | bytes 388
  (22 other events, 59.8 us)
Sparse Core Ops, SparseCore 0:
  15.3 128.2 all-gather.5
  145.8 123.1 all-gather.7
  300.9 17.7 reduce-scatter.4
  321.7 19.5 reduce-scatter.2
where the time goes:
time: 349 us; the launch traced here: 348 us
  waiting for transfers between devices  206 us (59%)
  matrix products  44.9 us (13%)
  local copies, waits for them, and re-layouts  29 us (8%)
  other arithmetic  28.2 us (8%)
  blocking collectives  24.5 us (7%)
  between operations  15 us (4%)
    all_gather x2, waiting for transfers between devices, entering(): pieces = jax.tree.map(lambda part: lax.all_gather(part, axis), value)  175 us
    unnamed x1, blocking collectives  24.5 us
    reduce_scatter x1, waiting for transfers between devices, shards(): lax.psum_scatter(total_b, 'head', scatter_dimension=0, tiled=True)  22.6 us
    select_n x14, other arithmetic, hop(): jnp.where(position < mine, new, old)  20.5 us
    rev x2, local copies, waits for them, and re-layouts, entering(): pieces = jax.tree.map(lambda part: part[::-1], pieces)  9.7 us
    mul x14, local copies, waits for them, and re-layouts, combine_links(): later[0][:, None, None] * earlier[1] + later[1]  9.61 us
    dot_general x2, matrix products, shards(): jnp.einsum('hjn,hpn->jhp', b_decayed.astype(jnp.float32), finish, precisi...  8.63 us
    reduce_scatter x1, waiting for transfers between devices, shards(): lax.psum_scatter(total_c, 'head', scatter_dimension=0, tiled=True)  8.03 us
  transfers between devices with their start and end apart: 4, of which 4 were waited for; matrix products, arithmetic and copies ran while one was open for 18% of the time, Pallas kernels for 0%

commit v1 on v0

v1 whole, which is shorter than its diff:
```python
import functools

import jax
import jax.numpy as jnp
from jax import lax
from jax.experimental import pallas as pl
from jax.experimental.pallas import tpu as pltpu
from jax.sharding import PartitionSpec as P

HEAD_DIM = 64
STATE = 128
HEADS = 8
WIDE = HEADS * HEAD_DIM
PAIR_FIRST = (True, True, False, False)

F32 = jnp.float32
BF16 = jnp.bfloat16
HIGHEST = lax.Precision.HIGHEST
NN = (((1,), (0,)), ((), ()))
NT = (((1,), (1,)), ((), ()))
TN = (((0,), (0,)), ((), ()))
VMEM_LIMIT = 48 * 1024 * 1024


def dot(a, b, dims=NN):
    return lax.dot_general(a, b, dims, preferred_element_type=F32)


def dot_full(a, b, dims=NN):
    return lax.dot_general(a, b, dims, precision=HIGHEST, preferred_element_type=F32)


def halves(a):
    high = a.astype(BF16)
    return high, (a - high.astype(F32)).astype(BF16)


def dot_halves(a, b, dims=NN):
    high, low = halves(a)
    return dot(high, b, dims) + dot(low, b, dims)


def at_least(shape, row_dim, col_dim):
    return lax.broadcasted_iota(jnp.int32, shape, row_dim) >= lax.broadcasted_iota(
        jnp.int32, shape, col_dim
    )


def spread_matrix(heads):
    shape = (heads, heads * HEAD_DIM)
    lane = lax.broadcasted_iota(jnp.int32, shape, 1)
    first = lax.broadcasted_iota(jnp.int32, shape, 0) * HEAD_DIM
    return jnp.where((lane >= first) & (lane < first + HEAD_DIM), 1.0, 0.0).astype(F32)


def running_rows(decay):
    length = decay.shape[1]
    tri = jnp.where(at_least((length, length), 1, 0), 1.0, 0.0).astype(F32)
    return dot_full(decay, tri)


def running_columns(decay):
    length = decay.shape[1]
    tri = jnp.where(at_least((length, length), 0, 1), 1.0, 0.0).astype(F32)
    return dot_full(tri, decay, NT)


def decay_kernel(decay_ref, out_ref):
    totals = jnp.sum(decay_ref[...], axis=1, keepdims=True)
    heads = totals.shape[0]
    row = jnp.sum(spread_matrix(heads) * totals, axis=0, keepdims=True)
    out_ref[...] = jnp.broadcast_to(jnp.exp(row), out_ref.shape)


def local_kernel(decay_ref, x_ref, dy_ref, b_ref, c_ref, state_ref, adjoint_ref, xs_ref, dys_ref):
    columns = running_columns(decay_ref[...])
    length = columns.shape[0]
    last = columns[length - 1 : length, :]
    spread = spread_matrix(HEADS).astype(BF16)
    into_end = dot_halves(jnp.exp(last - columns), spread)
    from_start = dot_halves(jnp.exp(columns), spread)
    xs = (x_ref[...].astype(F32) * into_end).astype(BF16)
    dys = (dy_ref[...].astype(F32) * from_start).astype(BF16)
    xs_ref[...] = xs
    dys_ref[...] = dys
    state_ref[0] = dot(b_ref[...], xs, TN)
    adjoint_ref[0] = dot(c_ref[...], dys, TN)


def intra_kernel(
    decay_ref, x_ref, dy_ref, b_ref, c_ref, dx_ref, change_ref, gb_ref, gc_ref, table_ref
):
    step = pl.program_id(0)
    decay = decay_ref[...]
    rows = running_rows(decay)
    columns = running_columns(decay)
    length = rows.shape[1]
    b, c = b_ref[...], c_ref[...]
    scores = dot(b, c, NT)
    keep = at_least((length, length), 1, 0)
    half = lax.broadcasted_iota(jnp.int32, (length, 2 * HEAD_DIM), 1) < HEAD_DIM
    total = jnp.zeros((length, length), F32)
    for pair in range(HEADS // 2):
        lanes = slice(pair * 2 * HEAD_DIM, (pair + 1) * 2 * HEAD_DIM)
        x2 = x_ref[:, lanes]
        dy2 = dy_ref[:, lanes]
        parts = []
        for side in range(2):
            head = 2 * pair + side
            own = half if side == 0 else jnp.logical_not(half)
            x1 = jnp.where(own, x2.astype(F32), 0.0).astype(BF16)
            pairs = dot(x1, dy2, NT)
            gap = rows[head : head + 1, :] - columns[:, head : head + 1]
            mask = jnp.exp(jnp.where(keep, gap, -1e30))
            weights = (mask * scores).astype(BF16)
            total = total + mask * pairs
            change_ref[head : head + 1, :] = jnp.sum(
                weights.astype(F32) * pairs, axis=0, keepdims=True
            )
            parts.append(dot(weights, dy2))
        dx_ref[:, lanes] = jnp.where(half, parts[0], parts[1])

    @pl.when(step == 0)
    def _():
        table_ref[...] = total

    @pl.when(step > 0)
    def _():
        table_ref[...] += total

    @pl.when(step == pl.num_programs(0) - 1)
    def _():
        table = table_ref[...]
        gb_ref[...] = dot_halves(table, c)
        gc_ref[...] = dot_halves(table, b, TN)


def inter_kernel(
    decay_ref,
    state_in_ref,
    adjoint_in_ref,
    state_ref,
    total_ref,
    x_ref,
    xs_ref,
    dys_ref,
    b_ref,
    c_ref,
    dx_ref,
    change_ref,
    gb_ref,
    gc_ref,
    gx_ref,
    gd_ref,
    gb_out_ref,
    gc_out_ref,
):
    columns = running_columns(decay_ref[...])
    length = columns.shape[0]
    last = columns[length - 1 : length, :]
    spread = spread_matrix(HEADS).astype(BF16)
    into_end = dot_halves(jnp.exp(last - columns), spread)
    state_in = state_in_ref[...]
    adjoint_in = adjoint_in_ref[...]
    state_low = state_in.astype(BF16)
    adjoint_low = adjoint_in.astype(BF16)
    xs = xs_ref[...]
    dys = dys_ref[...]
    gb_out_ref[...] = gb_ref[...] + dot(xs, adjoint_low, NT)
    gc_out_ref[...] = gc_ref[...] + dot(dys, state_low, NT)
    grad_full = dx_ref[...] + into_end * dot(b_ref[...], adjoint_low)
    gx_ref[...] = grad_full.astype(BF16)
    change = dys.astype(F32) * dot(c_ref[...], state_low) - x_ref[...].astype(F32) * grad_full
    high, low = halves(change)
    per_head = change_ref[...] + dot(spread, high, NT) + dot(spread, low, NT)
    after = jnp.where(at_least((length, length), 0, 1), 1.0, 0.0).astype(F32)
    suffix = dot_full(per_head, after)
    state_end = total_ref[0:1, :] * state_in + state_ref[0]
    high, low = halves(state_end * adjoint_in)
    later = dot(spread, high, NT) + dot(spread, low, NT)
    gd_ref[...] = suffix + jnp.sum(later, axis=1, keepdims=True)


def params():
    return pltpu.CompilerParams(vmem_limit_bytes=VMEM_LIMIT)


def cost(flops, nbytes):
    return pl.CostEstimate(flops=flops, bytes_accessed=nbytes, transcendentals=0)


def whole(shape):
    return pl.BlockSpec(shape, lambda k: (0,) * len(shape))


def decay_totals(log_decay):
    heads = log_decay.shape[0]
    return pl.pallas_call(
        decay_kernel,
        out_shape=jax.ShapeDtypeStruct((8, heads * HEAD_DIM), F32),
        name="decay_totals",
    )(log_decay)


def local_states(log_decay, x, dy, b, c):
    tokens, width = x.shape
    chunks = width // WIDE
    wide = pl.BlockSpec((tokens, WIDE), lambda k: (0, k))
    rows = pl.BlockSpec((HEADS, tokens), lambda k: (k, 0))
    proj = whole((tokens, STATE))
    states = pl.BlockSpec((1, STATE, WIDE), lambda k: (k, 0, 0))
    return pl.pallas_call(
        local_kernel,
        grid=(chunks,),
        in_specs=[rows, wide, wide, proj, proj],
        out_specs=[states, states, wide, wide],
        out_shape=[
            jax.ShapeDtypeStruct((chunks, STATE, WIDE), F32),
            jax.ShapeDtypeStruct((chunks, STATE, WIDE), F32),
            jax.ShapeDtypeStruct((tokens, width), BF16),
            jax.ShapeDtypeStruct((tokens, width), BF16),
        ],
        compiler_params=params(),
        cost_estimate=cost(4 * tokens * STATE * width, 12 * tokens * width),
        name="local_states",
    )(log_decay, x, dy, b, c)


def intra(log_decay, x, dy, b, c):
    tokens, width = x.shape
    chunks = width // WIDE
    wide = pl.BlockSpec((tokens, WIDE), lambda k: (0, k))
    rows = pl.BlockSpec((HEADS, tokens), lambda k: (k, 0))
    proj = whole((tokens, STATE))
    return pl.pallas_call(
        intra_kernel,
        grid=(chunks,),
        in_specs=[rows, wide, wide, proj, proj],
        out_specs=[wide, rows, proj, proj],
        out_shape=[
            jax.ShapeDtypeStruct((tokens, width), F32),
            jax.ShapeDtypeStruct(log_decay.shape, F32),
            jax.ShapeDtypeStruct((tokens, STATE), F32),
            jax.ShapeDtypeStruct((tokens, STATE), F32),
        ],
        scratch_shapes=[pltpu.VMEM((tokens, tokens), F32)],
        compiler_params=params(),
        cost_estimate=cost(4 * tokens * tokens * width, 8 * tokens * width),
        name="intra",
    )(log_decay, x, dy, b, c)


def inter(
    chunk, log_decay, state_in, adjoint_in, states, totals, x, xs, dys, b, c, dx, change, gb, gc
):
    tokens = x.shape[0]
    wide = pl.BlockSpec((tokens, WIDE), lambda k: (0, chunk))
    rows = pl.BlockSpec((HEADS, tokens), lambda k: (chunk, 0))
    proj = whole((tokens, STATE))
    return pl.pallas_call(
        inter_kernel,
        grid=(1,),
        in_specs=[
            rows,
            whole((STATE, WIDE)),
            whole((STATE, WIDE)),
            pl.BlockSpec((1, STATE, WIDE), lambda k: (chunk, 0, 0)),
            pl.BlockSpec((8, WIDE), lambda k: (0, chunk)),
            wide,
            wide,
            wide,
            proj,
            proj,
            wide,
            rows,
            proj,
            proj,
        ],
        out_specs=[whole((tokens, WIDE)), whole((HEADS, tokens)), proj, proj],
        out_shape=[
            jax.ShapeDtypeStruct((tokens, WIDE), BF16),
            jax.ShapeDtypeStruct((HEADS, tokens), F32),
            jax.ShapeDtypeStruct((tokens, STATE), F32),
            jax.ShapeDtypeStruct((tokens, STATE), F32),
        ],
        compiler_params=params(),
        cost_estimate=cost(8 * tokens * STATE * WIDE, 16 * tokens * WIDE),
        name="inter",
    )(log_decay, state_in, adjoint_in, states, totals, x, xs, dys, b, c, dx, change, gb, gc)


def group_rounds(groups):
    rounds = []
    span = 1
    while span < groups:
        permutes = []
        for step in range(span):
            links = []
            for first in range(0, groups, 2 * span):
                links.append((first + span - 1, first + span + step))
                links.append((first + span, first + span - 1 - step))
            permutes.append([(s, t) for s, t in links if s < groups and t < groups])
        rounds.append((span, permutes))
        span *= 2
    return rounds


def group_scan(forward, backward, total, group, groups):
    carried_f = carried_b = None
    decay_f = decay_b = jnp.ones_like(total)
    rounds = group_rounds(groups)
    for number, (span, permutes) in enumerate(rounds):
        upper = (group // span) % 2 == 1
        if carried_f is None:
            send = jnp.where(upper, backward, forward)
        else:
            send = jnp.where(
                upper, total * carried_b + backward, total * carried_f + forward
            )
        more = number + 1 < len(rounds)
        if more:
            decay = total * jnp.where(upper, decay_b, decay_f)
            send = jnp.concatenate([send, jnp.broadcast_to(decay, (8, send.shape[1]))], axis=0)
        got = None
        for links in permutes:
            both = [(2 * s + side, 2 * t + side) for s, t in links for side in range(2)]
            part = lax.ppermute(send, "ctx", both)
            got = part if got is None else got + part
        value = got[:STATE]
        if carried_f is None:
            carried_f = jnp.where(upper, value, 0.0)
            carried_b = jnp.where(upper, 0.0, value)
        else:
            carried_f = jnp.where(upper, decay_f * value + carried_f, carried_f)
            carried_b = jnp.where(upper, carried_b, decay_b * value + carried_b)
        if more:
            seen = got[STATE : STATE + 1]
            decay_f = jnp.where(upper, decay_f * seen, decay_f)
            decay_b = jnp.where(upper, decay_b, decay_b * seen)
    if carried_f is None:
        return jnp.zeros_like(forward), jnp.zeros_like(backward)
    return carried_f, carried_b


def shards(inputs, grad_out, b_proj, c_proj, log_decay):
    count = lax.axis_size("ctx")
    mine = lax.axis_index("ctx")
    second = mine % 2 == 1
    group, groups = mine // 2, count // 2
    swap = [(i, i ^ 1) for i in range(count)]

    totals = decay_totals(log_decay)
    other_totals = lax.ppermute(totals[0:1], "ctx", swap)
    states, adjoints, xs, dys = local_states(log_decay, inputs, grad_out, b_proj, c_proj)
    chunks = states.shape[0]
    entering = [None] * chunks
    for k in range(chunks):
        state, adjoint = states[k], adjoints[k]
        own = totals[0:1, k * WIDE : (k + 1) * WIDE]
        other = other_totals[0:1, k * WIDE : (k + 1) * WIDE]
        both = own * other
        if PAIR_FIRST[k % len(PAIR_FIRST)]:
            got = lax.ppermute(jnp.concatenate([state, adjoint], axis=0), "ctx", swap)
            state_p, adjoint_p = got[:STATE], got[STATE:]
            forward = jnp.where(second, own * state_p + state, other * state + state_p)
            backward = jnp.where(second, adjoint_p + other * adjoint, adjoint + own * adjoint_p)
            carried_f, carried_b = group_scan(forward, backward, both, group, groups)
            entering[k] = (
                jnp.where(second, other * carried_f + state_p, carried_f),
                jnp.where(second, carried_b, other * carried_b + adjoint_p),
            )
        else:
            forward = jnp.where(second, state, other * state)
            backward = jnp.where(second, other * adjoint, adjoint)
            carried_f, carried_b = group_scan(forward, backward, both, group, groups)
            send_f = jnp.where(second, carried_f, own * carried_f + state)
            send_b = jnp.where(second, own * carried_b + adjoint, carried_b)
            got = lax.ppermute(jnp.concatenate([send_f, send_b], axis=0), "ctx", swap)
            entering[k] = (
                jnp.where(second, other * carried_f, carried_f) + got[:STATE],
                jnp.where(second, carried_b, other * carried_b) + got[STATE:],
            )

    dx, change, gb, gc = intra(log_decay, inputs, grad_out, b_proj, c_proj)
    order = [k for i in range(chunks) for k in range(chunks) if k % 2 * 2 + k // 2 == i]
    parts_x, parts_d = [None] * chunks, [None] * chunks
    for k in order if chunks == 4 else range(chunks):
        parts_x[k], parts_d[k], gb, gc = inter(
            k, log_decay, *entering[k], states, totals, inputs, xs, dys, b_proj, c_proj,
            dx, change, gb, gc,
        )
    grad_x = jnp.concatenate(parts_x, axis=1)
    grad_decay = jnp.concatenate(parts_d, axis=0)

    ranks = lax.axis_size("head")
    rank = lax.axis_index("head")
    rows = gb.shape[0] // ranks
    sums = jnp.stack([gb, gc])

    def piece(owner):
        return lax.dynamic_slice_in_dim(sums, owner * rows, rows, axis=1)

    result = piece(rank)
    for step in range(1, ranks):
        links = [(i, i ^ step) for i in range(ranks)]
        result = result + lax.ppermute(piece(rank ^ step), "head", links)
    return grad_x, result[0], result[1], grad_decay


def solution(mesh):
    placed = (P("ctx", "head"), P("ctx", "head"), P("ctx", None), P("ctx", None), P("head", "ctx"))
    return jax.shard_map(
        shards,
        mesh=mesh,
        in_specs=placed,
        out_specs=(
            P("ctx", "head"),
            P(("ctx", "head"), None),
            P(("ctx", "head"), None),
            P("head", "ctx"),
        ),
        check_vma=False,
    )
```

time: 349 us -> 121 us (0.35)
  waiting for transfers between devices: 206 us -> 47.1 us
  matrix products: 44.9 us -> 0 us
  starting transfers between devices: 0.16 us -> 27 us
  Pallas kernels: 0 us -> 26.4 us
  blocking collectives: 24.5 us -> 0 us
  local copies, waits for them, and re-layouts: 29 us -> 7.19 us
  other arithmetic: 28.2 us -> 11.7 us
  between operations: 15 us -> 0.99 us
    all_gather x2 -> x0, waiting for transfers between devices: 175 us -> none  [entering(): pieces = jax.tree.map(lambda part: lax.all_gather(part, axis), value)]
    ppermute x0 -> x20, waiting for transfers between devices: none -> 47.1 us  [the longest x12 35.3 us: group_scan(): part = lax.ppermute(send, 'ctx', both)]
    dot_general x24 -> x0, matrix products: 44.9 us -> none  [the longest x2 8.63 us: shards(): jnp.einsum('hjn,hpn->jhp', b_decayed.astype(jnp.float32), finish, precisi...]
    reduce_scatter x2 -> x0, waiting for transfers between devices: 30.6 us -> none  [the longest x1 22.6 us: shards(): lax.psum_scatter(total_b, 'head', scatter_dimension=0, tiled=True)]
    ppermute x0 -> x20, starting transfers between devices: none -> 27 us  [the longest x12 16.9 us: group_scan(): part = lax.ppermute(send, 'ctx', both)]
    pallas_call x0 -> x7, Pallas kernels: none -> 26.4 us  [the longest x4 11.6 us: inter(): pl.pallas_call(inter_kernel, grid=(1,), in_specs=[rows, whole((STATE, WID...]
    unnamed x1 -> x0, blocking collectives: 24.5 us -> none
    select_n x14 -> x11, other arithmetic: 20.5 us -> 7.14 us  [the longest x2 2.79 us: group_scan(): jnp.where(upper, total * carried_b + backward, total * carried_f + forward)]
  transfers between devices with their start and end apart: 4 -> 20, of which waited for: 4 -> 9; matrix products, arithmetic and copies ran while one was open for 18% -> 10% of each run, Pallas kernels for 0% -> 14%
where the time goes in v1:
time: 121 us; the launch traced here: 120 us
  waiting for transfers between devices  47.1 us (39%)
  starting transfers between devices  27 us (22%)
  Pallas kernels  26.4 us (22%)
  other arithmetic  11.7 us (10%)
  local copies, waits for them, and re-layouts  7.19 us (6%)
    ppermute x12, waiting for transfers between devices, group_scan(): part = lax.ppermute(send, 'ctx', both)  35.3 us
    ppermute x12, starting transfers between devices, group_scan(): part = lax.ppermute(send, 'ctx', both)  16.9 us
    pallas_call x4, Pallas kernels, inter(): pl.pallas_call(inter_kernel, grid=(1,), in_specs=[rows, whole((STATE, WID...  11.6 us
    ppermute x1, waiting for transfers between devices, shards(): other_totals = lax.ppermute(totals[0:1], 'ctx', swap)  7.85 us
    pallas_call x1, Pallas kernels, intra(): pl.pallas_call(intra_kernel, grid=(chunks,), in_specs=[rows, wide, wide,...  6.72 us
    pallas_call x1, Pallas kernels, local_states(): pl.pallas_call(local_kernel, grid=(chunks,), in_specs=[rows, wide, wide,...  6.56 us
    unnamed x30, local copies, waits for them, and re-layouts  5.64 us
    ppermute x2, starting transfers between devices, shards(): got = lax.ppermute(jnp.concatenate([state, adjoint], axis=0), 'ctx', swap)  5.03 us
  transfers between devices with their start and end apart: 20, of which 9 were waited for; matrix products, arithmetic and copies ran while one was open for 10% of the time, Pallas kernels for 14%

profile of v1, /device:TPU:0, one launch (start us, length us, event | category | flops | bytes accessed | tf_op | source)
XLA Modules:
  0.0 120.3 jit_solution(8652583169951728800)
XLA Ops:
  4.3 6.6 %local_states.1 = (f32[4,128,512]{2,1,0:T(8,128)S(1)}, f32[4,128,512]{2,1,0:T(8,128)S(1)}, bf16[256,2048]{1,0:T(8,128)(2,1)S(1)}, bf16[256,2048]{1,0:T(8,128)(2,1)S(1)}) custom-call(f32[32,256]{1,0:T(8,128)S(1)} %copy-done.13, bf16[256,2048]{1,0:T(8,128)(2,1)S(1)} %copy-done, bf16[256,2048]{1,0:T(8,128)(2,1)} %dy_ref.3, bf16[256,128]{1,0:T(8,128)(2,1)S(1)} %copy-done.8, ...), custom_call_target="tpu_custom_call" | custom-call | flops 268435456 | bytes 6291456 | tf_op jit(solution)/shard_map/local_states/pallas_call | solution.py:212
  13.7 2.9 %collective-permute-start.1 = (f32[256,512]{1,0:T(8,128)}, f32[256,512]{1,0:T(8,128)}, u32[]{:S(2)}, u32[]{:S(2)}) collective-permute-start(f32[256,512]{1,0:T(8,128)} %pad_maximum_fusion.1), channel_id=1, source_target_pairs={{0,4},{4,0},{8,12},{12,8},{16,20},{20,16},{24,28},{28,24},{1,5},{5... | collective-permute-start | bytes 1572872 | tf_op jit(solution)/shard_map/ppermute | solution.py:363
  16.7 1.5 %decay_totals.1.total_ref = f32[8,2048]{1,0:T(8,128)} custom-call(f32[32,256]{1,0:T(8,128)} %decay_ref.13), custom_call_target="tpu_custom_call" | custom-call | tf_op jit(solution)/shard_map/decay_totals/pallas_call | solution.py:198
  19.9 2.1 %collective-permute-start.5 = (f32[256,512]{1,0:T(8,128)}, f32[256,512]{1,0:T(8,128)}, u32[]{:S(2)}, u32[]{:S(2)}) collective-permute-start(f32[256,512]{1,0:T(8,128)} %pad_maximum_fusion.2), channel_id=1, source_target_pairs={{0,4},{4,0},{8,12},{12,8},{16,20},{20,16},{24,28},{28,24},{1,5},{5... | collective-permute-start | bytes 1572872 | tf_op jit(solution)/shard_map/ppermute | solution.py:363
  22.0 7.8 %collective-permute-done = f32[1,2048]{1,0:T(1,128)S(1)} collective-permute-done((f32[1,2048]{1,0:T(1,128)S(1)}, f32[1,2048]{1,0:T(1,128)S(1)}, u32[]{:S(2)}, u32[]{:S(2)}) %collective-permute-start) | collective-permute-done | bytes 8224 | tf_op jit(solution)/shard_map/ppermute | solution.py:353
  30.6 1.5 %broadcast_select_fusion.1 = (f32[128,512]{1,0:T(8,128)S(1)}, f32[128,512]{1,0:T(8,128)S(1)}, f32[128,512]{1,0:T(8,128)S(1)}) fusion(pred[]{:T(512)S(6)} %eq.27, f32[512]{0:T(512)S(1)} %bitcast.112, f32[512]{0:T(512)S(1)} %bitcast.99, f32[256,512]{1,0:T(8,128)} %collective-permute-done.1, pred[]{:T(512)S(6)} %eq.25, ...), kind=kLoop, calls=%fused_computation.72 | loop fusion | flops 1376256 | bytes 2891778 | tf_op jit(solution)/shard_map/jit(_where)/select_n | solution.py:315
  32.2 2.2 %collective-permute-start.2 = (f32[136,512]{1,0:T(8,128)S(1)}, f32[136,512]{1,0:T(8,128)S(1)}, u32[]{:S(2)}, u32[]{:S(2)}) collective-permute-start(f32[136,512]{1,0:T(8,128)S(1)} %pad_maximum_fusion.5), channel_id=1, source_target_pairs={{0,8},{4,12},{8,0},{12,4},{16,24},{20,28},{24,16},{28,20},{1,9},{5... | collective-permute-start | bytes 835592 | tf_op jit(solution)/shard_map/ppermute | solution.py:327
  34.4 6.7 %intra.1 = (f32[256,2048]{1,0:T(8,128)S(1)}, f32[32,256]{1,0:T(8,128)S(1)}, f32[256,128]{1,0:T(8,128)S(1)}, f32[256,128]{1,0:T(8,128)S(1)}) custom-call(f32[32,256]{1,0:T(8,128)S(1)} %copy-done.14, bf16[256,2048]{1,0:T(8,128)(2,1)S(1)} %copy-done.1, bf16[256,2048]{1,0:T(8,128)(2,1)S(1)} %copy-done.7, bf16[256,128]{1,0:T(8,128)(2,1)S(1)} %copy-done.9, ...), custom_call_target="tpu_custom_call" | custom-call | flops 536870912 | bytes 4194304 | tf_op jit(solution)/shard_map/intra/pallas_call | solution.py:235
  41.3 2.1 %collective-permute-start.13 = (f32[136,512]{1,0:T(8,128)S(1)}, f32[136,512]{1,0:T(8,128)S(1)}, u32[]{:S(2)}, u32[]{:S(2)}) collective-permute-start(f32[136,512]{1,0:T(8,128)S(1)} %pad_maximum_fusion.8), channel_id=1, source_target_pairs={{0,8},{4,12},{8,0},{12,4},{16,24},{20,28},{24,16},{28,20},{1,9},{5... | collective-permute-start | bytes 835592 | tf_op jit(solution)/shard_map/ppermute | solution.py:327
  43.4 1.5 %add_select_fusion.17 = (f32[128,512]{1,0:T(8,128)S(1)}, f32[128,512]{1,0:T(8,128)S(1)}) fusion(f32[136,512]{1,0:T(8,128)S(1)} %collective-permute-done.2, f32[512]{0:T(512)S(1)} %bitcast.111, pred[]{:T(512)S(6)} %eq.27, pred[]{:T(512)S(6)} %eq.26, f32[512]{0:T(512)S(1)} %bitcast.113, f32[512]{0:T(512)S(1)} %bitcast.100, ...), kind=kLoop, calls=%fused_computation.56 | loop fusion | flops 1835008 | bytes 2893827 | tf_op jit(solution)/shard_map/jit(_where)/select_n | solution.py:317
  46.9 4.5 %collective-permute-start.6 = (f32[136,512]{1,0:T(8,128)S(1)}, f32[136,512]{1,0:T(8,128)S(1)}, u32[]{:S(2)}, u32[]{:S(2)}) collective-permute-start(f32[136,512]{1,0:T(8,128)S(1)} %pad_maximum_fusion.6), channel_id=1, source_target_pairs={{0,8},{4,12},{8,0},{12,4},{16,24},{20,28},{24,16},{28,20},{1,9},{5... | collective-permute-start | bytes 835592 | tf_op jit(solution)/shard_map/ppermute | solution.py:327
  52.5 9.6 %collective-permute-done.13 = f32[136,512]{1,0:T(8,128)S(1)} collective-permute-done((f32[136,512]{1,0:T(8,128)S(1)}, f32[136,512]{1,0:T(8,128)S(1)}, u32[]{:S(2)}, u32[]{:S(2)}) %collective-permute-start.13) | collective-permute-done | bytes 278560 | tf_op jit(solution)/shard_map/ppermute | solution.py:327
  62.0 3.0 %collective-permute-done.6 = f32[136,512]{1,0:T(8,128)S(1)} collective-permute-done((f32[136,512]{1,0:T(8,128)S(1)}, f32[136,512]{1,0:T(8,128)S(1)}, u32[]{:S(2)}, u32[]{:S(2)}) %collective-permute-start.6) | collective-permute-done | bytes 278560 | tf_op jit(solution)/shard_map/ppermute | solution.py:327
  69.5 2.9 %inter.4 = (bf16[256,512]{1,0:T(8,128)(2,1)S(1)}, f32[8,256]{1,0:T(8,128)S(1)}, f32[256,128]{1,0:T(8,128)S(1)}, f32[256,128]{1,0:T(8,128)S(1)}) custom-call(f32[32,256]{1,0:T(8,128)S(1)} %copy-done.14, f32[128,512]{1,0:T(8,128)S(1)} %get-tuple-element.68.state_in_ref, f32[128,512]{1,0:T(8,128)S(1)} %get-tuple-element.67.adjoint_in_ref, ...), custom_call_target="tpu_custom_call" | custom-call | flops 134217728 | bytes 2097152 | tf_op jit(solution)/shard_map/inter/pallas_call | solution.py:260
  74.4 4.5 %collective-permute-done.11 = f32[128,512]{1,0:T(8,128)S(1)} collective-permute-done((f32[128,512]{1,0:T(8,128)S(1)}, f32[128,512]{1,0:T(8,128)S(1)}, u32[]{:S(2)}, u32[]{:S(2)}) %collective-permute-start.11) | collective-permute-done | bytes 262176 | tf_op jit(solution)/shard_map/ppermute | solution.py:327
  81.4 1.6 %collective-permute-start.12 = (f32[256,512]{1,0:T(8,128)S(1)}, f32[256,512]{1,0:T(8,128)S(1)}, u32[]{:S(2)}, u32[]{:S(2)}) collective-permute-start(f32[256,512]{1,0:T(8,128)S(1)} %pad_maximum_fusion.3), channel_id=1, source_target_pairs={{0,4},{4,0},{8,12},{12,8},{16,20},{20,16},{24,28},{28,24},{1,5},{5... | collective-permute-start | bytes 1572872 | tf_op jit(solution)/shard_map/ppermute | solution.py:378
  83.0 17.2 %collective-permute-done.15 = f32[128,512]{1,0:T(8,128)S(1)} collective-permute-done((f32[128,512]{1,0:T(8,128)S(1)}, f32[128,512]{1,0:T(8,128)S(1)}, u32[]{:S(2)}, u32[]{:S(2)}) %collective-permute-start.15) | collective-permute-done | bytes 262176 | tf_op jit(solution)/shard_map/ppermute | solution.py:327
  100.4 1.6 %collective-permute-start.16 = (f32[256,512]{1,0:T(8,128)S(1)}, f32[256,512]{1,0:T(8,128)S(1)}, u32[]{:S(2)}, u32[]{:S(2)}) collective-permute-start(f32[256,512]{1,0:T(8,128)S(1)} %pad_maximum_fusion.4), channel_id=1, source_target_pairs={{0,4},{4,0},{8,12},{12,8},{16,20},{20,16},{24,28},{28,24},{1,5},{5... | collective-permute-start | bytes 1572872 | tf_op jit(solution)/shard_map/ppermute | solution.py:378
  103.3 2.9 %inter.5 = (bf16[256,512]{1,0:T(8,128)(2,1)S(1)}, f32[8,256]{1,0:T(8,128)S(1)}, f32[256,128]{1,0:T(8,128)S(1)}, f32[256,128]{1,0:T(8,128)S(1)}) custom-call(f32[32,256]{1,0:T(8,128)S(1)} %copy-done.14, f32[128,512]{1,0:T(8,128)S(1)} %get-tuple-element.81.state_in_ref, f32[128,512]{1,0:T(8,128)S(1)} %get-tuple-element.80.adjoint_in_ref, ...), custom_call_target="tpu_custom_call" | custom-call | flops 134217728 | bytes 2097152 | tf_op jit(solution)/shard_map/inter/pallas_call | solution.py:260
  106.2 2.9 %inter.6 = (bf16[256,512]{1,0:T(8,128)(2,1)S(1)}, f32[8,256]{1,0:T(8,128)S(1)}, f32[256,128]{1,0:T(8,128)S(1)}, f32[256,128]{1,0:T(8,128)S(1)}) custom-call(f32[32,256]{1,0:T(8,128)S(1)} %copy-done.14, f32[128,512]{1,0:T(8,128)S(1)} %get-tuple-element.70.state_in_ref, f32[128,512]{1,0:T(8,128)S(1)} %get-tuple-element.69.adjoint_in_ref, ...), custom_call_target="tpu_custom_call" | custom-call | flops 134217728 | bytes 2097152 | tf_op jit(solution)/shard_map/inter/pallas_call | solution.py:260
  109.1 1.7 %collective-permute-done.16 = f32[256,512]{1,0:T(8,128)S(1)} collective-permute-done((f32[256,512]{1,0:T(8,128)S(1)}, f32[256,512]{1,0:T(8,128)S(1)}, u32[]{:S(2)}, u32[]{:S(2)}) %collective-permute-start.16) | collective-permute-done | bytes 524320 | tf_op jit(solution)/shard_map/ppermute | solution.py:378
  110.9 2.9 %inter.7 = (bf16[256,512]{1,0:T(8,128)(2,1)S(1)}, f32[8,256]{1,0:T(8,128)S(1)}, f32[256,128]{1,0:T(8,128)S(1)}, f32[256,128]{1,0:T(8,128)S(1)}) custom-call(f32[32,256]{1,0:T(8,128)S(1)} %copy-done.14, f32[128,512]{1,0:T(8,128)S(1)} %get-tuple-element.83.state_in_ref, f32[128,512]{1,0:T(8,128)S(1)} %get-tuple-element.82.adjoint_in_ref, ...), custom_call_target="tpu_custom_call" | custom-call | flops 134217728 | bytes 2097152 | tf_op jit(solution)/shard_map/inter/pallas_call | solution.py:260
  113.9 1.6 %collective-permute-start.18 = (f32[2,64,128]{2,1,0:T(8,128)S(1)}, f32[2,64,128]{2,1,0:T(8,128)S(1)}, u32[]{:S(2)}, u32[]{:S(2)}) collective-permute-start(f32[2,64,128]{2,1,0:T(8,128)S(1)} %get-tuple-element.93), channel_id=1, source_target_pairs={{0,2},{1,3},{2,0},{3,1},{4,6},{5,7},{6,4},{7,5},{8,10},{9,11},{10,... | collective-permute-start | bytes 196616 | tf_op jit(solution)/shard_map/ppermute | solution.py:406
  118.2 1.5 %collective-permute-done.18 = f32[2,64,128]{2,1,0:T(8,128)S(1)} collective-permute-done((f32[2,64,128]{2,1,0:T(8,128)S(1)}, f32[2,64,128]{2,1,0:T(8,128)S(1)}, u32[]{:S(2)}, u32[]{:S(2)}) %collective-permute-start.18) | collective-permute-done | bytes 65568 | tf_op jit(solution)/shard_map/ppermute | solution.py:406
  (86 shorter events, 26.2 us)
Async XLA Ops:
  13.7 16.9 %collective-permute-start.1 = (f32[256,512]{1,0:T(8,128)}, f32[256,512]{1,0:T(8,128)}, u32[]{:S(2)}, u32[]{:S(2)}) collective-permute-start(f32[256,512]{1,0:T(8,128)} %pad_maximum_fusion.1), channel_id=1, source_target_pairs={{0,4},{4,0},{8,12},{12,8},{16,20},{20,16},{24,28},{28,24},{1,5},{5... | collective-permute-start | bytes 1572872 | tf_op jit(solution)/shard_map/ppermute | solution.py:363
  19.0 10.8 %collective-permute-start = (f32[1,2048]{1,0:T(1,128)S(1)}, f32[1,2048]{1,0:T(1,128)S(1)}, u32[]{:S(2)}, u32[]{:S(2)}) collective-permute-start(f32[1,2048]{1,0:T(1,128)S(1)} %slice.140), channel_id=1, source_target_pairs={{0,4},{4,0},{8,12},{12,8},{16,20},{20,16},{24,28},{28,24},{1,5},{5... | collective-permute-start | bytes 24584 | tf_op jit(solution)/shard_map/ppermute | solution.py:353
  19.9 14.5 %copy-start.1 = (bf16[256,2048]{1,0:T(8,128)(2,1)S(1)}, bf16[256,2048]{1,0:T(8,128)(2,1)}, u32[]{:S(2)}) copy-start(bf16[256,2048]{1,0:T(8,128)(2,1)} %x_ref.11) | copy-start | bytes 3145732
  19.9 14.5 %copy-start.9 = (bf16[256,128]{1,0:T(8,128)(2,1)S(1)}, bf16[256,128]{1,0:T(8,128)(2,1)}, u32[]{:S(2)}) copy-start(bf16[256,128]{1,0:T(8,128)(2,1)} %b_ref.11) | copy-start | bytes 196612
  19.9 14.5 %copy-start.11 = (bf16[256,128]{1,0:T(8,128)(2,1)S(1)}, bf16[256,128]{1,0:T(8,128)(2,1)}, u32[]{:S(2)}) copy-start(bf16[256,128]{1,0:T(8,128)(2,1)} %c_ref.11) | copy-start | bytes 196612
  19.9 14.5 %copy-start.14 = (f32[32,256]{1,0:T(8,128)S(1)}, f32[32,256]{1,0:T(8,128)}, u32[]{:S(2)}) copy-start(f32[32,256]{1,0:T(8,128)} %decay_ref.13) | copy-start | bytes 98308
  19.9 23.5 %collective-permute-start.5 = (f32[256,512]{1,0:T(8,128)}, f32[256,512]{1,0:T(8,128)}, u32[]{:S(2)}, u32[]{:S(2)}) collective-permute-start(f32[256,512]{1,0:T(8,128)} %pad_maximum_fusion.2), channel_id=1, source_target_pairs={{0,4},{4,0},{8,12},{12,8},{16,20},{20,16},{24,28},{28,24},{1,5},{5... | collective-permute-start | bytes 1572872 | tf_op jit(solution)/shard_map/ppermute | solution.py:363
  32.2 11.2 %collective-permute-start.2 = (f32[136,512]{1,0:T(8,128)S(1)}, f32[136,512]{1,0:T(8,128)S(1)}, u32[]{:S(2)}, u32[]{:S(2)}) collective-permute-start(f32[136,512]{1,0:T(8,128)S(1)} %pad_maximum_fusion.5), channel_id=1, source_target_pairs={{0,8},{4,12},{8,0},{12,4},{16,24},{20,28},{24,16},{28,20},{1,9},{5... | collective-permute-start | bytes 835592 | tf_op jit(solution)/shard_map/ppermute | solution.py:327
  41.2 11.3 %collective-permute-start.9 = (f32[136,512]{1,0:T(8,128)S(1)}, f32[136,512]{1,0:T(8,128)S(1)}, u32[]{:S(2)}, u32[]{:S(2)}) collective-permute-start(f32[136,512]{1,0:T(8,128)S(1)} %pad_maximum_fusion.7), channel_id=1, source_target_pairs={{0,8},{4,12},{8,0},{12,4},{16,24},{20,28},{24,16},{28,20},{1,9},{5... | collective-permute-start | bytes 835592 | tf_op jit(solution)/shard_map/ppermute | solution.py:327
  41.3 20.7 %collective-permute-start.13 = (f32[136,512]{1,0:T(8,128)S(1)}, f32[136,512]{1,0:T(8,128)S(1)}, u32[]{:S(2)}, u32[]{:S(2)}) collective-permute-start(f32[136,512]{1,0:T(8,128)S(1)} %pad_maximum_fusion.8), channel_id=1, source_target_pairs={{0,8},{4,12},{8,0},{12,4},{16,24},{20,28},{24,16},{28,20},{1,9},{5... | collective-permute-start | bytes 835592 | tf_op jit(solution)/shard_map/ppermute | solution.py:327
  44.9 23.4 %collective-permute-start.3 = (f32[128,512]{1,0:T(8,128)S(1)}, f32[128,512]{1,0:T(8,128)S(1)}, u32[]{:S(2)}, u32[]{:S(2)}) collective-permute-start(f32[128,512]{1,0:T(8,128)S(1)} %get-tuple-element.60), channel_id=1, source_target_pairs={{8,16},{12,20},{16,8},{20,12},{9,17},{13,21},{17,9},{21,13},{10,18... | collective-permute-start | bytes 786440 | tf_op jit(solution)/shard_map/ppermute | solution.py:327
  45.6 22.7 %collective-permute-start.4 = (f32[128,512]{1,0:T(8,128)S(1)}, f32[128,512]{1,0:T(8,128)S(1)}, u32[]{:S(2)}, u32[]{:S(2)}) collective-permute-start(f32[128,512]{1,0:T(8,128)S(1)} %get-tuple-element.60), channel_id=1, source_target_pairs={{8,24},{12,28},{16,0},{20,4},{9,25},{13,29},{17,1},{21,5},{10,26},... | collective-permute-start | bytes 786440 | tf_op jit(solution)/shard_map/ppermute | solution.py:327
  46.9 18.1 %collective-permute-start.6 = (f32[136,512]{1,0:T(8,128)S(1)}, f32[136,512]{1,0:T(8,128)S(1)}, u32[]{:S(2)}, u32[]{:S(2)}) collective-permute-start(f32[136,512]{1,0:T(8,128)S(1)} %pad_maximum_fusion.6), channel_id=1, source_target_pairs={{0,8},{4,12},{8,0},{12,4},{16,24},{20,28},{24,16},{28,20},{1,9},{5... | collective-permute-start | bytes 835592 | tf_op jit(solution)/shard_map/ppermute | solution.py:327
  66.3 8.1 %collective-permute-start.10 = (f32[128,512]{1,0:T(8,128)S(1)}, f32[128,512]{1,0:T(8,128)S(1)}, u32[]{:S(2)}, u32[]{:S(2)}) collective-permute-start(f32[128,512]{1,0:T(8,128)S(1)} %get-tuple-element.65), channel_id=1, source_target_pairs={{8,16},{12,20},{16,8},{20,12},{9,17},{13,21},{17,9},{21,13},{10,18... | collective-permute-start | bytes 786440 | tf_op jit(solution)/shard_map/ppermute | solution.py:327
  67.0 11.9 %collective-permute-start.11 = (f32[128,512]{1,0:T(8,128)S(1)}, f32[128,512]{1,0:T(8,128)S(1)}, u32[]{:S(2)}, u32[]{:S(2)}) collective-permute-start(f32[128,512]{1,0:T(8,128)S(1)} %get-tuple-element.65), channel_id=1, source_target_pairs={{8,24},{12,28},{16,0},{20,4},{9,25},{13,29},{17,1},{21,5},{10,26},... | collective-permute-start | bytes 786440 | tf_op jit(solution)/shard_map/ppermute | solution.py:327
  72.4 29.5 %collective-permute-start.7 = (f32[128,512]{1,0:T(8,128)S(1)}, f32[128,512]{1,0:T(8,128)S(1)}, u32[]{:S(2)}, u32[]{:S(2)}) collective-permute-start(f32[128,512]{1,0:T(8,128)S(1)} %get-tuple-element.66), channel_id=1, source_target_pairs={{8,16},{12,20},{16,8},{20,12},{9,17},{13,21},{17,9},{21,13},{10,18... | collective-permute-start | bytes 786440 | tf_op jit(solution)/shard_map/ppermute | solution.py:327
  73.1 28.9 %collective-permute-start.8 = (f32[128,512]{1,0:T(8,128)S(1)}, f32[128,512]{1,0:T(8,128)S(1)}, u32[]{:S(2)}, u32[]{:S(2)}) collective-permute-start(f32[128,512]{1,0:T(8,128)S(1)} %get-tuple-element.66), channel_id=1, source_target_pairs={{8,24},{12,28},{16,0},{20,4},{9,25},{13,29},{17,1},{21,5},{10,26},... | collective-permute-start | bytes 786440 | tf_op jit(solution)/shard_map/ppermute | solution.py:327
  79.2 3.8 %collective-permute-start.14 = (f32[128,512]{1,0:T(8,128)S(1)}, f32[128,512]{1,0:T(8,128)S(1)}, u32[]{:S(2)}, u32[]{:S(2)}) collective-permute-start(f32[128,512]{1,0:T(8,128)S(1)} %get-tuple-element.75), channel_id=1, source_target_pairs={{8,16},{12,20},{16,8},{20,12},{9,17},{13,21},{17,9},{21,13},{10,18... | collective-permute-start | bytes 786440 | tf_op jit(solution)/shard_map/ppermute | solution.py:327
  79.9 20.3 %collective-permute-start.15 = (f32[128,512]{1,0:T(8,128)S(1)}, f32[128,512]{1,0:T(8,128)S(1)}, u32[]{:S(2)}, u32[]{:S(2)}) collective-permute-start(f32[128,512]{1,0:T(8,128)S(1)} %get-tuple-element.75), channel_id=1, source_target_pairs={{8,24},{12,28},{16,0},{20,4},{9,25},{13,29},{17,1},{21,5},{10,26},... | collective-permute-start | bytes 786440 | tf_op jit(solution)/shard_map/ppermute | solution.py:327
  81.4 21.7 %collective-permute-start.12 = (f32[256,512]{1,0:T(8,128)S(1)}, f32[256,512]{1,0:T(8,128)S(1)}, u32[]{:S(2)}, u32[]{:S(2)}) collective-permute-start(f32[256,512]{1,0:T(8,128)S(1)} %pad_maximum_fusion.3), channel_id=1, source_target_pairs={{0,4},{4,0},{8,12},{12,8},{16,20},{20,16},{24,28},{28,24},{1,5},{5... | collective-permute-start | bytes 1572872 | tf_op jit(solution)/shard_map/ppermute | solution.py:378
  100.4 10.4 %collective-permute-start.16 = (f32[256,512]{1,0:T(8,128)S(1)}, f32[256,512]{1,0:T(8,128)S(1)}, u32[]{:S(2)}, u32[]{:S(2)}) collective-permute-start(f32[256,512]{1,0:T(8,128)S(1)} %pad_maximum_fusion.4), channel_id=1, source_target_pairs={{0,4},{4,0},{8,12},{12,8},{16,20},{20,16},{24,28},{28,24},{1,5},{5... | collective-permute-start | bytes 1572872 | tf_op jit(solution)/shard_map/ppermute | solution.py:378
  113.8 4.4 %collective-permute-start.19 = (f32[2,64,128]{2,1,0:T(8,128)S(1)}, f32[2,64,128]{2,1,0:T(8,128)S(1)}, u32[]{:S(2)}, u32[]{:S(2)}) collective-permute-start(f32[2,64,128]{2,1,0:T(8,128)S(1)} %get-tuple-element.94), channel_id=1, source_target_pairs={{0,3},{1,2},{2,1},{3,0},{4,7},{5,6},{6,5},{7,4},{8,11},{9,10},{10,... | collective-permute-start | bytes 196616 | tf_op jit(solution)/shard_map/ppermute | solution.py:406
  113.9 5.8 %collective-permute-start.18 = (f32[2,64,128]{2,1,0:T(8,128)S(1)}, f32[2,64,128]{2,1,0:T(8,128)S(1)}, u32[]{:S(2)}, u32[]{:S(2)}) collective-permute-start(f32[2,64,128]{2,1,0:T(8,128)S(1)} %get-tuple-element.93), channel_id=1, source_target_pairs={{0,2},{1,3},{2,0},{3,1},{4,6},{5,7},{6,4},{7,5},{8,10},{9,11},{10,... | collective-permute-start | bytes 196616 | tf_op jit(solution)/shard_map/ppermute | solution.py:406
  115.5 4.2 %collective-permute-start.17 = (f32[2,64,128]{2,1,0:T(8,128)S(1)}, f32[2,64,128]{2,1,0:T(8,128)S(1)}, u32[]{:S(2)}, u32[]{:S(2)}) collective-permute-start(f32[2,64,128]{2,1,0:T(8,128)S(1)} %get-tuple-element.92), channel_id=1, source_target_pairs={{0,1},{1,0},{2,3},{3,2},{4,5},{5,4},{6,7},{7,6},{8,9},{9,8},{10,11... | collective-permute-start | bytes 196616 | tf_op jit(solution)/shard_map/ppermute | solution.py:406
  (11 other events, 50.0 us)

commit v2 on v1

v2 whole, which is shorter than its diff:
```python
import functools

import jax
import jax.numpy as jnp
from jax import lax
from jax.experimental import pallas as pl
from jax.experimental.pallas import tpu as pltpu
from jax.sharding import PartitionSpec as P

HEAD_DIM = 64
STATE = 128
HEADS = 8
WIDE = HEADS * HEAD_DIM

F32 = jnp.float32
BF16 = jnp.bfloat16
HIGHEST = lax.Precision.HIGHEST
NN = (((1,), (0,)), ((), ()))
NT = (((1,), (1,)), ((), ()))
TN = (((0,), (0,)), ((), ()))
VMEM_LIMIT = 16 * 1024 * 1024
VMEM_ALL = 61 * 1024 * 1024


def dot(a, b, dims=NN):
    return lax.dot_general(a, b, dims, preferred_element_type=F32)


def dot_full(a, b, dims=NN):
    return lax.dot_general(a, b, dims, precision=HIGHEST, preferred_element_type=F32)


def halves(a):
    high = a.astype(BF16)
    return high, (a - high.astype(F32)).astype(BF16)


def dot_halves(a, b, dims=NN):
    high, low = halves(a)
    return dot(high, b, dims) + dot(low, b, dims)


def at_least(shape, row_dim, col_dim):
    return lax.broadcasted_iota(jnp.int32, shape, row_dim) >= lax.broadcasted_iota(
        jnp.int32, shape, col_dim
    )


def spread_matrix(heads):
    shape = (heads, heads * HEAD_DIM)
    lane = lax.broadcasted_iota(jnp.int32, shape, 1)
    first = lax.broadcasted_iota(jnp.int32, shape, 0) * HEAD_DIM
    return jnp.where((lane >= first) & (lane < first + HEAD_DIM), 1.0, 0.0).astype(F32)


def lower_ones(length, row_dim, col_dim):
    return jnp.where(at_least((length, length), row_dim, col_dim), 1.0, 0.0).astype(F32)


def per_head(values):
    spread = spread_matrix(values.shape[1] // HEAD_DIM).astype(BF16)
    high, low = halves(values)
    return dot(spread, high, NT) + dot(spread, low, NT)


def first_half(rows):
    return lax.broadcasted_iota(jnp.int32, (rows, 2 * HEAD_DIM), 1) < HEAD_DIM


def over_lanes(columns):
    rows, heads = columns.shape
    half = first_half(rows)
    parts = []
    for head in range(0, heads, 2):
        left = jnp.broadcast_to(columns[:, head : head + 1], half.shape)
        right = jnp.broadcast_to(columns[:, head + 1 : head + 2], half.shape)
        parts.append(jnp.where(half, left, right))
    return jnp.concatenate(parts, axis=1)


def local_kernel(groups, decay_in, x_in, dy_in, b_in, c_in, *refs):
    chunks = x_in.shape[1] // WIDE
    late = chunks // 2
    count = 5 + chunks + late
    outs = refs[:count]
    decay_ref, x_ref, dy_ref, b_ref, c_ref = refs[count : count + 5]
    kept = refs[count + 5 : count + 10]
    rows_ref, columns_ref, into_ref, from_ref, totals_ref = kept
    messages, sends, small_sem, wide_sem, out_sem = refs[count + 10 :]
    pending = []

    def leave(source, target):
        copy = pltpu.make_async_copy(source, target, out_sem.at[len(pending)])
        copy.start()
        pending.append(copy)

    small = [
        pltpu.make_async_copy(source, target, small_sem.at[i])
        for i, (source, target) in enumerate(((decay_in, decay_ref), (b_in, b_ref), (c_in, c_ref)))
    ]
    wide = []
    for chunk in range(chunks):
        lanes = pl.ds(chunk * WIDE, WIDE)
        wide.append(
            [
                pltpu.make_async_copy(source.at[:, lanes], target.at[:, lanes], wide_sem.at[i, chunk])
                for i, (source, target) in enumerate(((x_in, x_ref), (dy_in, dy_ref)))
            ]
        )
    for copy in small + [copy for pair in wide for copy in pair]:
        copy.start()
    last_group = lax.axis_index("ctx") // 2 == groups - 1
    small[0].wait()
    length = decay_ref.shape[1]
    rows = dot_full(decay_ref[...], lower_ones(length, 1, 0))
    rows_ref[...] = rows
    columns_ref[...] = rows.T
    into_end = jnp.exp(rows[:, length - 1 : length] - rows)
    from_start = jnp.exp(rows)
    into_ref[...] = into_end.T
    from_column = from_start.T
    from_ref[...] = from_column
    small[1].wait()
    small[2].wait()
    b_t = b_ref[...].astype(F32).T
    c_t = c_ref[...].astype(F32).T
    half = first_half(STATE)

    def gathered(proj, factors, values_ref, pair):
        head = 2 * pair
        scaled = jnp.concatenate(
            [proj * factors[head : head + 1, :], proj * factors[head + 1 : head + 2, :]], axis=0
        )
        sums = dot(scaled.astype(BF16), values_ref[:, pl.ds(pair * STATE, STATE)])
        return jnp.where(half, sums[:STATE], sums[STATE:])

    for chunk in range(chunks):
        lanes = pl.ds(chunk * WIDE, WIDE)
        heads = slice(chunk * HEADS, (chunk + 1) * HEADS)
        pairs = range(chunk * HEADS // 2, (chunk + 1) * HEADS // 2)
        totals_ref[:, lanes] = over_lanes(from_column[length - 8 :, heads])[7:8, :]
        for place, (proj, factors, values_ref, rows_at) in enumerate(
            ((b_t, into_end, x_ref, 0), (c_t, from_start, dy_ref, STATE))
        ):
            wide[chunk][place].wait()
            for pair in pairs:
                at = (pair - pairs[0]) * STATE
                messages[chunk, rows_at : rows_at + STATE, at : at + STATE] = gathered(
                    proj, factors, values_ref, pair
                )
        leave(messages.at[chunk], outs[5 + chunk])
        if chunk >= chunks - late:
            sends[chunk - chunks + late] = jnp.where(
                last_group, messages[chunk, STATE:, :], messages[chunk, :STATE, :]
            )
            leave(sends.at[chunk - chunks + late], outs[5 + late + chunk])
    for source, target in zip(kept, outs[:5]):
        leave(source, target)
    for copy in pending:
        copy.wait()


def intra_kernel(
    chunk,
    rows_ref,
    columns_ref,
    into_ref,
    from_ref,
    x_ref,
    dy_ref,
    b_ref,
    c_ref,
    dx_ref,
    xs_ref,
    dys_ref,
    change_ref,
    gb_ref,
    gc_ref,
    table_ref,
):
    rows = rows_ref[...]
    heads = slice(chunk * HEADS, (chunk + 1) * HEADS)
    columns = columns_ref[:, heads]
    xs_ref[...] = (x_ref[...].astype(F32) * over_lanes(into_ref[:, heads])).astype(BF16)
    dys_ref[...] = (dy_ref[...].astype(F32) * over_lanes(from_ref[:, heads])).astype(BF16)
    length = rows.shape[1]
    b, c = b_ref[...], c_ref[...]
    scores = dot(b, c, NT)
    size = STATE
    keep = at_least((size, size), 1, 0)
    half = first_half(size)
    blocks = length // size

    table_ref[...] = jnp.zeros_like(table_ref)

    for pair in range(HEADS // 2):
        lanes = slice(pair * 2 * HEAD_DIM, (pair + 1) * 2 * HEAD_DIM)
        dy2 = dy_ref[:, lanes]
        sums = [None, None]
        for block in range(blocks):
            first = block * size
            x2 = x_ref[first : first + size, lanes].astype(F32)
            parts = []
            for side in range(2):
                head = 2 * pair + side
                own = half if side == 0 else jnp.logical_not(half)
                x1 = jnp.where(own, x2, 0.0).astype(BF16)
                pairs = dot(x1, dy2[first:], NT)
                gap = rows[head : head + 1, first:] - columns[first : first + size, head : head + 1]
                near = jnp.where(keep, gap[:, :size], -1e30)
                if length - first > size:
                    near = jnp.concatenate([near, gap[:, size:]], axis=1)
                mask = jnp.exp(near)
                weights = (mask * scores[first : first + size, first:]).astype(BF16)
                table_ref[first : first + size, first:] += mask * pairs
                change = jnp.sum(weights.astype(F32) * pairs, axis=0, keepdims=True)
                if block == 0:
                    sums[side] = change
                else:
                    sums[side] = jnp.concatenate(
                        [sums[side][:, :first], sums[side][:, first:] + change], axis=1
                    )
                parts.append(dot(weights, dy2[first:]))
            dx_ref[first : first + size, lanes] = jnp.where(half, parts[0], parts[1])
        for side in range(2):
            head = 2 * pair + side
            change_ref[head : head + 1, :] = sums[side]

    change_ref[...] -= per_head(x_ref[...].astype(F32) * dx_ref[...])
    table = table_ref[...]
    gb_ref[...] = dot_halves(table, c)
    gc_ref[...] = dot_halves(table, b, TN)


def inter_kernel(
    chunk,
    into_ref,
    state_in_ref,
    adjoint_in_ref,
    total_ref,
    xs_ref,
    dys_ref,
    b_ref,
    c_ref,
    dx_ref,
    gb_ref,
    gc_ref,
    gx_ref,
    change_ref,
    earlier_ref,
    later_ref,
    gb_out_ref,
    gc_out_ref,
):
    lanes = slice(chunk * WIDE, (chunk + 1) * WIDE)
    heads = slice(chunk * HEADS, (chunk + 1) * HEADS)
    state_in = state_in_ref[...]
    adjoint_in = adjoint_in_ref[...]
    state_low = state_in.astype(BF16)
    adjoint_low = adjoint_in.astype(BF16)
    xs = xs_ref[...]
    dys = dys_ref[...]
    gb_out_ref[...] = gb_ref[...] + dot(xs, adjoint_low, NT)
    gc_out_ref[...] = gc_ref[...] + dot(dys, state_low, NT)
    outer = dot(b_ref[...], adjoint_low)
    gx_ref[...] = (dx_ref[...] + over_lanes(into_ref[:, heads]) * outer).astype(BF16)
    change_ref[...] = per_head(dys.astype(F32) * dot(c_ref[...], state_low))
    earlier_ref[...] = per_head(xs.astype(F32) * outer)
    later_ref[...] = per_head(total_ref[:, lanes] * state_in * adjoint_in)


def suffix_kernel(chunks, *refs):
    out_ref = refs[-1]
    length = out_ref.shape[1]

    def joined(place):
        return jnp.concatenate([ref[...] for ref in refs[place * chunks : (place + 1) * chunks]], 0)

    from_here = dot_full(joined(0) + joined(1), lower_ones(length, 0, 1))
    before = dot_full(joined(2), 1.0 - lower_ones(length, 0, 1))
    out_ref[...] = from_here + before + jnp.sum(joined(3), axis=1, keepdims=True)


def params(limit=VMEM_LIMIT):
    return pltpu.CompilerParams(vmem_limit_bytes=limit)


def cost(flops, nbytes):
    return pl.CostEstimate(flops=flops, bytes_accessed=nbytes, transcendentals=0)


def shape(dims, dtype=F32):
    return jax.ShapeDtypeStruct(dims, dtype)


def vmem(count):
    return [pl.BlockSpec(memory_space=pltpu.VMEM)] * count


def local_states(groups, log_decay, x, dy, b, c):
    tokens, width = x.shape
    heads = log_decay.shape[0]
    chunks = width // WIDE
    kept = [(heads, tokens)] + [(tokens, heads)] * 3 + [(1, width)]
    late = chunks // 2
    outs = kept + [(2 * STATE, WIDE)] * chunks + [(STATE, WIDE)] * late
    hbm = pl.BlockSpec(memory_space=pltpu.HBM)
    outs = pl.pallas_call(
        functools.partial(local_kernel, groups),
        in_specs=[hbm] * 5,
        out_specs=[hbm] * len(outs),
        out_shape=[shape(dims) for dims in outs],
        scratch_shapes=[
            pltpu.VMEM(log_decay.shape, F32),
            pltpu.VMEM(x.shape, BF16),
            pltpu.VMEM(x.shape, BF16),
            pltpu.VMEM(b.shape, BF16),
            pltpu.VMEM(b.shape, BF16),
            *[pltpu.VMEM(dims, F32) for dims in kept],
            pltpu.VMEM((chunks, 2 * STATE, WIDE), F32),
            pltpu.VMEM((late, STATE, WIDE), F32),
            pltpu.SemaphoreType.DMA((3,)),
            pltpu.SemaphoreType.DMA((2, chunks)),
            pltpu.SemaphoreType.DMA((len(outs),)),
        ],
        compiler_params=params(VMEM_ALL),
        cost_estimate=cost(4 * tokens * STATE * width, 12 * tokens * width),
        name="local_states",
    )(log_decay, x, dy, b, c)
    return outs[:5], outs[5 : 5 + chunks], [None] * (chunks - late) + list(outs[5 + chunks :])


def intra(chunk, rows, columns, into, start, x, dy, b, c):
    tokens = x.shape[0]
    wide = pl.BlockSpec((tokens, WIDE), lambda k: (0, chunk))
    proj = pl.BlockSpec((tokens, STATE), lambda k: (0, 0))
    return pl.pallas_call(
        functools.partial(intra_kernel, chunk),
        grid=(1,),
        in_specs=[
            pl.BlockSpec((HEADS, tokens), lambda k: (chunk, 0)),
            *[pl.BlockSpec(columns.shape, lambda k: (0, 0))] * 3,
            wide,
            wide,
            proj,
            proj,
        ],
        out_specs=[
            *[pl.BlockSpec((tokens, WIDE), lambda k: (0, 0))] * 3,
            pl.BlockSpec((HEADS, tokens), lambda k: (0, 0)),
            proj,
            proj,
        ],
        out_shape=[
            shape((tokens, WIDE)),
            shape((tokens, WIDE), BF16),
            shape((tokens, WIDE), BF16),
            shape((HEADS, tokens)),
            shape((tokens, STATE)),
            shape((tokens, STATE)),
        ],
        scratch_shapes=[pltpu.VMEM((tokens, tokens), F32)],
        compiler_params=params(),
        cost_estimate=cost(4 * tokens * tokens * WIDE, 8 * tokens * WIDE),
        name="intra",
    )(rows, columns, into, start, x, dy, b, c)


def inter(chunk, into, state_in, adjoint_in, totals, xs, dys, b, c, dx, gb, gc):
    tokens = xs.shape[0]
    args = (into, state_in, adjoint_in, totals, xs, dys, b, c, dx, gb, gc)
    out_shape = [
        shape((tokens, WIDE), BF16),
        shape((HEADS, tokens)),
        shape((HEADS, tokens)),
        shape((HEADS, STATE)),
        shape((tokens, STATE)),
        shape((tokens, STATE)),
    ]
    return pl.pallas_call(
        functools.partial(inter_kernel, chunk),
        in_specs=vmem(len(args)),
        out_specs=vmem(len(out_shape)),
        out_shape=out_shape,
        compiler_params=params(),
        cost_estimate=cost(8 * tokens * STATE * WIDE, 16 * tokens * WIDE),
        name="inter",
    )(*args)


def suffix_sums(*parts):
    chunks = len(parts[0])
    args = [item for part in parts for item in part]
    return pl.pallas_call(
        functools.partial(suffix_kernel, chunks),
        in_specs=vmem(len(args)),
        out_specs=vmem(1)[0],
        out_shape=shape((chunks * HEADS, args[0].shape[1])),
        compiler_params=params(),
        cost_estimate=cost(0, 1 << 17),
        name="suffix_sums",
    )(*args)


class Chunk:
    def __init__(self, first, message, own, other, diagonal, second):
        self.first, self.own, self.other, self.second = first, own, other, second
        self.state, self.adjoint = message[:STATE], message[STATE:]
        both = own * other
        if first:
            self.step_f = self.step_b = both
            self.seen_f = self.seen_b = jnp.ones_like(own)
        else:
            self.forward, self.backward = self.state, self.adjoint
            self.step_f, self.step_b = jnp.where(second, both, own), jnp.where(second, own, both)
            self.seen_f = jnp.where(second, 1.0, diagonal)
            self.seen_b = jnp.where(second, diagonal, 1.0)

    def joined(self, got):
        self.got_f, self.got_b = got[:STATE], got[STATE:]
        own, other = self.own, self.other
        self.forward = jnp.where(
            self.second, own * self.got_f + self.state, other * self.state + self.got_f
        )
        self.backward = jnp.where(
            self.second, self.got_b + other * self.adjoint, self.adjoint + own * self.got_b
        )

    def leaving_f(self, carried):
        return self.step_f * carried + self.forward

    def leaving_b(self, carried):
        return self.step_b * carried + self.backward

    def message(self):
        send_f = jnp.where(self.second, self.in_f, self.own * self.in_f + self.state)
        send_b = jnp.where(self.second, self.own * self.in_b + self.adjoint, self.in_b)
        return jnp.concatenate([send_f, send_b], axis=0)

    def entering(self, got=None):
        decayed_f = jnp.where(self.second, self.other, 1.0) * self.in_f
        decayed_b = jnp.where(self.second, 1.0, self.other) * self.in_b
        if got is not None:
            return decayed_f + got[:STATE], decayed_b + got[STATE:]
        return (
            decayed_f + jnp.where(self.second, self.got_f, 0.0),
            decayed_b + jnp.where(self.second, 0.0, self.got_b),
        )


def between(links):
    return [(2 * s + side, 2 * t + side) for s, t in links for side in range(2)]


def group_scan(chunk, group, groups):
    carried_f, carried_b = jnp.zeros_like(chunk.forward), jnp.zeros_like(chunk.backward)
    for hop in range(1, groups):
        send = jnp.where(
            group == groups - hop, chunk.leaving_b(carried_b), chunk.leaving_f(carried_f)
        )
        links = [(hop - 1, hop), (groups - hop, groups - hop - 1)]
        got = lax.ppermute(send, "ctx", between(links))
        carried_f = jnp.where(group == hop, chunk.seen_f * got, carried_f)
        carried_b = jnp.where(group == groups - hop - 1, chunk.seen_b * got, carried_b)
    chunk.in_f, chunk.in_b = carried_f, carried_b


class Four:
    def __init__(self, group):
        self.lower = group < 2
        self.inner = (group == 1) | (group == 2)

    def first(self, chunk):
        return jnp.where(self.lower, chunk.forward, chunk.backward)

    def second(self, chunk, got):
        chunk.hop1 = got
        scale = jnp.where(self.lower, chunk.step_f * chunk.seen_f, chunk.step_b * chunk.seen_b)
        return scale * got + jnp.where(self.lower, chunk.forward, chunk.backward)

    def third(self, chunk, got):
        chunk.hop2 = got
        scale = jnp.where(self.lower, chunk.step_b * chunk.seen_b, chunk.step_f * chunk.seen_f)
        return scale * got + jnp.where(self.lower, chunk.backward, chunk.forward)

    def done(self, chunk, got):
        near = jnp.where(self.inner, chunk.hop1, 0.0)
        far = jnp.where(self.inner, chunk.hop2, got)
        chunk.in_f = chunk.seen_f * jnp.where(self.lower, near, far)
        chunk.in_b = chunk.seen_b * jnp.where(self.lower, far, near)


def fence(*items):
    return lax.optimization_barrier(items)


def shards(inputs, grad_out, b_proj, c_proj, log_decay):
    count = lax.axis_size("ctx")
    mine = lax.axis_index("ctx")
    second = mine % 2 == 1
    group, groups = mine // 2, count // 2

    def permute(value, links):
        return lax.ppermute(value, "ctx", links)

    swap = [(i, i ^ 1) for i in range(count)]
    diagonals = [(2 * g + 1, 2 * g + 2) for g in range(groups - 1)]
    diagonals += [(t, s) for s, t in diagonals]

    (rows, columns, into, start, totals), messages, sends = local_states(
        groups, log_decay, inputs, grad_out, b_proj, c_proj
    )
    chunks = len(messages)
    other = permute(totals, swap)
    diagonal = permute(totals, diagonals)

    def chunk_of(k, first, message, other, diagonal):
        lanes = slice(k * WIDE, (k + 1) * WIDE)
        return Chunk(
            first, message, totals[:, lanes], other[:, lanes], diagonal[:, lanes], second
        )

    def local(k, rows, columns):
        return intra(k, rows, columns, into, start, inputs, grad_out, b_proj, c_proj)

    def carried(k, entering, near, gb, gc):
        dx, xs, dys = near[:3]
        return inter(k, into, *entering, totals, xs, dys, b_proj, c_proj, dx, gb, gc)

    near, far = [None] * chunks, [None] * chunks
    if groups == 4 and chunks == 4:
        four = Four(group)
        middle = between([(1, 2), (2, 1)])
        sides = between([(0, 1), (1, 0), (2, 3), (3, 2)])

        pair0 = permute(messages[0], swap)
        hop = permute(sends[2], sides)
        other, diagonal, hop, message1, send3, rows, columns = fence(
            other, diagonal, hop, messages[1], sends[3], rows, columns
        )
        c0 = chunk_of(0, True, messages[0], other, diagonal)
        c1 = chunk_of(1, True, message1, other, diagonal)
        c2 = chunk_of(2, False, messages[2], other, diagonal)
        c3 = chunk_of(3, False, messages[3], other, diagonal)

        mid = permute(four.second(c2, hop), middle)
        hop = permute(send3, sides)
        pair1 = permute(message1, swap)
        mid, hop, pair0, rows, columns = fence(mid, hop, pair0, rows, columns)
        c0.joined(pair0)

        side = permute(jnp.where(four.inner, four.third(c2, mid), four.first(c0)), sides)
        mid = permute(four.second(c3, hop), middle)
        near[0], near[1] = local(0, rows, columns), local(1, rows, columns)
        side, mid, pair1, near[0], near[1], rows = fence(side, mid, pair1, near[0], near[1], rows)
        four.done(c2, side)
        c1.joined(pair1)

        pair2 = permute(c2.message(), swap)
        hop = side
        side = permute(jnp.where(four.inner, four.third(c3, mid), four.first(c1)), sides)
        mid = permute(four.second(c0, hop), middle)
        near[2] = local(2, rows, columns)
        side, mid, near[2], rows = fence(side, mid, near[2], rows)
        four.done(c3, side)

        pair3 = permute(c3.message(), swap)
        hop = side
        side = permute(four.third(c0, mid), sides)
        mid = permute(four.second(c1, hop), middle)
        near[3] = local(3, rows, columns)
        gb = sum(item[4] for item in near)
        gc = sum(item[5] for item in near)
        side, mid, pair2, gb, gc = fence(side, mid, pair2, gb, gc)
        four.done(c0, side)

        side = permute(four.third(c1, mid), sides)
        *far[0], gb, gc = carried(0, c0.entering(), near[0], gb, gc)
        *far[2], gb, gc = carried(2, c2.entering(pair2), near[2], gb, gc)
        side, pair3, far[0], far[2], gb, gc = fence(side, pair3, far[0], far[2], gb, gc)
        four.done(c1, side)

        *far[1], gb, gc = carried(1, c1.entering(), near[1], gb, gc)
        *far[3], gb, gc = carried(3, c3.entering(pair3), near[3], gb, gc)
    else:
        near = [local(k, rows, columns) for k in range(chunks)]
        gb = sum(item[4] for item in near)
        gc = sum(item[5] for item in near)
        for k in range(chunks):
            first = k < chunks // 2
            chunk = chunk_of(k, first, messages[k], other, diagonal)
            if first:
                chunk.joined(permute(messages[k], swap))
            group_scan(chunk, group, groups)
            got = None if first else permute(chunk.message(), swap)
            *far[k], gb, gc = carried(k, chunk.entering(got), near[k], gb, gc)
    grad_x = jnp.concatenate([item[0] for item in far], axis=1)
    grad_decay = suffix_sums(
        [item[3] for item in near], *([item[i] for item in far] for i in (1, 2, 3))
    )

    ranks = lax.axis_size("head")
    rank = lax.axis_index("head")
    size = gb.shape[0] // ranks
    sums = jnp.stack([gb, gc])

    def piece(owner):
        return lax.dynamic_slice_in_dim(sums, owner * size, size, axis=1)

    parts = [piece(rank)]
    for step in range(1, ranks):
        links = [(i, i ^ step) for i in range(ranks)]
        parts.append(lax.ppermute(piece(rank ^ step), "head", links))
    grad_b, grad_c = (sum(part[i] for part in parts) for i in range(2))
    return grad_x, grad_b, grad_c, grad_decay


def solution(mesh):
    placed = (P("ctx", "head"), P("ctx", "head"), P("ctx", None), P("ctx", None), P("head", "ctx"))
    return jax.shard_map(
        shards,
        mesh=mesh,
        in_specs=placed,
        out_specs=(
            P("ctx", "head"),
            P(("ctx", "head"), None),
            P(("ctx", "head"), None),
            P("head", "ctx"),
        ),
        check_vma=False,
    )
```

time: 121 us -> 80.2 us (0.66)
  waiting for transfers between devices: 47.1 us -> 8.47 us
  Pallas kernels: 26.4 us -> 16.5 us
  starting transfers between devices: 27 us -> 36 us
  local copies, waits for them, and re-layouts: 7.19 us -> 5.35 us
    ppermute x20 -> x19, waiting for transfers between devices: 47.1 us -> 8.47 us  [the longest x16 6.62 us: permute(): return lax.ppermute(value, 'ctx', links)]
    pallas_call x7 -> x10, Pallas kernels: 26.4 us -> 16.5 us  [the longest x4 6.29 us: intra(): pl.pallas_call(functools.partial(intra_kernel, chunk), grid=(1,), in_spec...]
    ppermute x20 -> x19, starting transfers between devices: 27 us -> 36 us  [the longest x16 34.1 us: permute(): return lax.ppermute(value, 'ctx', links)]
    add x3 -> x10, other arithmetic: 0.22 us -> 3.57 us  [the longest x2 1.18 us: third(): return scale * got + jnp.where(self.lower, chunk.backward, chunk.forward)]
    concatenate x10 -> x3, other arithmetic: 3.55 us -> 2.2 us  [the longest x1 1.1 us: shards(): grad_x = jnp.concatenate([item[0] for item in far], axis=1)]
    select_n x11 -> x8, other arithmetic: 7.14 us -> 6 us  [the longest x1 2.54 us: shards(): jnp.where(four.inner, four.third(c3, mid), four.first(c1))]
    unnamed x30 -> x100, local copies, waits for them, and re-layouts: 5.64 us -> 4.67 us
  transfers between devices with their start and end apart: 20 -> 19, of which waited for: 9 -> 6; matrix products, arithmetic and copies ran while one was open for 10% -> 11% of each run, Pallas kernels for 14% -> 11%
where the time goes in v2:
time: 80.2 us; the launch traced here: 79.5 us
  starting transfers between devices  36 us (45%)
  Pallas kernels  16.5 us (21%)
  other arithmetic  11.8 us (15%)
  waiting for transfers between devices  8.47 us (11%)
  local copies, waits for them, and re-layouts  5.35 us (7%)
  between operations  1.38 us (2%)
    ppermute x16, starting transfers between devices, permute(): return lax.ppermute(value, 'ctx', links)  34.1 us
    ppermute x16, waiting for transfers between devices, permute(): return lax.ppermute(value, 'ctx', links)  6.62 us
    pallas_call x4, Pallas kernels, intra(): pl.pallas_call(functools.partial(intra_kernel, chunk), grid=(1,), in_spec...  6.29 us
    pallas_call x1, Pallas kernels, local_states(): pl.pallas_call(functools.partial(local_kernel, groups), in_specs=[hbm] *...  5.46 us
    unnamed x100, local copies, waits for them, and re-layouts  4.67 us
    pallas_call x4, Pallas kernels, inter(): pl.pallas_call(functools.partial(inter_kernel, chunk), in_specs=vmem(len(...  3.74 us
    select_n x1, other arithmetic, shards(): jnp.where(four.inner, four.third(c3, mid), four.first(c1))  2.54 us
    select_n x2, other arithmetic, message(): jnp.where(self.second, self.in_f, self.own * self.in_f + self.state)  2.37 us
  transfers between devices with their start and end apart: 19, of which 6 were waited for; matrix products, arithmetic and copies ran while one was open for 11% of the time, Pallas kernels for 11%

profile of v2, /device:TPU:0, one launch (start us, length us, event | category | flops | bytes accessed | tf_op | source)
XLA Modules:
  0.0 79.5 jit_solution(15149470773686708707)
XLA Ops:
  0.6 5.5 %local_states.1 = (f32[32,256]{1,0:T(8,128)}, f32[256,32]{1,0:T(8,128)}, f32[256,32]{1,0:T(8,128)}, f32[256,32]{1,0:T(8,128)}, f32[1,2048]{1,0:T(1,128)}, /*inde...) custom-call(f32[32,256]{1,0:T(8,128)} %decay_in.1, ...), custom_call_target="tpu_custom_call" | custom-call | flops 268435456 | bytes 6291456 | tf_op jit(solution)/shard_map/local_states/pallas_call | solution.py:308
  6.1 3.1 %collective-permute-start.2 = (f32[128,512]{1,0:T(8,128)}, f32[128,512]{1,0:T(8,128)S(1)}, u32[]{:S(2)}, u32[]{:S(2)}) collective-permute-start(f32[128,512]{1,0:T(8,128)} %get-tuple-element.118), channel_id=1, source_target_pairs={{0,8},{4,12},{8,0},{12,4},{16,24},{20,28},{24,16},{28,20},{1,9},{5... | collective-permute-start | bytes 786440 | tf_op jit(solution)/shard_map/ppermute | solution.py:504
  9.2 1.5 %collective-permute-start = (f32[1,2048]{1,0:T(1,128)}, f32[1,2048]{1,0:T(1,128)S(1)}, u32[]{:S(2)}, u32[]{:S(2)}) collective-permute-start(f32[1,2048]{1,0:T(1,128)} %get-tuple-element.117.total_ref), channel_id=1, source_target_pairs={{0,4},{4,0},{8,12},{12,8},{16,20},{20,16},{24,28},{28,24},{1,5},{5... | collective-permute-start | bytes 24584 | tf_op jit(solution)/shard_map/ppermute | solution.py:504
  11.4 3.2 %collective-permute-start.5 = (f32[256,512]{1,0:T(8,128)}, f32[256,512]{1,0:T(8,128)S(1)}, u32[]{:S(2)}, u32[]{:S(2)}) collective-permute-start(f32[256,512]{1,0:T(8,128)} %get-tuple-element.128), channel_id=1, source_target_pairs={{0,4},{4,0},{8,12},{12,8},{16,20},{20,16},{24,28},{28,24},{1,5},{5... | collective-permute-start | bytes 1572872 | tf_op jit(solution)/shard_map/ppermute | solution.py:504
  16.7 1.1 %select_add_fusion.7 = f32[128,512]{1,0:T(8,128)S(1)} fusion(f32[128,512]{1,0:T(8,128)S(1)} %collective-permute-done.2, f32[256,512]{1,0:T(8,128)} %get-tuple-element.126, f32[512]{0:T(512)S(1)} %bitcast.53, pred[]{:T(512)S(6)} %lt.21), kind=kLoop, calls=%fused_computation.38 | loop fusion | flops 196608 | bytes 1050625 | tf_op jit(solution)/shard_map/add | solution.py:479
  18.5 6.1 %collective-permute-start.4 = (f32[128,512]{1,0:T(8,128)}, f32[128,512]{1,0:T(8,128)S(1)}, u32[]{:S(2)}, u32[]{:S(2)}) collective-permute-start(f32[128,512]{1,0:T(8,128)} %get-tuple-element.127), channel_id=1, source_target_pairs={{0,8},{4,12},{8,0},{12,4},{16,24},{20,28},{24,16},{28,20},{1,9},{5... | collective-permute-start | bytes 786440 | tf_op jit(solution)/shard_map/ppermute | solution.py:504
  25.1 4.0 %collective-permute-done.4 = f32[128,512]{1,0:T(8,128)S(1)} collective-permute-done((f32[128,512]{1,0:T(8,128)}, f32[128,512]{1,0:T(8,128)S(1)}, u32[]{:S(2)}, u32[]{:S(2)}) %collective-permute-start.4) | collective-permute-done | bytes 262176 | tf_op jit(solution)/shard_map/ppermute | solution.py:504
  30.3 2.1 %collective-permute-start.6 = (f32[128,512]{1,0:T(8,128)S(1)}, f32[128,512]{1,0:T(8,128)S(1)}, u32[]{:S(2)}, u32[]{:S(2)}) collective-permute-start(f32[128,512]{1,0:T(8,128)S(1)} %get-tuple-element.244), channel_id=1, source_target_pairs={{0,8},{4,12},{8,0},{12,4},{16,24},{20,28},{24,16},{28,20},{1,9},{5... | collective-permute-start | bytes 786440 | tf_op jit(solution)/shard_map/ppermute | solution.py:504
  33.3 1.6 %intra.4 = (f32[256,512]{1,0:T(8,128)S(1)}, bf16[256,512]{1,0:T(8,128)(2,1)S(1)}, bf16[256,512]{1,0:T(8,128)(2,1)S(1)}, f32[8,256]{1,0:T(8,128)S(1)}, f32[256,128]{1,0:T(8,128)S(1)}, /*index=5*/f32[256,128]{1,0:T(8,128)S(1)}) custom-call(f32[32,256]{1,0:T(8,128)S(1)} %copy-done.9, f32[256,32]{1,0:T(8,128)S(1)} %copy-done.5, f32[256,32]{1,0:T(8,128)S(1)} %copy-done.2, ...), custom_call_target="tpu_custom_call" | custom-call | flops 134217728 | bytes 1048576 | tf_op jit(solution)/shard_map/intra/pallas_call | solution.py:337
  37.6 1.6 %intra.5 = (f32[256,512]{1,0:T(8,128)S(1)}, bf16[256,512]{1,0:T(8,128)(2,1)S(1)}, bf16[256,512]{1,0:T(8,128)(2,1)S(1)}, f32[8,256]{1,0:T(8,128)S(1)}, f32[256,128]{1,0:T(8,128)S(1)}, /*index=5*/f32[256,128]{1,0:T(8,128)S(1)}) custom-call(f32[32,256]{1,0:T(8,128)S(1)} %copy-done.9, f32[256,32]{1,0:T(8,128)S(1)} %copy-done.5, f32[256,32]{1,0:T(8,128)S(1)} %copy-done.2, ...), custom_call_target="tpu_custom_call" | custom-call | flops 134217728 | bytes 1048576 | tf_op jit(solution)/shard_map/intra/pallas_call | solution.py:337
  39.3 2.5 %add_select_fusion.6 = (f32[128,512]{1,0:T(8,128)}, f32[128,512]{1,0:T(8,128)}, f32[128,512]{1,0:T(8,128)}) fusion(f32[128,512]{1,0:T(8,128)S(1)} %collective-permute-done.7, f32[256,512]{1,0:T(8,128)S(1)} %copy-done.25, f32[512]{0:T(512)S(1)} %bitcast.48, pred[]{:T(512)S(6)} %lt.21, pred[]{:T(512)S(6)} %or.3, f32[512]{0:T(512)S(1)} %bitcast.40, ...), kind=kLoop, calls=%fused_computation.33 | loop fusion | flops 983040 | bytes 2627587 | tf_op jit(solution)/shard_map/jit(_where)/select_n | solution.py:561
  41.9 3.1 %collective-permute-start.9 = (f32[128,512]{1,0:T(8,128)}, f32[128,512]{1,0:T(8,128)}, u32[]{:S(2)}, u32[]{:S(2)}) collective-permute-start(f32[128,512]{1,0:T(8,128)} %get-tuple-element.238), channel_id=1, source_target_pairs={{0,8},{4,12},{8,0},{12,4},{16,24},{20,28},{24,16},{28,20},{1,9},{5... | collective-permute-start | bytes 786440 | tf_op jit(solution)/shard_map/ppermute | solution.py:504
  45.0 1.2 %add_select_fusion.3 = (f32[128,512]{1,0:T(8,128)}, f32[128,512]{1,0:T(8,128)}, f32[128,512]{1,0:T(8,128)}, f32[128,512]{1,0:T(8,128)}, f32[128,512]{1,0:T(8,128)}) fusion(f32[256,512]{1,0:T(8,128)S(1)} %copy-done.28, f32[512]{0:T(512)S(1)} %bitcast.47, pred[]{:T(512)S(6)} %eq.13, f32[128,512]{1,0:T(8,128)S(1)} %collective-permute-done.3, ...), kind=kLoop, calls=%fused_computation.26 | loop fusion | flops 983040 | bytes 3153923 | tf_op jit(solution)/shard_map/jit(_where)/select_n | solution.py:436
  46.2 1.4 %collective-permute-start.10 = (f32[128,512]{1,0:T(8,128)}, f32[128,512]{1,0:T(8,128)}, u32[]{:S(2)}, u32[]{:S(2)}) collective-permute-start(f32[128,512]{1,0:T(8,128)} %get-tuple-element.269), channel_id=1, source_target_pairs={{8,16},{12,20},{16,8},{20,12},{9,17},{13,21},{17,9},{21,13},{10,18... | collective-permute-start | bytes 786440 | tf_op jit(solution)/shard_map/ppermute | solution.py:504
  49.3 1.6 %intra.6 = (f32[256,512]{1,0:T(8,128)S(1)}, bf16[256,512]{1,0:T(8,128)(2,1)S(1)}, bf16[256,512]{1,0:T(8,128)(2,1)S(1)}, f32[8,256]{1,0:T(8,128)S(1)}, f32[256,128]{1,0:T(8,128)S(1)}, /*index=5*/f32[256,128]{1,0:T(8,128)S(1)}) custom-call(f32[32,256]{1,0:T(8,128)S(1)} %copy-done.9, f32[256,32]{1,0:T(8,128)S(1)} %copy-done.5, f32[256,32]{1,0:T(8,128)S(1)} %copy-done.2, ...), custom_call_target="tpu_custom_call" | custom-call | flops 134217728 | bytes 1048576 | tf_op jit(solution)/shard_map/intra/pallas_call | solution.py:337
  50.9 1.1 %select_add_fusion.5 = f32[128,512]{1,0:T(8,128)S(1)} fusion(f32[128,512]{1,0:T(8,128)S(1)} %copy-done.32, f32[128,512]{1,0:T(8,128)S(1)} %copy-done.34, f32[128,512]{1,0:T(8,128)} %collective-permute-done.10, f32[512]{0:T(512)S(1)} %bitcast.35, pred[]{:T(512)S(6)} %lt.21), kind=kLoop, calls=%fused_computation.29 | loop fusion | flops 196608 | bytes 1050625 | tf_op jit(solution)/shard_map/add | solution.py:484
  52.0 3.8 %collective-permute-start.11 = (f32[128,512]{1,0:T(8,128)S(1)}, f32[128,512]{1,0:T(8,128)S(1)}, u32[]{:S(2)}, u32[]{:S(2)}) collective-permute-start(f32[128,512]{1,0:T(8,128)S(1)} %select_add_fusion.5), channel_id=1, source_target_pairs={{0,8},{4,12},{8,0},{12,4},{16,24},{20,28},{24,16},{28,20},{1,9},{5... | collective-permute-start | bytes 786440 | tf_op jit(solution)/shard_map/ppermute | solution.py:504
  55.9 1.2 %add_select_fusion.1 = (f32[128,512]{1,0:T(8,128)S(1)}, f32[128,512]{1,0:T(8,128)S(1)}, f32[128,512]{1,0:T(8,128)S(1)}, f32[128,512]{1,0:T(8,128)S(1)}, f32[128,512]{1,0:T(8,128)S(1)}) fusion(f32[256,512]{1,0:T(8,128)S(1)} %copy-done.26, f32[512]{0:T(512)S(1)} %bitcast.44, pred[]{:T(512)S(6)} %eq.13, f32[128,512]{1,0:T(8,128)S(1)} %copy-done.40, ...), kind=kLoop, calls=%fused_computation.21 | loop fusion | flops 983040 | bytes 3153923 | tf_op jit(solution)/shard_map/jit(_where)/select_n | solution.py:436
  58.0 1.6 %intra.7 = (f32[256,512]{1,0:T(8,128)S(1)}, bf16[256,512]{1,0:T(8,128)(2,1)S(1)}, bf16[256,512]{1,0:T(8,128)(2,1)S(1)}, f32[8,256]{1,0:T(8,128)S(1)}, f32[256,128]{1,0:T(8,128)S(1)}, /*index=5*/f32[256,128]{1,0:T(8,128)S(1)}) custom-call(f32[32,256]{1,0:T(8,128)S(1)} %copy-done.9, f32[256,32]{1,0:T(8,128)S(1)} %copy-done.5, f32[256,32]{1,0:T(8,128)S(1)} %copy-done.2, ...), custom_call_target="tpu_custom_call" | custom-call | flops 134217728 | bytes 1048576 | tf_op jit(solution)/shard_map/intra/pallas_call | solution.py:337
  60.5 5.0 %collective-permute-start.14 = (f32[128,512]{1,0:T(8,128)S(1)}, f32[128,512]{1,0:T(8,128)S(1)}, u32[]{:S(2)}, u32[]{:S(2)}) collective-permute-start(f32[128,512]{1,0:T(8,128)S(1)} %select_add_fusion.4), channel_id=1, source_target_pairs={{0,8},{4,12},{8,0},{12,4},{16,24},{20,28},{24,16},{28,20},{1,9},{5... | collective-permute-start | bytes 786440 | tf_op jit(solution)/shard_map/ppermute | solution.py:504
  67.9 1.9 %collective-permute-done.15 = f32[256,512]{1,0:T(8,128)S(1)} collective-permute-done((f32[256,512]{1,0:T(8,128)S(1)}, f32[256,512]{1,0:T(8,128)S(1)}, u32[]{:S(2)}, u32[]{:S(2)}) %collective-permute-start.15) | collective-permute-done | bytes 524320 | tf_op jit(solution)/shard_map/ppermute | solution.py:504
  73.0 1.6 %collective-permute-start.17 = (f32[2,64,128]{2,1,0:T(8,128)S(1)}, f32[2,64,128]{2,1,0:T(8,128)S(1)}, u32[]{:S(2)}, u32[]{:S(2)}) collective-permute-start(f32[2,64,128]{2,1,0:T(8,128)S(1)} %get-tuple-element.266), channel_id=1, source_target_pairs={{0,2},{1,3},{2,0},{3,1},{4,6},{5,7},{6,4},{7,5},{8,10},{9,11},{10,... | collective-permute-start | bytes 196616 | tf_op jit(solution)/shard_map/ppermute | solution.py:613
  74.9 1.1 %pad_maximum_fusion = bf16[256,2048]{1,0:T(8,128)(2,1)} fusion(bf16[256,512]{1,0:T(8,128)(2,1)S(1)} %get-tuple-element.211, bf16[256,512]{1,0:T(8,128)(2,1)S(1)} %get-tuple-element.204, bf16[256,512]{1,0:T(8,128)(2,1)S(1)} %get-tuple-element.203, bf16[256,512]{1,0:T(8,128)(2,1)S(1)} %get-tuple-element.196), kind=kLoop, calls=%fused_computation | loop fusion | flops 4194304 | bytes 2097152 | tf_op jit(solution)/shard_map/concatenate | solution.py:597
  77.3 1.5 %collective-permute-done.17 = f32[2,64,128]{2,1,0:T(8,128)S(1)} collective-permute-done((f32[2,64,128]{2,1,0:T(8,128)S(1)}, f32[2,64,128]{2,1,0:T(8,128)S(1)}, u32[]{:S(2)}, u32[]{:S(2)}) %collective-permute-start.17) | collective-permute-done | bytes 65568 | tf_op jit(solution)/shard_map/ppermute | solution.py:613
  (147 shorter events, 19.9 us)
Async XLA Ops:
  6.1 23.9 %copy-start.27 = (f32[256,512]{1,0:T(8,128)S(1)}, f32[256,512]{1,0:T(8,128)}, u32[]{:S(2)}) copy-start(f32[256,512]{1,0:T(8,128)} %get-tuple-element.126) | copy-start | bytes 1572868
  6.1 23.9 %copy-start.49 = (f32[256,512]{1,0:T(8,128)S(1)}, f32[256,512]{1,0:T(8,128)}, u32[]{:S(2)}) copy-start(f32[256,512]{1,0:T(8,128)} %get-tuple-element.128) | copy-start | bytes 1572868
  6.1 9.7 %collective-permute-start.2 = (f32[128,512]{1,0:T(8,128)}, f32[128,512]{1,0:T(8,128)S(1)}, u32[]{:S(2)}, u32[]{:S(2)}) collective-permute-start(f32[128,512]{1,0:T(8,128)} %get-tuple-element.118), channel_id=1, source_target_pairs={{0,8},{4,12},{8,0},{12,4},{16,24},{20,28},{24,16},{28,20},{1,9},{5... | collective-permute-start | bytes 786440 | tf_op jit(solution)/shard_map/ppermute | solution.py:504
  9.2 6.1 %collective-permute-start = (f32[1,2048]{1,0:T(1,128)}, f32[1,2048]{1,0:T(1,128)S(1)}, u32[]{:S(2)}, u32[]{:S(2)}) collective-permute-start(f32[1,2048]{1,0:T(1,128)} %get-tuple-element.117.total_ref), channel_id=1, source_target_pairs={{0,4},{4,0},{8,12},{12,8},{16,20},{20,16},{24,28},{28,24},{1,5},{5... | collective-permute-start | bytes 24584 | tf_op jit(solution)/shard_map/ppermute | solution.py:504
  10.7 4.6 %collective-permute-start.1 = (f32[1,2048]{1,0:T(1,128)}, f32[1,2048]{1,0:T(1,128)S(1)}, u32[]{:S(2)}, u32[]{:S(2)}) collective-permute-start(f32[1,2048]{1,0:T(1,128)} %get-tuple-element.117.total_ref), channel_id=1, source_target_pairs={{4,8},{12,16},{20,24},{8,4},{16,12},{24,20},{5,9},{13,17},{21,25},... | collective-permute-start | bytes 24584 | tf_op jit(solution)/shard_map/ppermute | solution.py:504
  11.4 17.8 %collective-permute-start.5 = (f32[256,512]{1,0:T(8,128)}, f32[256,512]{1,0:T(8,128)S(1)}, u32[]{:S(2)}, u32[]{:S(2)}) collective-permute-start(f32[256,512]{1,0:T(8,128)} %get-tuple-element.128), channel_id=1, source_target_pairs={{0,4},{4,0},{8,12},{12,8},{16,20},{20,16},{24,28},{28,24},{1,5},{5... | collective-permute-start | bytes 1572872 | tf_op jit(solution)/shard_map/ppermute | solution.py:504
  15.8 13.3 %copy-start.41 = (f32[128,512]{1,0:T(8,128)}, f32[128,512]{1,0:T(8,128)S(1)}, u32[]{:S(2)}) copy-start(f32[128,512]{1,0:T(8,128)S(1)} %collective-permute-done.2) | copy-start | bytes 786436
  17.8 7.3 %collective-permute-start.3 = (f32[128,512]{1,0:T(8,128)S(1)}, f32[128,512]{1,0:T(8,128)S(1)}, u32[]{:S(2)}, u32[]{:S(2)}) collective-permute-start(f32[128,512]{1,0:T(8,128)S(1)} %select_add_fusion.7), channel_id=1, source_target_pairs={{8,16},{12,20},{16,8},{20,12},{9,17},{13,21},{17,9},{21,13},{10,18... | collective-permute-start | bytes 786440 | tf_op jit(solution)/shard_map/ppermute | solution.py:504
  18.5 10.7 %collective-permute-start.4 = (f32[128,512]{1,0:T(8,128)}, f32[128,512]{1,0:T(8,128)S(1)}, u32[]{:S(2)}, u32[]{:S(2)}) collective-permute-start(f32[128,512]{1,0:T(8,128)} %get-tuple-element.127), channel_id=1, source_target_pairs={{0,8},{4,12},{8,0},{12,4},{16,24},{20,28},{24,16},{28,20},{1,9},{5... | collective-permute-start | bytes 786440 | tf_op jit(solution)/shard_map/ppermute | solution.py:504
  24.6 14.7 %collective-permute-start.8 = (f32[256,512]{1,0:T(8,128)}, f32[256,512]{1,0:T(8,128)S(1)}, u32[]{:S(2)}, u32[]{:S(2)}) collective-permute-start(f32[256,512]{1,0:T(8,128)} %get-tuple-element.135), channel_id=1, source_target_pairs={{0,4},{4,0},{8,12},{12,8},{16,20},{20,16},{24,28},{28,24},{1,5},{5... | collective-permute-start | bytes 1572872 | tf_op jit(solution)/shard_map/ppermute | solution.py:504
  30.3 14.6 %copy-start.31 = (f32[128,512]{1,0:T(8,128)}, f32[128,512]{1,0:T(8,128)S(1)}, u32[]{:S(2)}) copy-start(f32[128,512]{1,0:T(8,128)S(1)} %get-tuple-element.245) | copy-start | bytes 786436
  30.3 14.6 %copy-start.33 = (f32[128,512]{1,0:T(8,128)}, f32[128,512]{1,0:T(8,128)S(1)}, u32[]{:S(2)}) copy-start(f32[128,512]{1,0:T(8,128)S(1)} %get-tuple-element.246) | copy-start | bytes 786436
  30.3 8.9 %collective-permute-start.6 = (f32[128,512]{1,0:T(8,128)S(1)}, f32[128,512]{1,0:T(8,128)S(1)}, u32[]{:S(2)}, u32[]{:S(2)}) collective-permute-start(f32[128,512]{1,0:T(8,128)S(1)} %get-tuple-element.244), channel_id=1, source_target_pairs={{0,8},{4,12},{8,0},{12,4},{16,24},{20,28},{24,16},{28,20},{1,9},{5... | collective-permute-start | bytes 786440 | tf_op jit(solution)/shard_map/ppermute | solution.py:504
  32.5 6.7 %collective-permute-start.7 = (f32[128,512]{1,0:T(8,128)S(1)}, f32[128,512]{1,0:T(8,128)S(1)}, u32[]{:S(2)}, u32[]{:S(2)}) collective-permute-start(f32[128,512]{1,0:T(8,128)S(1)} %select_add_fusion.6), channel_id=1, source_target_pairs={{8,16},{12,20},{16,8},{20,12},{9,17},{13,21},{17,9},{21,13},{10,18... | collective-permute-start | bytes 786440 | tf_op jit(solution)/shard_map/ppermute | solution.py:504
  41.9 9.0 %collective-permute-start.9 = (f32[128,512]{1,0:T(8,128)}, f32[128,512]{1,0:T(8,128)}, u32[]{:S(2)}, u32[]{:S(2)}) collective-permute-start(f32[128,512]{1,0:T(8,128)} %get-tuple-element.238), channel_id=1, source_target_pairs={{0,8},{4,12},{8,0},{12,4},{16,24},{20,28},{24,16},{28,20},{1,9},{5... | collective-permute-start | bytes 786440 | tf_op jit(solution)/shard_map/ppermute | solution.py:504
  46.2 4.7 %collective-permute-start.10 = (f32[128,512]{1,0:T(8,128)}, f32[128,512]{1,0:T(8,128)}, u32[]{:S(2)}, u32[]{:S(2)}) collective-permute-start(f32[128,512]{1,0:T(8,128)} %get-tuple-element.269), channel_id=1, source_target_pairs={{8,16},{12,20},{16,8},{20,12},{9,17},{13,21},{17,9},{21,13},{10,18... | collective-permute-start | bytes 786440 | tf_op jit(solution)/shard_map/ppermute | solution.py:504
  48.6 11.8 %collective-permute-start.13 = (f32[256,512]{1,0:T(8,128)S(1)}, f32[256,512]{1,0:T(8,128)S(1)}, u32[]{:S(2)}, u32[]{:S(2)}) collective-permute-start(f32[256,512]{1,0:T(8,128)S(1)} %pad_maximum_fusion.1), channel_id=1, source_target_pairs={{0,4},{4,0},{8,12},{12,8},{16,20},{20,16},{24,28},{28,24},{1,5},{5... | collective-permute-start | bytes 1572872 | tf_op jit(solution)/shard_map/ppermute | solution.py:504
  52.0 8.4 %collective-permute-start.11 = (f32[128,512]{1,0:T(8,128)S(1)}, f32[128,512]{1,0:T(8,128)S(1)}, u32[]{:S(2)}, u32[]{:S(2)}) collective-permute-start(f32[128,512]{1,0:T(8,128)S(1)} %select_add_fusion.5), channel_id=1, source_target_pairs={{0,8},{4,12},{8,0},{12,4},{16,24},{20,28},{24,16},{28,20},{1,9},{5... | collective-permute-start | bytes 786440 | tf_op jit(solution)/shard_map/ppermute | solution.py:504
  57.1 3.3 %collective-permute-start.12 = (f32[128,512]{1,0:T(8,128)S(1)}, f32[128,512]{1,0:T(8,128)S(1)}, u32[]{:S(2)}, u32[]{:S(2)}) collective-permute-start(f32[128,512]{1,0:T(8,128)S(1)} %get-tuple-element.268), channel_id=1, source_target_pairs={{8,16},{12,20},{16,8},{20,12},{9,17},{13,21},{17,9},{21,13},{10,18... | collective-permute-start | bytes 786440 | tf_op jit(solution)/shard_map/ppermute | solution.py:504
  59.6 10.1 %collective-permute-start.15 = (f32[256,512]{1,0:T(8,128)S(1)}, f32[256,512]{1,0:T(8,128)S(1)}, u32[]{:S(2)}, u32[]{:S(2)}) collective-permute-start(f32[256,512]{1,0:T(8,128)S(1)} %pad_maximum_fusion.2), channel_id=1, source_target_pairs={{0,4},{4,0},{8,12},{12,8},{16,20},{20,16},{24,28},{28,24},{1,5},{5... | collective-permute-start | bytes 1572872 | tf_op jit(solution)/shard_map/ppermute | solution.py:504
  60.5 9.4 %collective-permute-start.14 = (f32[128,512]{1,0:T(8,128)S(1)}, f32[128,512]{1,0:T(8,128)S(1)}, u32[]{:S(2)}, u32[]{:S(2)}) collective-permute-start(f32[128,512]{1,0:T(8,128)S(1)} %select_add_fusion.4), channel_id=1, source_target_pairs={{0,8},{4,12},{8,0},{12,4},{16,24},{20,28},{24,16},{28,20},{1,9},{5... | collective-permute-start | bytes 786440 | tf_op jit(solution)/shard_map/ppermute | solution.py:504
  73.0 4.4 %collective-permute-start.18 = (f32[2,64,128]{2,1,0:T(8,128)S(1)}, f32[2,64,128]{2,1,0:T(8,128)S(1)}, u32[]{:S(2)}, u32[]{:S(2)}) collective-permute-start(f32[2,64,128]{2,1,0:T(8,128)S(1)} %get-tuple-element.267), channel_id=1, source_target_pairs={{0,3},{1,2},{2,1},{3,0},{4,7},{5,6},{6,5},{7,4},{8,11},{9,10},{10,... | collective-permute-start | bytes 196616 | tf_op jit(solution)/shard_map/ppermute | solution.py:613
  73.0 5.8 %collective-permute-start.17 = (f32[2,64,128]{2,1,0:T(8,128)S(1)}, f32[2,64,128]{2,1,0:T(8,128)S(1)}, u32[]{:S(2)}, u32[]{:S(2)}) collective-permute-start(f32[2,64,128]{2,1,0:T(8,128)S(1)} %get-tuple-element.266), channel_id=1, source_target_pairs={{0,2},{1,3},{2,0},{3,1},{4,6},{5,7},{6,4},{7,5},{8,10},{9,11},{10,... | collective-permute-start | bytes 196616 | tf_op jit(solution)/shard_map/ppermute | solution.py:613
  74.6 4.2 %collective-permute-start.16 = (f32[2,64,128]{2,1,0:T(8,128)S(1)}, f32[2,64,128]{2,1,0:T(8,128)S(1)}, u32[]{:S(2)}, u32[]{:S(2)}) collective-permute-start(f32[2,64,128]{2,1,0:T(8,128)S(1)} %get-tuple-element.265), channel_id=1, source_target_pairs={{0,1},{1,0},{2,3},{3,2},{4,5},{5,4},{6,7},{7,6},{8,9},{9,8},{10,11... | collective-permute-start | bytes 196616 | tf_op jit(solution)/shard_map/ppermute | solution.py:613
  (45 other events, 146.7 us)

commit v3 on v2

--- a/solution.py
+++ b/solution.py
@@ -82,11 +82,14 @@
     chunks = x_in.shape[1] // WIDE
     late = chunks // 2
     count = 5 + chunks + late
+    lower = lax.axis_index("ctx") // 2 < groups // 2
+    near_at = pl.multiple_of(jnp.where(lower, 0, STATE), STATE)
+    far_at = pl.multiple_of(jnp.where(lower, STATE, 0), STATE)
     outs = refs[:count]
     decay_ref, x_ref, dy_ref, b_ref, c_ref = refs[count : count + 5]
     kept = refs[count + 5 : count + 10]
     rows_ref, columns_ref, into_ref, from_ref, totals_ref = kept
-    messages, sends, small_sem, wide_sem, out_sem = refs[count + 10 :]
+    messages, small_sem, wide_sem, out_sem = refs[count + 10 :]
     pending = []
 
     def leave(source, target):
@@ -109,17 +112,15 @@
         )
     for copy in small + [copy for pair in wide for copy in pair]:
         copy.start()
-    last_group = lax.axis_index("ctx") // 2 == groups - 1
     small[0].wait()
     length = decay_ref.shape[1]
     rows = dot_full(decay_ref[...], lower_ones(length, 1, 0))
     rows_ref[...] = rows
-    columns_ref[...] = rows.T
+    columns = rows.T
     into_end = jnp.exp(rows[:, length - 1 : length] - rows)
     from_start = jnp.exp(rows)
-    into_ref[...] = into_end.T
+    into_column = into_end.T
     from_column = from_start.T
-    from_ref[...] = from_column
     small[1].wait()
     small[2].wait()
     b_t = b_ref[...].astype(F32).T
@@ -138,22 +139,25 @@
         lanes = pl.ds(chunk * WIDE, WIDE)
         heads = slice(chunk * HEADS, (chunk + 1) * HEADS)
         pairs = range(chunk * HEADS // 2, (chunk + 1) * HEADS // 2)
+        columns_ref[chunk] = columns[:, heads]
+        into_ref[chunk] = into_column[:, heads]
+        from_ref[chunk] = from_column[:, heads]
         totals_ref[:, lanes] = over_lanes(from_column[length - 8 :, heads])[7:8, :]
         for place, (proj, factors, values_ref, rows_at) in enumerate(
-            ((b_t, into_end, x_ref, 0), (c_t, from_start, dy_ref, STATE))
+            ((b_t, into_end, x_ref, near_at), (c_t, from_start, dy_ref, far_at))
         ):
             wide[chunk][place].wait()
             for pair in pairs:
                 at = (pair - pairs[0]) * STATE
-                messages[chunk, rows_at : rows_at + STATE, at : at + STATE] = gathered(
+                messages[chunk, pl.ds(rows_at, STATE), at : at + STATE] = gathered(
                     proj, factors, values_ref, pair
                 )
-        leave(messages.at[chunk], outs[5 + chunk])
-        if chunk >= chunks - late:
-            sends[chunk - chunks + late] = jnp.where(
-                last_group, messages[chunk, STATE:, :], messages[chunk, :STATE, :]
-            )
-            leave(sends.at[chunk - chunks + late], outs[5 + late + chunk])
+        if chunk < chunks - late:
+            leave(messages.at[chunk], outs[5 + chunk])
+        else:
+            place = 5 + late + 2 * (chunk - late)
+            leave(messages.at[chunk, :STATE], outs[place])
+            leave(messages.at[chunk, STATE:], outs[place + 1])
     for source, target in zip(kept, outs[:5]):
         leave(source, target)
     for copy in pending:
@@ -161,7 +165,6 @@
 
 
 def intra_kernel(
-    chunk,
     rows_ref,
     columns_ref,
     into_ref,
@@ -170,6 +173,8 @@
     dy_ref,
     b_ref,
     c_ref,
+    gb_in_ref,
+    gc_in_ref,
     dx_ref,
     xs_ref,
     dys_ref,
@@ -178,11 +183,11 @@
     gc_ref,
     table_ref,
 ):
+    step = pl.program_id(0)
     rows = rows_ref[...]
-    heads = slice(chunk * HEADS, (chunk + 1) * HEADS)
-    columns = columns_ref[:, heads]
-    xs_ref[...] = (x_ref[...].astype(F32) * over_lanes(into_ref[:, heads])).astype(BF16)
-    dys_ref[...] = (dy_ref[...].astype(F32) * over_lanes(from_ref[:, heads])).astype(BF16)
+    columns = columns_ref[0]
+    xs_ref[...] = (x_ref[...].astype(F32) * over_lanes(into_ref[0])).astype(BF16)
+    dys_ref[...] = (dy_ref[...].astype(F32) * over_lanes(from_ref[0])).astype(BF16)
     length = rows.shape[1]
     b, c = b_ref[...], c_ref[...]
     scores = dot(b, c, NT)
@@ -191,7 +196,10 @@
     half = first_half(size)
     blocks = length // size
 
-    table_ref[...] = jnp.zeros_like(table_ref)
+    @pl.when(step == 0)
+    def _():
+        table_ref[...] = jnp.zeros_like(table_ref)
+
 
     for pair in range(HEADS // 2):
         lanes = slice(pair * 2 * HEAD_DIM, (pair + 1) * 2 * HEAD_DIM)
@@ -227,9 +235,12 @@
             change_ref[head : head + 1, :] = sums[side]
 
     change_ref[...] -= per_head(x_ref[...].astype(F32) * dx_ref[...])
-    table = table_ref[...]
-    gb_ref[...] = dot_halves(table, c)
-    gc_ref[...] = dot_halves(table, b, TN)
+
+    @pl.when(step == pl.num_programs(0) - 1)
+    def _():
+        table = table_ref[...]
+        gb_ref[...] = gb_in_ref[...] + dot_halves(table, c)
+        gc_ref[...] = gc_in_ref[...] + dot_halves(table, b, TN)
 
 
 def inter_kernel(
@@ -253,7 +264,6 @@
     gc_out_ref,
 ):
     lanes = slice(chunk * WIDE, (chunk + 1) * WIDE)
-    heads = slice(chunk * HEADS, (chunk + 1) * HEADS)
     state_in = state_in_ref[...]
     adjoint_in = adjoint_in_ref[...]
     state_low = state_in.astype(BF16)
@@ -263,7 +273,7 @@
     gb_out_ref[...] = gb_ref[...] + dot(xs, adjoint_low, NT)
     gc_out_ref[...] = gc_ref[...] + dot(dys, state_low, NT)
     outer = dot(b_ref[...], adjoint_low)
-    gx_ref[...] = (dx_ref[...] + over_lanes(into_ref[:, heads]) * outer).astype(BF16)
+    gx_ref[...] = (dx_ref[...] + over_lanes(into_ref[chunk]) * outer).astype(BF16)
     change_ref[...] = per_head(dys.astype(F32) * dot(c_ref[...], state_low))
     earlier_ref[...] = per_head(xs.astype(F32) * outer)
     later_ref[...] = per_head(total_ref[:, lanes] * state_in * adjoint_in)
@@ -301,9 +311,9 @@
     tokens, width = x.shape
     heads = log_decay.shape[0]
     chunks = width // WIDE
-    kept = [(heads, tokens)] + [(tokens, heads)] * 3 + [(1, width)]
+    kept = [(heads, tokens)] + [(chunks, tokens, HEADS)] * 3 + [(1, width)]
     late = chunks // 2
-    outs = kept + [(2 * STATE, WIDE)] * chunks + [(STATE, WIDE)] * late
+    outs = kept + [(2 * STATE, WIDE)] * (chunks - late) + [(STATE, WIDE)] * (2 * late)
     hbm = pl.BlockSpec(memory_space=pltpu.HBM)
     outs = pl.pallas_call(
         functools.partial(local_kernel, groups),
@@ -318,7 +328,6 @@
             pltpu.VMEM(b.shape, BF16),
             *[pltpu.VMEM(dims, F32) for dims in kept],
             pltpu.VMEM((chunks, 2 * STATE, WIDE), F32),
-            pltpu.VMEM((late, STATE, WIDE), F32),
             pltpu.SemaphoreType.DMA((3,)),
             pltpu.SemaphoreType.DMA((2, chunks)),
             pltpu.SemaphoreType.DMA((len(outs),)),
@@ -327,30 +336,26 @@
         cost_estimate=cost(4 * tokens * STATE * width, 12 * tokens * width),
         name="local_states",
     )(log_decay, x, dy, b, c)
-    return outs[:5], outs[5 : 5 + chunks], [None] * (chunks - late) + list(outs[5 + chunks :])
-
-
-def intra(chunk, rows, columns, into, start, x, dy, b, c):
+    pairs, sides = outs[5 : 5 + chunks - late], outs[5 + chunks - late :]
+    return outs[:5], pairs, [sides[i : i + 2] for i in range(0, 2 * late, 2)]
+
+
+def intra(chunk, rows, columns, into, start, x, dy, b, c, gb, gc):
     tokens = x.shape[0]
     wide = pl.BlockSpec((tokens, WIDE), lambda k: (0, chunk))
+    own = pl.BlockSpec((tokens, WIDE), lambda k: (0, 0))
     proj = pl.BlockSpec((tokens, STATE), lambda k: (0, 0))
     return pl.pallas_call(
-        functools.partial(intra_kernel, chunk),
+        intra_kernel,
         grid=(1,),
         in_specs=[
             pl.BlockSpec((HEADS, tokens), lambda k: (chunk, 0)),
-            *[pl.BlockSpec(columns.shape, lambda k: (0, 0))] * 3,
+            *[pl.BlockSpec((1, tokens, HEADS), lambda k: (chunk, 0, 0))] * 3,
             wide,
             wide,
-            proj,
-            proj,
+            *[proj] * 4,
         ],
-        out_specs=[
-            *[pl.BlockSpec((tokens, WIDE), lambda k: (0, 0))] * 3,
-            pl.BlockSpec((HEADS, tokens), lambda k: (0, 0)),
-            proj,
-            proj,
-        ],
+        out_specs=[own, own, own, pl.BlockSpec((HEADS, tokens), lambda k: (0, 0)), proj, proj],
         out_shape=[
             shape((tokens, WIDE)),
             shape((tokens, WIDE), BF16),
@@ -363,7 +368,7 @@
         compiler_params=params(),
         cost_estimate=cost(4 * tokens * tokens * WIDE, 8 * tokens * WIDE),
         name="intra",
-    )(rows, columns, into, start, x, dy, b, c)
+    )(rows, columns, into, start, x, dy, b, c, gb, gc)
 
 
 def inter(chunk, into, state_in, adjoint_in, totals, xs, dys, b, c, dx, gb, gc):
@@ -465,31 +470,6 @@
     chunk.in_f, chunk.in_b = carried_f, carried_b
 
 
-class Four:
-    def __init__(self, group):
-        self.lower = group < 2
-        self.inner = (group == 1) | (group == 2)
-
-    def first(self, chunk):
-        return jnp.where(self.lower, chunk.forward, chunk.backward)
-
-    def second(self, chunk, got):
-        chunk.hop1 = got
-        scale = jnp.where(self.lower, chunk.step_f * chunk.seen_f, chunk.step_b * chunk.seen_b)
-        return scale * got + jnp.where(self.lower, chunk.forward, chunk.backward)
-
-    def third(self, chunk, got):
-        chunk.hop2 = got
-        scale = jnp.where(self.lower, chunk.step_b * chunk.seen_b, chunk.step_f * chunk.seen_f)
-        return scale * got + jnp.where(self.lower, chunk.backward, chunk.forward)
-
-    def done(self, chunk, got):
-        near = jnp.where(self.inner, chunk.hop1, 0.0)
-        far = jnp.where(self.inner, chunk.hop2, got)
-        chunk.in_f = chunk.seen_f * jnp.where(self.lower, near, far)
-        chunk.in_b = chunk.seen_b * jnp.where(self.lower, far, near)
-
-
 def fence(*items):
     return lax.optimization_barrier(items)
 
@@ -506,98 +486,135 @@
     swap = [(i, i ^ 1) for i in range(count)]
     diagonals = [(2 * g + 1, 2 * g + 2) for g in range(groups - 1)]
     diagonals += [(t, s) for s, t in diagonals]
-
-    (rows, columns, into, start, totals), messages, sends = local_states(
+    lower = group < groups // 2
+    inner = (group > 0) & (group < groups - 1)
+
+    (rows, columns, into, start, totals), pairs, sides = local_states(
         groups, log_decay, inputs, grad_out, b_proj, c_proj
     )
-    chunks = len(messages)
-    other = permute(totals, swap)
-    diagonal = permute(totals, diagonals)
-
-    def chunk_of(k, first, message, other, diagonal):
-        lanes = slice(k * WIDE, (k + 1) * WIDE)
-        return Chunk(
-            first, message, totals[:, lanes], other[:, lanes], diagonal[:, lanes], second
-        )
-
-    def local(k, rows, columns):
-        return intra(k, rows, columns, into, start, inputs, grad_out, b_proj, c_proj)
-
-    def carried(k, entering, near, gb, gc):
-        dx, xs, dys = near[:3]
+    late = len(pairs)
+    chunks = late + len(sides)
+    own = totals
+    other = permute(own, swap)
+    diagonal = permute(own, diagonals)
+    none = jnp.zeros((inputs.shape[0], STATE), F32)
+    near = [None] * chunks
+
+    def local(k, rows, gb, gc):
+        *near[k], gb, gc = intra(
+            k, rows, columns, into, start, inputs, grad_out, b_proj, c_proj, gb, gc
+        )
+        return gb, gc
+
+    def carried(k, entering, gb, gc):
+        dx, xs, dys, _ = near[k]
         return inter(k, into, *entering, totals, xs, dys, b_proj, c_proj, dx, gb, gc)
 
-    near, far = [None] * chunks, [None] * chunks
+    def ways(forward, backward):
+        return jnp.where(lower, forward, backward), jnp.where(lower, backward, forward)
+
+    far = [None] * chunks
     if groups == 4 and chunks == 4:
-        four = Four(group)
         middle = between([(1, 2), (2, 1)])
-        sides = between([(0, 1), (1, 0), (2, 3), (3, 2)])
-
-        pair0 = permute(messages[0], swap)
-        hop = permute(sends[2], sides)
-        other, diagonal, hop, message1, send3, rows, columns = fence(
-            other, diagonal, hop, messages[1], sends[3], rows, columns
-        )
-        c0 = chunk_of(0, True, messages[0], other, diagonal)
-        c1 = chunk_of(1, True, message1, other, diagonal)
-        c2 = chunk_of(2, False, messages[2], other, diagonal)
-        c3 = chunk_of(3, False, messages[3], other, diagonal)
-
-        mid = permute(four.second(c2, hop), middle)
-        hop = permute(send3, sides)
-        pair1 = permute(message1, swap)
-        mid, hop, pair0, rows, columns = fence(mid, hop, pair0, rows, columns)
-        c0.joined(pair0)
-
-        side = permute(jnp.where(four.inner, four.third(c2, mid), four.first(c0)), sides)
-        mid = permute(four.second(c3, hop), middle)
-        near[0], near[1] = local(0, rows, columns), local(1, rows, columns)
-        side, mid, pair1, near[0], near[1], rows = fence(side, mid, pair1, near[0], near[1], rows)
-        four.done(c2, side)
-        c1.joined(pair1)
-
-        pair2 = permute(c2.message(), swap)
-        hop = side
-        side = permute(jnp.where(four.inner, four.third(c3, mid), four.first(c1)), sides)
-        mid = permute(four.second(c0, hop), middle)
-        near[2] = local(2, rows, columns)
-        side, mid, near[2], rows = fence(side, mid, near[2], rows)
-        four.done(c3, side)
-
-        pair3 = permute(c3.message(), swap)
-        hop = side
-        side = permute(four.third(c0, mid), sides)
-        mid = permute(four.second(c1, hop), middle)
-        near[3] = local(3, rows, columns)
-        gb = sum(item[4] for item in near)
-        gc = sum(item[5] for item in near)
-        side, mid, pair2, gb, gc = fence(side, mid, pair2, gb, gc)
-        four.done(c0, side)
-
-        side = permute(four.third(c1, mid), sides)
-        *far[0], gb, gc = carried(0, c0.entering(), near[0], gb, gc)
-        *far[2], gb, gc = carried(2, c2.entering(pair2), near[2], gb, gc)
-        side, pair3, far[0], far[2], gb, gc = fence(side, pair3, far[0], far[2], gb, gc)
-        four.done(c1, side)
-
-        *far[1], gb, gc = carried(1, c1.entering(), near[1], gb, gc)
-        *far[3], gb, gc = carried(3, c3.entering(pair3), near[3], gb, gc)
+        steps = between([(0, 1), (1, 0), (2, 3), (3, 2)])
+        (near2, far2), (near3, far3) = sides
+
+        pair0 = permute(pairs[0], swap)
+        hop2 = permute(near2, steps)
+        message1 = pairs[1]
+        pair1 = permute(fence(message1, other)[0], swap)
+
+        def after(value, *events):
+            return fence(value, *events)[0]
+
+
+        one, zero = jnp.ones_like(own), jnp.zeros_like(own)
+        both = own * other
+        mine_n, mine_f = ways(jnp.where(second, one, other), jnp.where(second, other, one))
+        theirs_n, theirs_f = ways(jnp.where(second, own, one), jnp.where(second, one, own))
+        seen_n, seen_f = ways(
+            jnp.where(second, one, diagonal), jnp.where(second, diagonal, one)
+        )
+        step_n, step_f = ways(jnp.where(second, both, own), jnp.where(second, own, both))
+        pass_n, pass_f = step_n * seen_n, step_f * seen_f
+        cross_n, cross_f = ways(jnp.where(second, one, own), jnp.where(second, own, one))
+        cross_n = jnp.where(inner, cross_n * seen_n, zero)
+        cross_f = cross_f * seen_f
+        with_n, with_f = ways(jnp.where(second, zero, one), jnp.where(second, one, zero))
+        last_n, last_f = ways(jnp.where(second, other, one), jnp.where(second, one, other))
+        mate_n, mate_f = ways(jnp.where(second, one, zero), jnp.where(second, zero, one))
+        reach_n = jnp.where(inner, last_n, zero)
+
+        def at(row, k):
+            return row[:, k * WIDE : (k + 1) * WIDE]
+
+        mid2 = permute(at(pass_n, 2) * hop2 + near2, middle)
+        hop3 = permute(after(near3, hop2), steps)
+        gb, gc = local(0, after(rows, hop2), none, none)
+
+        sum0 = at(mine_n, 0) * pairs[0][:STATE] + at(theirs_n, 0) * pair0[:STATE]
+        side2 = permute(jnp.where(inner, at(pass_f, 2) * mid2 + far2, sum0), steps)
+        mid3 = permute(at(pass_n, 3) * hop3 + near3, middle)
+        cross2 = permute(at(cross_n, 2) * hop2 + at(with_n, 2) * near2, swap)
+        gb, gc = local(1, after(rows, mid2), gb, gc)
+
+        sum1 = at(mine_n, 1) * message1[:STATE] + at(theirs_n, 1) * pair1[:STATE]
+        side3 = permute(jnp.where(inner, at(pass_f, 3) * mid3 + far3, sum1), steps)
+        mid0 = permute(at(both, 0) * side2 + sum0, middle)
+        end2 = at(cross_f, 2) * jnp.where(inner, mid2, side2) + at(with_f, 2) * far2
+        cross2f = permute(end2, swap)
+        cross3 = permute(at(cross_n, 3) * hop3 + at(with_n, 3) * near3, swap)
+        gb, gc = local(2, after(rows, side2), gb, gc)
+
+        rest0 = at(mine_f, 0) * pairs[0][STATE:] + at(theirs_f, 0) * pair0[STATE:]
+        last0 = permute(at(both, 0) * mid0 + rest0, steps)
+        mid1 = permute(at(both, 1) * side3 + sum1, middle)
+        end3 = at(cross_f, 3) * jnp.where(inner, mid3, side3) + at(with_f, 3) * far3
+        cross3f = permute(end3, swap)
+        gb, gc = local(3, after(rows, side3), gb, gc)
+
+        rest1 = at(mine_f, 1) * message1[STATE:] + at(theirs_f, 1) * pair1[STATE:]
+        last1 = permute(at(both, 1) * mid1 + rest1, steps)
+
+        def entering(k, first, near, middle, far, got_near, got_far):
+            far = jnp.where(inner, middle, far)
+            if first:
+                near = at(reach_n, k) * near + at(mate_n, k) * got_near
+                far = at(last_f, k) * far + at(mate_f, k) * got_far
+            else:
+                near = at(reach_n * seen_n, k) * near + got_near
+                far = at(last_f * seen_f, k) * far + got_far
+            return ways(near, far)
+
+        enter0 = entering(0, True, side2, mid0, last0, pair0[:STATE], pair0[STATE:])
+        *far[0], gb, gc = carried(0, enter0, gb, gc)
+        enter2 = entering(2, False, hop2, mid2, side2, cross2, cross2f)
+        *far[2], gb, gc = carried(2, enter2, gb, gc)
+        cross3f, gb, gc = fence(cross3f, gb, gc)
+        enter3 = entering(3, False, hop3, mid3, side3, cross3, cross3f)
+        *far[3], gb, gc = carried(3, enter3, gb, gc)
+        last1, gb, gc = fence(last1, gb, gc)
+        enter1 = entering(1, True, side3, mid1, last1, pair1[:STATE], pair1[STATE:])
+        *far[1], gb, gc = carried(1, enter1, gb, gc)
     else:
-        near = [local(k, rows, columns) for k in range(chunks)]
-        gb = sum(item[4] for item in near)
-        gc = sum(item[5] for item in near)
+        gb = gc = none
         for k in range(chunks):
-            first = k < chunks // 2
-            chunk = chunk_of(k, first, messages[k], other, diagonal)
+            gb, gc = local(k, rows, gb, gc)
+            first = k < late
+            lanes = slice(k * WIDE, (k + 1) * WIDE)
+            message = pairs[k] if first else jnp.concatenate(sides[k - late], axis=0)
+            flipped = jnp.concatenate([message[STATE:], message[:STATE]], axis=0)
+            message = jnp.where(lower, message, flipped)
+            chunk = Chunk(
+                first, message, own[:, lanes], other[:, lanes], diagonal[:, lanes], second
+            )
             if first:
-                chunk.joined(permute(messages[k], swap))
+                chunk.joined(permute(message, swap))
             group_scan(chunk, group, groups)
             got = None if first else permute(chunk.message(), swap)
-            *far[k], gb, gc = carried(k, chunk.entering(got), near[k], gb, gc)
+            *far[k], gb, gc = carried(k, chunk.entering(got), gb, gc)
     grad_x = jnp.concatenate([item[0] for item in far], axis=1)
-    grad_decay = suffix_sums(
-        [item[3] for item in near], *([item[i] for item in far] for i in (1, 2, 3))
-    )
+    grad_decay = suffix_sums([item[3] for item in near], *([item[i] for item in far] for i in (1, 2, 3)))
 
     ranks = lax.axis_size("head")
     rank = lax.axis_index("head")

time: 80.2 us -> 75.1 us (0.936)
  waiting for transfers between devices: 8.47 us -> 16.9 us
  other arithmetic: 11.8 us -> 5.95 us
  local copies, waits for them, and re-layouts: 5.35 us -> 0.1 us
  starting transfers between devices: 36 us -> 32.9 us
    ppermute x16 -> x18, waiting for transfers between devices: 6.62 us -> 15.2 us  [permute(): return lax.ppermute(value, 'ctx', links)]
    select_n x8 -> x10, other arithmetic: 6 us -> 1.16 us  [the longest x4 0.6 us: ways(): jnp.where(lower, backward, forward)]
    unnamed x100 -> x28, local copies, waits for them, and re-layouts: 4.67 us -> 0.07 us
    ppermute x16 -> x18, starting transfers between devices: 34.1 us -> 30.9 us  [permute(): return lax.ppermute(value, 'ctx', links)]
    mul x0 -> x2, other arithmetic: none -> 1.47 us  [the longest x1 0.76 us: entering(): far = at(last_f * seen_f, k) * far + got_far]
    add x9 -> x6, other arithmetic: 2.92 us -> 1.53 us  [the longest x1 1.09 us: shards(): mid2 = permute(at(pass_n, 2) * hop2 + near2, middle)]
    concatenate x2 -> x0, other arithmetic: 1.1 us -> none  [message(): return jnp.concatenate([send_f, send_b], axis=0)]
  transfers between devices with their start and end apart: 19 -> 21, of which waited for: 6 -> 8; matrix products, arithmetic and copies ran while one was open for 11% -> 7% of each run, Pallas kernels for 11% -> 14%
where the time goes in v3:
time: 75.1 us; the launch traced here: 73.9 us
  starting transfers between devices  32.9 us (44%)
  Pallas kernels  17 us (23%)
  waiting for transfers between devices  16.9 us (23%)
  other arithmetic  5.95 us (8%)
  between operations  1.04 us (1%)
    ppermute x18, starting transfers between devices, permute(): return lax.ppermute(value, 'ctx', links)  30.9 us
    ppermute x18, waiting for transfers between devices, permute(): return lax.ppermute(value, 'ctx', links)  15.2 us
    pallas_call x4, Pallas kernels, intra(): pl.pallas_call(intra_kernel, grid=(1,), in_specs=[pl.BlockSpec((HEADS, to...  6.39 us
    pallas_call x1, Pallas kernels, local_states(): pl.pallas_call(functools.partial(local_kernel, groups), in_specs=[hbm] *...  5.85 us
    pallas_call x4, Pallas kernels, inter(): pl.pallas_call(functools.partial(inter_kernel, chunk), in_specs=vmem(len(...  3.77 us
    ppermute x3, starting transfers between devices, shards(): parts.append(lax.ppermute(piece(rank ^ step), 'head', links))  1.93 us
    ppermute x3, waiting for transfers between devices, shards(): parts.append(lax.ppermute(piece(rank ^ step), 'head', links))  1.68 us
  transfers between devices with their start and end apart: 21, of which 8 were waited for; matrix products, arithmetic and copies ran while one was open for 7% of the time, Pallas kernels for 14%

profile of v3, /device:TPU:0, one launch (start us, length us, event | category | flops | bytes accessed | tf_op | source)
XLA Modules:
  0.0 73.9 jit_solution(13051257528354634589)
XLA Ops:
  0.6 5.9 %local_states.1 = (f32[32,256]{1,0:T(8,128)}, f32[4,256,8]{2,1,0:T(8,128)}, f32[4,256,8]{2,1,0:T(8,128)}, f32[4,256,8]{2,1,0:T(8,128)}, f32[1,2048]{1,0:T(1,128)...) custom-call(f32[32,256]{1,0:T(8,128)} %decay_in.1, ...), custom_call_target="tpu_custom_call" | custom-call | flops 268435456 | bytes 6291456 | tf_op jit(solution)/shard_map/local_states/pallas_call | solution.py:318
  7.3 5.8 %collective-permute-start = (f32[1,2048]{1,0:T(1,128)}, f32[1,2048]{1,0:T(1,128)S(1)}, u32[]{:S(2)}, u32[]{:S(2)}) collective-permute-start(f32[1,2048]{1,0:T(1,128)} %get-tuple-element.76.total_ref), channel_id=1, source_target_pairs={{0,4},{4,0},{8,12},{12,8},{16,20},{20,16},{24,28},{28,24},{1,5},{5... | collective-permute-start | bytes 24584 | tf_op jit(solution)/shard_map/ppermute | solution.py:484
  13.1 1.6 %collective-permute-start.2 = (f32[128,512]{1,0:T(8,128)}, f32[128,512]{1,0:T(8,128)S(1)}, u32[]{:S(2)}, u32[]{:S(2)}) collective-permute-start(f32[128,512]{1,0:T(8,128)} %get-tuple-element.77), channel_id=1, source_target_pairs={{0,8},{4,12},{8,0},{12,4},{16,24},{20,28},{24,16},{28,20},{1,9},{5... | collective-permute-start | bytes 786440 | tf_op jit(solution)/shard_map/ppermute | solution.py:484
  16.6 2.1 %collective-permute-start.10 = (f32[256,512]{1,0:T(8,128)}, f32[256,512]{1,0:T(8,128)S(1)}, u32[]{:S(2)}, u32[]{:S(2)}) collective-permute-start(f32[256,512]{1,0:T(8,128)} %get-tuple-element.91), channel_id=1, source_target_pairs={{0,4},{4,0},{8,12},{12,8},{16,20},{20,16},{24,28},{28,24},{1,5},{5... | collective-permute-start | bytes 1572872 | tf_op jit(solution)/shard_map/ppermute | solution.py:484
  18.6 2.2 %collective-permute-done.2 = f32[128,512]{1,0:T(8,128)S(1)} collective-permute-done((f32[128,512]{1,0:T(8,128)}, f32[128,512]{1,0:T(8,128)S(1)}, u32[]{:S(2)}, u32[]{:S(2)}) %collective-permute-start.2) | collective-permute-done | bytes 262176 | tf_op jit(solution)/shard_map/ppermute | solution.py:484
  20.8 1.6 %collective-permute-start.8 = (f32[128,512]{1,0:T(8,128)}, f32[128,512]{1,0:T(8,128)S(1)}, u32[]{:S(2)}, u32[]{:S(2)}) collective-permute-start(f32[128,512]{1,0:T(8,128)} %get-tuple-element.88), channel_id=1, source_target_pairs={{0,8},{4,12},{8,0},{12,4},{16,24},{20,28},{24,16},{28,20},{1,9},{5... | collective-permute-start | bytes 786440 | tf_op jit(solution)/shard_map/ppermute | solution.py:484
  22.4 1.1 %multiply_add_fusion.17 = (f32[128,512]{1,0:T(8,128)S(1)}, f32[128,512]{1,0:T(8,128)S(1)}) fusion(f32[128,512]{1,0:T(8,128)} %get-tuple-element.77, f32[128,512]{1,0:T(8,128)S(1)} %collective-permute-done.2, f32[512]{0:T(512)S(1)} %bitcast.56, f32[]{:T(128)S(6)} %select_n.242, f32[512]{0:T(512)S(1)} %bitcast.57), kind=kLoop, calls=%fused_computation.30 | loop fusion | flops 327680 | bytes 1052676 | tf_op jit(solution)/shard_map/add | solution.py:551
  24.2 3.4 %collective-permute-done.8 = f32[128,512]{1,0:T(8,128)S(1)} collective-permute-done((f32[128,512]{1,0:T(8,128)}, f32[128,512]{1,0:T(8,128)S(1)}, u32[]{:S(2)}, u32[]{:S(2)}) %collective-permute-start.8) | collective-permute-done | bytes 262176 | tf_op jit(solution)/shard_map/ppermute | solution.py:484
  28.5 1.3 %collective-permute-done.4 = f32[256,512]{1,0:T(8,128)S(1)} collective-permute-done((f32[256,512]{1,0:T(8,128)}, f32[256,512]{1,0:T(8,128)S(1)}, u32[]{:S(2)}, u32[]{:S(2)}) %collective-permute-start.4) | collective-permute-done | bytes 524320 | tf_op jit(solution)/shard_map/ppermute | solution.py:484
  29.9 3.4 %collective-permute-start.5 = (f32[128,512]{1,0:T(8,128)S(1)}, f32[128,512]{1,0:T(8,128)S(1)}, u32[]{:S(2)}, u32[]{:S(2)}) collective-permute-start(f32[128,512]{1,0:T(8,128)S(1)} %add_select_fusion.1), channel_id=1, source_target_pairs={{0,8},{4,12},{8,0},{12,4},{16,24},{20,28},{24,16},{28,20},{1,9},{5... | collective-permute-start | bytes 786440 | tf_op jit(solution)/shard_map/ppermute | solution.py:484
  33.2 5.7 %collective-permute-done.10 = f32[256,512]{1,0:T(8,128)S(1)} collective-permute-done((f32[256,512]{1,0:T(8,128)}, f32[256,512]{1,0:T(8,128)S(1)}, u32[]{:S(2)}, u32[]{:S(2)}) %collective-permute-start.10) | collective-permute-done | bytes 524320 | tf_op jit(solution)/shard_map/ppermute | solution.py:484
  41.1 1.6 %intra.4 = (f32[256,512]{1,0:T(8,128)S(1)}, bf16[256,512]{1,0:T(8,128)(2,1)S(1)}, bf16[256,512]{1,0:T(8,128)(2,1)S(1)}, f32[8,256]{1,0:T(8,128)S(1)}, f32[256,128]{1,0:T(8,128)S(1)}, /*index=5*/f32[256,128]{1,0:T(8,128)S(1)}) custom-call(f32[32,256]{1,0:T(8,128)S(1)} %copy-done.7, f32[4,256,8]{2,1,0:T(8,128)S(1)} %copy-done.3, f32[4,256,8]{2,1,0:T(8,128)S(1)} %copy-done, ...), custom_call_target="tpu_custom_call" | custom-call | flops 134217728 | bytes 1048576 | tf_op jit(solution)/shard_map/intra/pallas_call | solution.py:348
  42.7 1.6 %collective-permute-start.14 = (f32[128,512]{1,0:T(8,128)S(1)}, f32[128,512]{1,0:T(8,128)S(1)}, u32[]{:S(2)}, u32[]{:S(2)}) collective-permute-start(f32[128,512]{1,0:T(8,128)S(1)} %get-tuple-element.168), channel_id=1, source_target_pairs={{0,4},{4,0},{8,12},{12,8},{16,20},{20,16},{24,28},{28,24},{1,5},{5... | collective-permute-start | bytes 786440 | tf_op jit(solution)/shard_map/ppermute | solution.py:484
  44.3 1.6 %intra.5 = (f32[256,512]{1,0:T(8,128)S(1)}, bf16[256,512]{1,0:T(8,128)(2,1)S(1)}, bf16[256,512]{1,0:T(8,128)(2,1)S(1)}, f32[8,256]{1,0:T(8,128)S(1)}, f32[256,128]{1,0:T(8,128)S(1)}, /*index=5*/f32[256,128]{1,0:T(8,128)S(1)}) custom-call(f32[32,256]{1,0:T(8,128)S(1)} %copy-done.7, f32[4,256,8]{2,1,0:T(8,128)S(1)} %copy-done.3, f32[4,256,8]{2,1,0:T(8,128)S(1)} %copy-done, ...), custom_call_target="tpu_custom_call" | custom-call | flops 134217728 | bytes 1048576 | tf_op jit(solution)/shard_map/intra/pallas_call | solution.py:348
  45.9 1.6 %intra.6 = (f32[256,512]{1,0:T(8,128)S(1)}, bf16[256,512]{1,0:T(8,128)(2,1)S(1)}, bf16[256,512]{1,0:T(8,128)(2,1)S(1)}, f32[8,256]{1,0:T(8,128)S(1)}, f32[256,128]{1,0:T(8,128)S(1)}, /*index=5*/f32[256,128]{1,0:T(8,128)S(1)}) custom-call(f32[32,256]{1,0:T(8,128)S(1)} %copy-done.7, f32[4,256,8]{2,1,0:T(8,128)S(1)} %copy-done.3, f32[4,256,8]{2,1,0:T(8,128)S(1)} %copy-done, ...), custom_call_target="tpu_custom_call" | custom-call | flops 134217728 | bytes 1048576 | tf_op jit(solution)/shard_map/intra/pallas_call | solution.py:348
  47.6 4.4 %collective-permute-start.7 = (f32[128,512]{1,0:T(8,128)S(1)}, f32[128,512]{1,0:T(8,128)S(1)}, u32[]{:S(2)}, u32[]{:S(2)}) collective-permute-start(f32[128,512]{1,0:T(8,128)S(1)} %add_add_fusion.1), channel_id=1, source_target_pairs={{0,8},{4,12},{8,0},{12,4},{16,24},{20,28},{24,16},{28,20},{1,9},{5... | collective-permute-start | bytes 786440 | tf_op jit(solution)/shard_map/ppermute | solution.py:484
  53.1 1.4 %collective-permute-start.15 = (f32[128,512]{1,0:T(8,128)S(1)}, f32[128,512]{1,0:T(8,128)S(1)}, u32[]{:S(2)}, u32[]{:S(2)}) collective-permute-start(f32[128,512]{1,0:T(8,128)S(1)} %get-tuple-element.176), channel_id=1, source_target_pairs={{0,4},{4,0},{8,12},{12,8},{16,20},{20,16},{24,28},{28,24},{1,5},{5... | collective-permute-start | bytes 786440 | tf_op jit(solution)/shard_map/ppermute | solution.py:484
  54.5 1.6 %intra.7 = (f32[256,512]{1,0:T(8,128)S(1)}, bf16[256,512]{1,0:T(8,128)(2,1)S(1)}, bf16[256,512]{1,0:T(8,128)(2,1)S(1)}, f32[8,256]{1,0:T(8,128)S(1)}, f32[256,128]{1,0:T(8,128)S(1)}, /*index=5*/f32[256,128]{1,0:T(8,128)S(1)}) custom-call(f32[32,256]{1,0:T(8,128)S(1)} %copy-done.7, f32[4,256,8]{2,1,0:T(8,128)S(1)} %copy-done.3, f32[4,256,8]{2,1,0:T(8,128)S(1)} %copy-done, ...), custom_call_target="tpu_custom_call" | custom-call | flops 134217728 | bytes 1048576 | tf_op jit(solution)/shard_map/intra/pallas_call | solution.py:348
  56.7 1.4 %collective-permute-start.17 = (f32[128,512]{1,0:T(8,128)S(1)}, f32[128,512]{1,0:T(8,128)S(1)}, u32[]{:S(2)}, u32[]{:S(2)}) collective-permute-start(f32[128,512]{1,0:T(8,128)S(1)} %get-tuple-element.178), channel_id=1, source_target_pairs={{0,4},{4,0},{8,12},{12,8},{16,20},{20,16},{24,28},{28,24},{1,5},{5... | collective-permute-start | bytes 786440 | tf_op jit(solution)/shard_map/ppermute | solution.py:484
  58.2 2.4 %collective-permute-start.13 = (f32[128,512]{1,0:T(8,128)S(1)}, f32[128,512]{1,0:T(8,128)S(1)}, u32[]{:S(2)}, u32[]{:S(2)}) collective-permute-start(f32[128,512]{1,0:T(8,128)S(1)} %add_add_fusion), channel_id=1, source_target_pairs={{0,8},{4,12},{8,0},{12,4},{16,24},{20,28},{24,16},{28,20},{1,9},{5... | collective-permute-start | bytes 786440 | tf_op jit(solution)/shard_map/ppermute | solution.py:484
  61.6 2.3 %collective-permute-done.17 = f32[128,512]{1,0:T(8,128)S(1)} collective-permute-done((f32[128,512]{1,0:T(8,128)S(1)}, f32[128,512]{1,0:T(8,128)S(1)}, u32[]{:S(2)}, u32[]{:S(2)}) %collective-permute-start.17) | collective-permute-done | bytes 262176 | tf_op jit(solution)/shard_map/ppermute | solution.py:484
  67.6 1.6 %collective-permute-start.19 = (f32[2,64,128]{2,1,0:T(8,128)S(1)}, f32[2,64,128]{2,1,0:T(8,128)S(1)}, u32[]{:S(2)}, u32[]{:S(2)}) collective-permute-start(f32[2,64,128]{2,1,0:T(8,128)S(1)} %get-tuple-element.173), channel_id=1, source_target_pairs={{0,2},{1,3},{2,0},{3,1},{4,6},{5,7},{6,4},{7,5},{8,10},{9,11},{10,... | collective-permute-start | bytes 196616 | tf_op jit(solution)/shard_map/ppermute | solution.py:630
  69.4 1.1 %pad_maximum_fusion = bf16[256,2048]{1,0:T(8,128)(2,1)} fusion(bf16[256,512]{1,0:T(8,128)(2,1)S(1)} %get-tuple-element.127, bf16[256,512]{1,0:T(8,128)(2,1)S(1)} %get-tuple-element.126, bf16[256,512]{1,0:T(8,128)(2,1)S(1)} %get-tuple-element.125, bf16[256,512]{1,0:T(8,128)(2,1)S(1)} %get-tuple-element.103), kind=kLoop, calls=%fused_computation | loop fusion | flops 4194304 | bytes 2097152 | tf_op jit(solution)/shard_map/concatenate | solution.py:616
  72.1 1.1 %collective-permute-done.20 = f32[2,64,128]{2,1,0:T(8,128)S(1)} collective-permute-done((f32[2,64,128]{2,1,0:T(8,128)S(1)}, f32[2,64,128]{2,1,0:T(8,128)S(1)}, u32[]{:S(2)}, u32[]{:S(2)}) %collective-permute-start.20) | collective-permute-done | bytes 65568 | tf_op jit(solution)/shard_map/ppermute | solution.py:630
  (85 shorter events, 15.2 us)
Async XLA Ops:
  6.5 21.1 %copy-start.13 = (f32[128,512]{1,0:T(8,128)S(1)}, f32[128,512]{1,0:T(8,128)}, u32[]{:S(2)}) copy-start(f32[128,512]{1,0:T(8,128)} %get-tuple-element.88) | copy-start | bytes 786436
  6.5 8.5 %collective-permute-start.1 = (f32[1,2048]{1,0:T(1,128)}, f32[1,2048]{1,0:T(1,128)S(1)}, u32[]{:S(2)}, u32[]{:S(2)}) collective-permute-start(f32[1,2048]{1,0:T(1,128)} %get-tuple-element.76.total_ref), channel_id=1, source_target_pairs={{4,8},{12,16},{20,24},{8,4},{16,12},{24,20},{5,9},{13,17},{21,25},... | collective-permute-start | bytes 24584 | tf_op jit(solution)/shard_map/ppermute | solution.py:484
  7.3 7.7 %collective-permute-start = (f32[1,2048]{1,0:T(1,128)}, f32[1,2048]{1,0:T(1,128)S(1)}, u32[]{:S(2)}, u32[]{:S(2)}) collective-permute-start(f32[1,2048]{1,0:T(1,128)} %get-tuple-element.76.total_ref), channel_id=1, source_target_pairs={{0,4},{4,0},{8,12},{12,8},{16,20},{20,16},{24,28},{28,24},{1,5},{5... | collective-permute-start | bytes 24584 | tf_op jit(solution)/shard_map/ppermute | solution.py:484
  13.1 7.7 %collective-permute-start.2 = (f32[128,512]{1,0:T(8,128)}, f32[128,512]{1,0:T(8,128)S(1)}, u32[]{:S(2)}, u32[]{:S(2)}) collective-permute-start(f32[128,512]{1,0:T(8,128)} %get-tuple-element.77), channel_id=1, source_target_pairs={{0,8},{4,12},{8,0},{12,4},{16,24},{20,28},{24,16},{28,20},{1,9},{5... | collective-permute-start | bytes 786440 | tf_op jit(solution)/shard_map/ppermute | solution.py:484
  14.7 15.1 %collective-permute-start.4 = (f32[256,512]{1,0:T(8,128)}, f32[256,512]{1,0:T(8,128)S(1)}, u32[]{:S(2)}, u32[]{:S(2)}) collective-permute-start(f32[256,512]{1,0:T(8,128)} %get-tuple-element.79), channel_id=1, source_target_pairs={{0,4},{4,0},{8,12},{12,8},{16,20},{20,16},{24,28},{28,24},{1,5},{5... | collective-permute-start | bytes 1572872 | tf_op jit(solution)/shard_map/ppermute | solution.py:484
  16.6 22.4 %collective-permute-start.10 = (f32[256,512]{1,0:T(8,128)}, f32[256,512]{1,0:T(8,128)S(1)}, u32[]{:S(2)}, u32[]{:S(2)}) collective-permute-start(f32[256,512]{1,0:T(8,128)} %get-tuple-element.91), channel_id=1, source_target_pairs={{0,4},{4,0},{8,12},{12,8},{16,20},{20,16},{24,28},{28,24},{1,5},{5... | collective-permute-start | bytes 1572872 | tf_op jit(solution)/shard_map/ppermute | solution.py:484
  20.8 6.8 %collective-permute-start.8 = (f32[128,512]{1,0:T(8,128)}, f32[128,512]{1,0:T(8,128)S(1)}, u32[]{:S(2)}, u32[]{:S(2)}) collective-permute-start(f32[128,512]{1,0:T(8,128)} %get-tuple-element.88), channel_id=1, source_target_pairs={{0,8},{4,12},{8,0},{12,4},{16,24},{20,28},{24,16},{28,20},{1,9},{5... | collective-permute-start | bytes 786440 | tf_op jit(solution)/shard_map/ppermute | solution.py:484
  23.5 5.0 %collective-permute-start.3 = (f32[128,512]{1,0:T(8,128)S(1)}, f32[128,512]{1,0:T(8,128)S(1)}, u32[]{:S(2)}, u32[]{:S(2)}) collective-permute-start(f32[128,512]{1,0:T(8,128)S(1)} %get-tuple-element.165), channel_id=1, source_target_pairs={{8,16},{12,20},{16,8},{20,12},{9,17},{13,21},{17,9},{21,13},{10,18... | collective-permute-start | bytes 786440 | tf_op jit(solution)/shard_map/ppermute | solution.py:484
  27.6 11.4 %copy-start.9 = (f32[256,512]{1,0:T(8,128)S(1)}, f32[256,512]{1,0:T(8,128)}, u32[]{:S(2)}) copy-start(f32[256,512]{1,0:T(8,128)} %get-tuple-element.91) | copy-start | bytes 1572868
  27.6 11.4 %copy-start.11 = (f32[128,512]{1,0:T(8,128)S(1)}, f32[128,512]{1,0:T(8,128)}, u32[]{:S(2)}) copy-start(f32[128,512]{1,0:T(8,128)} %get-tuple-element.89) | copy-start | bytes 786436
  27.7 11.3 %collective-permute-start.9 = (f32[128,512]{1,0:T(8,128)S(1)}, f32[128,512]{1,0:T(8,128)S(1)}, u32[]{:S(2)}, u32[]{:S(2)}) collective-permute-start(f32[128,512]{1,0:T(8,128)S(1)} %get-tuple-element.167), channel_id=1, source_target_pairs={{8,16},{12,20},{16,8},{20,12},{9,17},{13,21},{17,9},{21,13},{10,18... | collective-permute-start | bytes 786440 | tf_op jit(solution)/shard_map/ppermute | solution.py:484
  29.9 9.8 %collective-permute-start.5 = (f32[128,512]{1,0:T(8,128)S(1)}, f32[128,512]{1,0:T(8,128)S(1)}, u32[]{:S(2)}, u32[]{:S(2)}) collective-permute-start(f32[128,512]{1,0:T(8,128)S(1)} %add_select_fusion.1), channel_id=1, source_target_pairs={{0,8},{4,12},{8,0},{12,4},{16,24},{20,28},{24,16},{28,20},{1,9},{5... | collective-permute-start | bytes 786440 | tf_op jit(solution)/shard_map/ppermute | solution.py:484
  39.1 8.4 %collective-permute-start.11 = (f32[128,512]{1,0:T(8,128)S(1)}, f32[128,512]{1,0:T(8,128)S(1)}, u32[]{:S(2)}, u32[]{:S(2)}) collective-permute-start(f32[128,512]{1,0:T(8,128)S(1)} %add_select_fusion), channel_id=1, source_target_pairs={{0,8},{4,12},{8,0},{12,4},{16,24},{20,28},{24,16},{28,20},{1,9},{5... | collective-permute-start | bytes 786440 | tf_op jit(solution)/shard_map/ppermute | solution.py:484
  39.7 7.8 %collective-permute-start.6 = (f32[128,512]{1,0:T(8,128)S(1)}, f32[128,512]{1,0:T(8,128)S(1)}, u32[]{:S(2)}, u32[]{:S(2)}) collective-permute-start(f32[128,512]{1,0:T(8,128)S(1)} %multiply_add_fusion.14), channel_id=1, source_target_pairs={{8,16},{12,20},{16,8},{20,12},{9,17},{13,21},{17,9},{21,13},{10,18... | collective-permute-start | bytes 786440 | tf_op jit(solution)/shard_map/ppermute | solution.py:484
  40.4 21.1 %collective-permute-start.16 = (f32[128,512]{1,0:T(8,128)S(1)}, f32[128,512]{1,0:T(8,128)S(1)}, u32[]{:S(2)}, u32[]{:S(2)}) collective-permute-start(f32[128,512]{1,0:T(8,128)S(1)} %get-tuple-element.166), channel_id=1, source_target_pairs={{0,4},{4,0},{8,12},{12,8},{16,20},{20,16},{24,28},{28,24},{1,5},{5... | collective-permute-start | bytes 786440 | tf_op jit(solution)/shard_map/ppermute | solution.py:484
  42.7 22.3 %collective-permute-start.14 = (f32[128,512]{1,0:T(8,128)S(1)}, f32[128,512]{1,0:T(8,128)S(1)}, u32[]{:S(2)}, u32[]{:S(2)}) collective-permute-start(f32[128,512]{1,0:T(8,128)S(1)} %get-tuple-element.168), channel_id=1, source_target_pairs={{0,4},{4,0},{8,12},{12,8},{16,20},{20,16},{24,28},{28,24},{1,5},{5... | collective-permute-start | bytes 786440 | tf_op jit(solution)/shard_map/ppermute | solution.py:484
  47.6 8.8 %collective-permute-start.7 = (f32[128,512]{1,0:T(8,128)S(1)}, f32[128,512]{1,0:T(8,128)S(1)}, u32[]{:S(2)}, u32[]{:S(2)}) collective-permute-start(f32[128,512]{1,0:T(8,128)S(1)} %add_add_fusion.1), channel_id=1, source_target_pairs={{0,8},{4,12},{8,0},{12,4},{16,24},{20,28},{24,16},{28,20},{1,9},{5... | collective-permute-start | bytes 786440 | tf_op jit(solution)/shard_map/ppermute | solution.py:484
  52.2 5.9 %collective-permute-start.12 = (f32[128,512]{1,0:T(8,128)S(1)}, f32[128,512]{1,0:T(8,128)S(1)}, u32[]{:S(2)}, u32[]{:S(2)}) collective-permute-start(f32[128,512]{1,0:T(8,128)S(1)} %get-tuple-element.175), channel_id=1, source_target_pairs={{8,16},{12,20},{16,8},{20,12},{9,17},{13,21},{17,9},{21,13},{10,18... | collective-permute-start | bytes 786440 | tf_op jit(solution)/shard_map/ppermute | solution.py:484
  53.1 12.0 %collective-permute-start.15 = (f32[128,512]{1,0:T(8,128)S(1)}, f32[128,512]{1,0:T(8,128)S(1)}, u32[]{:S(2)}, u32[]{:S(2)}) collective-permute-start(f32[128,512]{1,0:T(8,128)S(1)} %get-tuple-element.176), channel_id=1, source_target_pairs={{0,4},{4,0},{8,12},{12,8},{16,20},{20,16},{24,28},{28,24},{1,5},{5... | collective-permute-start | bytes 786440 | tf_op jit(solution)/shard_map/ppermute | solution.py:484
  56.7 7.2 %collective-permute-start.17 = (f32[128,512]{1,0:T(8,128)S(1)}, f32[128,512]{1,0:T(8,128)S(1)}, u32[]{:S(2)}, u32[]{:S(2)}) collective-permute-start(f32[128,512]{1,0:T(8,128)S(1)} %get-tuple-element.178), channel_id=1, source_target_pairs={{0,4},{4,0},{8,12},{12,8},{16,20},{20,16},{24,28},{28,24},{1,5},{5... | collective-permute-start | bytes 786440 | tf_op jit(solution)/shard_map/ppermute | solution.py:484
  58.2 8.0 %collective-permute-start.13 = (f32[128,512]{1,0:T(8,128)S(1)}, f32[128,512]{1,0:T(8,128)S(1)}, u32[]{:S(2)}, u32[]{:S(2)}) collective-permute-start(f32[128,512]{1,0:T(8,128)S(1)} %add_add_fusion), channel_id=1, source_target_pairs={{0,8},{4,12},{8,0},{12,4},{16,24},{20,28},{24,16},{28,20},{1,9},{5... | collective-permute-start | bytes 786440 | tf_op jit(solution)/shard_map/ppermute | solution.py:484
  67.5 4.0 %collective-permute-start.18 = (f32[2,64,128]{2,1,0:T(8,128)S(1)}, f32[2,64,128]{2,1,0:T(8,128)S(1)}, u32[]{:S(2)}, u32[]{:S(2)}) collective-permute-start(f32[2,64,128]{2,1,0:T(8,128)S(1)} %get-tuple-element.172), channel_id=1, source_target_pairs={{0,1},{1,0},{2,3},{3,2},{4,5},{5,4},{6,7},{7,6},{8,9},{9,8},{10,11... | collective-permute-start | bytes 196616 | tf_op jit(solution)/shard_map/ppermute | solution.py:630
  67.6 4.5 %collective-permute-start.19 = (f32[2,64,128]{2,1,0:T(8,128)S(1)}, f32[2,64,128]{2,1,0:T(8,128)S(1)}, u32[]{:S(2)}, u32[]{:S(2)}) collective-permute-start(f32[2,64,128]{2,1,0:T(8,128)S(1)} %get-tuple-element.173), channel_id=1, source_target_pairs={{0,2},{1,3},{2,0},{3,1},{4,6},{5,7},{6,4},{7,5},{8,10},{9,11},{10,... | collective-permute-start | bytes 196616 | tf_op jit(solution)/shard_map/ppermute | solution.py:630
  69.2 4.0 %collective-permute-start.20 = (f32[2,64,128]{2,1,0:T(8,128)S(1)}, f32[2,64,128]{2,1,0:T(8,128)S(1)}, u32[]{:S(2)}, u32[]{:S(2)}) collective-permute-start(f32[2,64,128]{2,1,0:T(8,128)S(1)} %get-tuple-element.174), channel_id=1, source_target_pairs={{0,3},{1,2},{2,1},{3,0},{4,7},{5,6},{6,5},{7,4},{8,11},{9,10},{10,... | collective-permute-start | bytes 196616 | tf_op jit(solution)/shard_map/ppermute | solution.py:630
  (11 other events, 54.1 us)

commit v4 on v3

--- a/solution.py
+++ b/solution.py
@@ -121,6 +121,13 @@
     from_start = jnp.exp(rows)
     into_column = into_end.T
     from_column = from_start.T
+    for chunk in range(chunks):
+        heads = slice(chunk * HEADS, (chunk + 1) * HEADS)
+        columns_ref[chunk] = columns[:, heads]
+        into_ref[chunk] = into_column[:, heads]
+        from_ref[chunk] = from_column[:, heads]
+    for source, target in zip(kept[:4], outs[:4]):
+        leave(source, target)
     small[1].wait()
     small[2].wait()
     b_t = b_ref[...].astype(F32).T
@@ -139,9 +146,6 @@
         lanes = pl.ds(chunk * WIDE, WIDE)
         heads = slice(chunk * HEADS, (chunk + 1) * HEADS)
         pairs = range(chunk * HEADS // 2, (chunk + 1) * HEADS // 2)
-        columns_ref[chunk] = columns[:, heads]
-        into_ref[chunk] = into_column[:, heads]
-        from_ref[chunk] = from_column[:, heads]
         totals_ref[:, lanes] = over_lanes(from_column[length - 8 :, heads])[7:8, :]
         for place, (proj, factors, values_ref, rows_at) in enumerate(
             ((b_t, into_end, x_ref, near_at), (c_t, from_start, dy_ref, far_at))
@@ -158,8 +162,7 @@
             place = 5 + late + 2 * (chunk - late)
             leave(messages.at[chunk, :STATE], outs[place])
             leave(messages.at[chunk, STATE:], outs[place + 1])
-    for source, target in zip(kept, outs[:5]):
-        leave(source, target)
+    leave(totals_ref, outs[4])
     for copy in pending:
         copy.wait()
 

time: 75.1 us -> 74.8 us (level)
  no operation moved by 1% of the time
where the time goes in v4:
time: 74.8 us; the launch traced here: 73.6 us
  starting transfers between devices  32.9 us (44%)
  waiting for transfers between devices  16.9 us (23%)
  Pallas kernels  16.7 us (22%)
  other arithmetic  5.95 us (8%)
  between operations  1.04 us (1%)
    ppermute x18, starting transfers between devices, permute(): return lax.ppermute(value, 'ctx', links)  30.9 us
    ppermute x18, waiting for transfers between devices, permute(): return lax.ppermute(value, 'ctx', links)  15.2 us
    pallas_call x4, Pallas kernels, intra(): pl.pallas_call(intra_kernel, grid=(1,), in_specs=[pl.BlockSpec((HEADS, to...  6.39 us
    pallas_call x1, Pallas kernels, local_states(): pl.pallas_call(functools.partial(local_kernel, groups), in_specs=[hbm] *...  5.58 us
    pallas_call x4, Pallas kernels, inter(): pl.pallas_call(functools.partial(inter_kernel, chunk), in_specs=vmem(len(...  3.77 us
    ppermute x3, starting transfers between devices, shards(): parts.append(lax.ppermute(piece(rank ^ step), 'head', links))  1.93 us
    ppermute x3, waiting for transfers between devices, shards(): parts.append(lax.ppermute(piece(rank ^ step), 'head', links))  1.7 us
  transfers between devices with their start and end apart: 21, of which 8 were waited for; matrix products, arithmetic and copies ran while one was open for 7% of the time, Pallas kernels for 14%

profile of v4, /device:TPU:0, one launch (start us, length us, event | category | flops | bytes accessed | tf_op | source)
XLA Modules:
  0.0 73.6 jit_solution(17485192900357962453)
XLA Ops:
  0.6 5.6 %local_states.1 = (f32[32,256]{1,0:T(8,128)}, f32[4,256,8]{2,1,0:T(8,128)}, f32[4,256,8]{2,1,0:T(8,128)}, f32[4,256,8]{2,1,0:T(8,128)}, f32[1,2048]{1,0:T(1,128)...) custom-call(f32[32,256]{1,0:T(8,128)} %decay_in.1, ...), custom_call_target="tpu_custom_call" | custom-call | flops 268435456 | bytes 6291456 | tf_op jit(solution)/shard_map/local_states/pallas_call | solution.py:321
  7.0 5.8 %collective-permute-start = (f32[1,2048]{1,0:T(1,128)}, f32[1,2048]{1,0:T(1,128)S(1)}, u32[]{:S(2)}, u32[]{:S(2)}) collective-permute-start(f32[1,2048]{1,0:T(1,128)} %get-tuple-element.76.total_ref), channel_id=1, source_target_pairs={{0,4},{4,0},{8,12},{12,8},{16,20},{20,16},{24,28},{28,24},{1,5},{5... | collective-permute-start | bytes 24584 | tf_op jit(solution)/shard_map/ppermute | solution.py:487
  12.8 1.6 %collective-permute-start.2 = (f32[128,512]{1,0:T(8,128)}, f32[128,512]{1,0:T(8,128)S(1)}, u32[]{:S(2)}, u32[]{:S(2)}) collective-permute-start(f32[128,512]{1,0:T(8,128)} %get-tuple-element.77), channel_id=1, source_target_pairs={{0,8},{4,12},{8,0},{12,4},{16,24},{20,28},{24,16},{28,20},{1,9},{5... | collective-permute-start | bytes 786440 | tf_op jit(solution)/shard_map/ppermute | solution.py:487
  16.3 2.1 %collective-permute-start.10 = (f32[256,512]{1,0:T(8,128)}, f32[256,512]{1,0:T(8,128)S(1)}, u32[]{:S(2)}, u32[]{:S(2)}) collective-permute-start(f32[256,512]{1,0:T(8,128)} %get-tuple-element.91), channel_id=1, source_target_pairs={{0,4},{4,0},{8,12},{12,8},{16,20},{20,16},{24,28},{28,24},{1,5},{5... | collective-permute-start | bytes 1572872 | tf_op jit(solution)/shard_map/ppermute | solution.py:487
  18.4 2.2 %collective-permute-done.2 = f32[128,512]{1,0:T(8,128)S(1)} collective-permute-done((f32[128,512]{1,0:T(8,128)}, f32[128,512]{1,0:T(8,128)S(1)}, u32[]{:S(2)}, u32[]{:S(2)}) %collective-permute-start.2) | collective-permute-done | bytes 262176 | tf_op jit(solution)/shard_map/ppermute | solution.py:487
  20.5 1.6 %collective-permute-start.8 = (f32[128,512]{1,0:T(8,128)}, f32[128,512]{1,0:T(8,128)S(1)}, u32[]{:S(2)}, u32[]{:S(2)}) collective-permute-start(f32[128,512]{1,0:T(8,128)} %get-tuple-element.88), channel_id=1, source_target_pairs={{0,8},{4,12},{8,0},{12,4},{16,24},{20,28},{24,16},{28,20},{1,9},{5... | collective-permute-start | bytes 786440 | tf_op jit(solution)/shard_map/ppermute | solution.py:487
  22.1 1.1 %multiply_add_fusion.17 = (f32[128,512]{1,0:T(8,128)S(1)}, f32[128,512]{1,0:T(8,128)S(1)}) fusion(f32[128,512]{1,0:T(8,128)} %get-tuple-element.77, f32[128,512]{1,0:T(8,128)S(1)} %collective-permute-done.2, f32[512]{0:T(512)S(1)} %bitcast.56, f32[]{:T(128)S(6)} %select_n.242, f32[512]{0:T(512)S(1)} %bitcast.57), kind=kLoop, calls=%fused_computation.30 | loop fusion | flops 327680 | bytes 1052676 | tf_op jit(solution)/shard_map/add | solution.py:554
  23.9 3.4 %collective-permute-done.8 = f32[128,512]{1,0:T(8,128)S(1)} collective-permute-done((f32[128,512]{1,0:T(8,128)}, f32[128,512]{1,0:T(8,128)S(1)}, u32[]{:S(2)}, u32[]{:S(2)}) %collective-permute-start.8) | collective-permute-done | bytes 262176 | tf_op jit(solution)/shard_map/ppermute | solution.py:487
  28.2 1.3 %collective-permute-done.4 = f32[256,512]{1,0:T(8,128)S(1)} collective-permute-done((f32[256,512]{1,0:T(8,128)}, f32[256,512]{1,0:T(8,128)S(1)}, u32[]{:S(2)}, u32[]{:S(2)}) %collective-permute-start.4) | collective-permute-done | bytes 524320 | tf_op jit(solution)/shard_map/ppermute | solution.py:487
  29.6 3.4 %collective-permute-start.5 = (f32[128,512]{1,0:T(8,128)S(1)}, f32[128,512]{1,0:T(8,128)S(1)}, u32[]{:S(2)}, u32[]{:S(2)}) collective-permute-start(f32[128,512]{1,0:T(8,128)S(1)} %add_select_fusion.1), channel_id=1, source_target_pairs={{0,8},{4,12},{8,0},{12,4},{16,24},{20,28},{24,16},{28,20},{1,9},{5... | collective-permute-start | bytes 786440 | tf_op jit(solution)/shard_map/ppermute | solution.py:487
  33.0 5.7 %collective-permute-done.10 = f32[256,512]{1,0:T(8,128)S(1)} collective-permute-done((f32[256,512]{1,0:T(8,128)}, f32[256,512]{1,0:T(8,128)S(1)}, u32[]{:S(2)}, u32[]{:S(2)}) %collective-permute-start.10) | collective-permute-done | bytes 524320 | tf_op jit(solution)/shard_map/ppermute | solution.py:487
  40.9 1.6 %intra.4 = (f32[256,512]{1,0:T(8,128)S(1)}, bf16[256,512]{1,0:T(8,128)(2,1)S(1)}, bf16[256,512]{1,0:T(8,128)(2,1)S(1)}, f32[8,256]{1,0:T(8,128)S(1)}, f32[256,128]{1,0:T(8,128)S(1)}, /*index=5*/f32[256,128]{1,0:T(8,128)S(1)}) custom-call(f32[32,256]{1,0:T(8,128)S(1)} %copy-done.7, f32[4,256,8]{2,1,0:T(8,128)S(1)} %copy-done.3, f32[4,256,8]{2,1,0:T(8,128)S(1)} %copy-done, ...), custom_call_target="tpu_custom_call" | custom-call | flops 134217728 | bytes 1048576 | tf_op jit(solution)/shard_map/intra/pallas_call | solution.py:351
  42.5 1.6 %collective-permute-start.14 = (f32[128,512]{1,0:T(8,128)S(1)}, f32[128,512]{1,0:T(8,128)S(1)}, u32[]{:S(2)}, u32[]{:S(2)}) collective-permute-start(f32[128,512]{1,0:T(8,128)S(1)} %get-tuple-element.168), channel_id=1, source_target_pairs={{0,4},{4,0},{8,12},{12,8},{16,20},{20,16},{24,28},{28,24},{1,5},{5... | collective-permute-start | bytes 786440 | tf_op jit(solution)/shard_map/ppermute | solution.py:487
  44.0 1.6 %intra.5 = (f32[256,512]{1,0:T(8,128)S(1)}, bf16[256,512]{1,0:T(8,128)(2,1)S(1)}, bf16[256,512]{1,0:T(8,128)(2,1)S(1)}, f32[8,256]{1,0:T(8,128)S(1)}, f32[256,128]{1,0:T(8,128)S(1)}, /*index=5*/f32[256,128]{1,0:T(8,128)S(1)}) custom-call(f32[32,256]{1,0:T(8,128)S(1)} %copy-done.7, f32[4,256,8]{2,1,0:T(8,128)S(1)} %copy-done.3, f32[4,256,8]{2,1,0:T(8,128)S(1)} %copy-done, ...), custom_call_target="tpu_custom_call" | custom-call | flops 134217728 | bytes 1048576 | tf_op jit(solution)/shard_map/intra/pallas_call | solution.py:351
  45.6 1.6 %intra.6 = (f32[256,512]{1,0:T(8,128)S(1)}, bf16[256,512]{1,0:T(8,128)(2,1)S(1)}, bf16[256,512]{1,0:T(8,128)(2,1)S(1)}, f32[8,256]{1,0:T(8,128)S(1)}, f32[256,128]{1,0:T(8,128)S(1)}, /*index=5*/f32[256,128]{1,0:T(8,128)S(1)}) custom-call(f32[32,256]{1,0:T(8,128)S(1)} %copy-done.7, f32[4,256,8]{2,1,0:T(8,128)S(1)} %copy-done.3, f32[4,256,8]{2,1,0:T(8,128)S(1)} %copy-done, ...), custom_call_target="tpu_custom_call" | custom-call | flops 134217728 | bytes 1048576 | tf_op jit(solution)/shard_map/intra/pallas_call | solution.py:351
  47.3 4.4 %collective-permute-start.7 = (f32[128,512]{1,0:T(8,128)S(1)}, f32[128,512]{1,0:T(8,128)S(1)}, u32[]{:S(2)}, u32[]{:S(2)}) collective-permute-start(f32[128,512]{1,0:T(8,128)S(1)} %add_add_fusion.1), channel_id=1, source_target_pairs={{0,8},{4,12},{8,0},{12,4},{16,24},{20,28},{24,16},{28,20},{1,9},{5... | collective-permute-start | bytes 786440 | tf_op jit(solution)/shard_map/ppermute | solution.py:487
  52.8 1.4 %collective-permute-start.15 = (f32[128,512]{1,0:T(8,128)S(1)}, f32[128,512]{1,0:T(8,128)S(1)}, u32[]{:S(2)}, u32[]{:S(2)}) collective-permute-start(f32[128,512]{1,0:T(8,128)S(1)} %get-tuple-element.176), channel_id=1, source_target_pairs={{0,4},{4,0},{8,12},{12,8},{16,20},{20,16},{24,28},{28,24},{1,5},{5... | collective-permute-start | bytes 786440 | tf_op jit(solution)/shard_map/ppermute | solution.py:487
  54.2 1.6 %intra.7 = (f32[256,512]{1,0:T(8,128)S(1)}, bf16[256,512]{1,0:T(8,128)(2,1)S(1)}, bf16[256,512]{1,0:T(8,128)(2,1)S(1)}, f32[8,256]{1,0:T(8,128)S(1)}, f32[256,128]{1,0:T(8,128)S(1)}, /*index=5*/f32[256,128]{1,0:T(8,128)S(1)}) custom-call(f32[32,256]{1,0:T(8,128)S(1)} %copy-done.7, f32[4,256,8]{2,1,0:T(8,128)S(1)} %copy-done.3, f32[4,256,8]{2,1,0:T(8,128)S(1)} %copy-done, ...), custom_call_target="tpu_custom_call" | custom-call | flops 134217728 | bytes 1048576 | tf_op jit(solution)/shard_map/intra/pallas_call | solution.py:351
  56.4 1.4 %collective-permute-start.17 = (f32[128,512]{1,0:T(8,128)S(1)}, f32[128,512]{1,0:T(8,128)S(1)}, u32[]{:S(2)}, u32[]{:S(2)}) collective-permute-start(f32[128,512]{1,0:T(8,128)S(1)} %get-tuple-element.178), channel_id=1, source_target_pairs={{0,4},{4,0},{8,12},{12,8},{16,20},{20,16},{24,28},{28,24},{1,5},{5... | collective-permute-start | bytes 786440 | tf_op jit(solution)/shard_map/ppermute | solution.py:487
  57.9 2.4 %collective-permute-start.13 = (f32[128,512]{1,0:T(8,128)S(1)}, f32[128,512]{1,0:T(8,128)S(1)}, u32[]{:S(2)}, u32[]{:S(2)}) collective-permute-start(f32[128,512]{1,0:T(8,128)S(1)} %add_add_fusion), channel_id=1, source_target_pairs={{0,8},{4,12},{8,0},{12,4},{16,24},{20,28},{24,16},{28,20},{1,9},{5... | collective-permute-start | bytes 786440 | tf_op jit(solution)/shard_map/ppermute | solution.py:487
  61.3 2.3 %collective-permute-done.17 = f32[128,512]{1,0:T(8,128)S(1)} collective-permute-done((f32[128,512]{1,0:T(8,128)S(1)}, f32[128,512]{1,0:T(8,128)S(1)}, u32[]{:S(2)}, u32[]{:S(2)}) %collective-permute-start.17) | collective-permute-done | bytes 262176 | tf_op jit(solution)/shard_map/ppermute | solution.py:487
  67.3 1.6 %collective-permute-start.19 = (f32[2,64,128]{2,1,0:T(8,128)S(1)}, f32[2,64,128]{2,1,0:T(8,128)S(1)}, u32[]{:S(2)}, u32[]{:S(2)}) collective-permute-start(f32[2,64,128]{2,1,0:T(8,128)S(1)} %get-tuple-element.173), channel_id=1, source_target_pairs={{0,2},{1,3},{2,0},{3,1},{4,6},{5,7},{6,4},{7,5},{8,10},{9,11},{10,... | collective-permute-start | bytes 196616 | tf_op jit(solution)/shard_map/ppermute | solution.py:633
  69.2 1.1 %pad_maximum_fusion = bf16[256,2048]{1,0:T(8,128)(2,1)} fusion(bf16[256,512]{1,0:T(8,128)(2,1)S(1)} %get-tuple-element.127, bf16[256,512]{1,0:T(8,128)(2,1)S(1)} %get-tuple-element.126, bf16[256,512]{1,0:T(8,128)(2,1)S(1)} %get-tuple-element.125, bf16[256,512]{1,0:T(8,128)(2,1)S(1)} %get-tuple-element.103), kind=kLoop, calls=%fused_computation | loop fusion | flops 4194304 | bytes 2097152 | tf_op jit(solution)/shard_map/concatenate | solution.py:619
  71.8 1.1 %collective-permute-done.20 = f32[2,64,128]{2,1,0:T(8,128)S(1)} collective-permute-done((f32[2,64,128]{2,1,0:T(8,128)S(1)}, f32[2,64,128]{2,1,0:T(8,128)S(1)}, u32[]{:S(2)}, u32[]{:S(2)}) %collective-permute-start.20) | collective-permute-done | bytes 65568 | tf_op jit(solution)/shard_map/ppermute | solution.py:633
  (85 shorter events, 15.1 us)
Async XLA Ops:
  6.2 21.1 %copy-start.13 = (f32[128,512]{1,0:T(8,128)S(1)}, f32[128,512]{1,0:T(8,128)}, u32[]{:S(2)}) copy-start(f32[128,512]{1,0:T(8,128)} %get-tuple-element.88) | copy-start | bytes 786436
  6.2 8.5 %collective-permute-start.1 = (f32[1,2048]{1,0:T(1,128)}, f32[1,2048]{1,0:T(1,128)S(1)}, u32[]{:S(2)}, u32[]{:S(2)}) collective-permute-start(f32[1,2048]{1,0:T(1,128)} %get-tuple-element.76.total_ref), channel_id=1, source_target_pairs={{4,8},{12,16},{20,24},{8,4},{16,12},{24,20},{5,9},{13,17},{21,25},... | collective-permute-start | bytes 24584 | tf_op jit(solution)/shard_map/ppermute | solution.py:487
  7.0 7.7 %collective-permute-start = (f32[1,2048]{1,0:T(1,128)}, f32[1,2048]{1,0:T(1,128)S(1)}, u32[]{:S(2)}, u32[]{:S(2)}) collective-permute-start(f32[1,2048]{1,0:T(1,128)} %get-tuple-element.76.total_ref), channel_id=1, source_target_pairs={{0,4},{4,0},{8,12},{12,8},{16,20},{20,16},{24,28},{28,24},{1,5},{5... | collective-permute-start | bytes 24584 | tf_op jit(solution)/shard_map/ppermute | solution.py:487
  12.8 7.7 %collective-permute-start.2 = (f32[128,512]{1,0:T(8,128)}, f32[128,512]{1,0:T(8,128)S(1)}, u32[]{:S(2)}, u32[]{:S(2)}) collective-permute-start(f32[128,512]{1,0:T(8,128)} %get-tuple-element.77), channel_id=1, source_target_pairs={{0,8},{4,12},{8,0},{12,4},{16,24},{20,28},{24,16},{28,20},{1,9},{5... | collective-permute-start | bytes 786440 | tf_op jit(solution)/shard_map/ppermute | solution.py:487
  14.4 15.1 %collective-permute-start.4 = (f32[256,512]{1,0:T(8,128)}, f32[256,512]{1,0:T(8,128)S(1)}, u32[]{:S(2)}, u32[]{:S(2)}) collective-permute-start(f32[256,512]{1,0:T(8,128)} %get-tuple-element.79), channel_id=1, source_target_pairs={{0,4},{4,0},{8,12},{12,8},{16,20},{20,16},{24,28},{28,24},{1,5},{5... | collective-permute-start | bytes 1572872 | tf_op jit(solution)/shard_map/ppermute | solution.py:487
  16.3 22.4 %collective-permute-start.10 = (f32[256,512]{1,0:T(8,128)}, f32[256,512]{1,0:T(8,128)S(1)}, u32[]{:S(2)}, u32[]{:S(2)}) collective-permute-start(f32[256,512]{1,0:T(8,128)} %get-tuple-element.91), channel_id=1, source_target_pairs={{0,4},{4,0},{8,12},{12,8},{16,20},{20,16},{24,28},{28,24},{1,5},{5... | collective-permute-start | bytes 1572872 | tf_op jit(solution)/shard_map/ppermute | solution.py:487
  20.5 6.8 %collective-permute-start.8 = (f32[128,512]{1,0:T(8,128)}, f32[128,512]{1,0:T(8,128)S(1)}, u32[]{:S(2)}, u32[]{:S(2)}) collective-permute-start(f32[128,512]{1,0:T(8,128)} %get-tuple-element.88), channel_id=1, source_target_pairs={{0,8},{4,12},{8,0},{12,4},{16,24},{20,28},{24,16},{28,20},{1,9},{5... | collective-permute-start | bytes 786440 | tf_op jit(solution)/shard_map/ppermute | solution.py:487
  23.2 5.0 %collective-permute-start.3 = (f32[128,512]{1,0:T(8,128)S(1)}, f32[128,512]{1,0:T(8,128)S(1)}, u32[]{:S(2)}, u32[]{:S(2)}) collective-permute-start(f32[128,512]{1,0:T(8,128)S(1)} %get-tuple-element.165), channel_id=1, source_target_pairs={{8,16},{12,20},{16,8},{20,12},{9,17},{13,21},{17,9},{21,13},{10,18... | collective-permute-start | bytes 786440 | tf_op jit(solution)/shard_map/ppermute | solution.py:487
  27.3 11.4 %copy-start.9 = (f32[256,512]{1,0:T(8,128)S(1)}, f32[256,512]{1,0:T(8,128)}, u32[]{:S(2)}) copy-start(f32[256,512]{1,0:T(8,128)} %get-tuple-element.91) | copy-start | bytes 1572868
  27.3 11.4 %copy-start.11 = (f32[128,512]{1,0:T(8,128)S(1)}, f32[128,512]{1,0:T(8,128)}, u32[]{:S(2)}) copy-start(f32[128,512]{1,0:T(8,128)} %get-tuple-element.89) | copy-start | bytes 786436
  27.4 11.3 %collective-permute-start.9 = (f32[128,512]{1,0:T(8,128)S(1)}, f32[128,512]{1,0:T(8,128)S(1)}, u32[]{:S(2)}, u32[]{:S(2)}) collective-permute-start(f32[128,512]{1,0:T(8,128)S(1)} %get-tuple-element.167), channel_id=1, source_target_pairs={{8,16},{12,20},{16,8},{20,12},{9,17},{13,21},{17,9},{21,13},{10,18... | collective-permute-start | bytes 786440 | tf_op jit(solution)/shard_map/ppermute | solution.py:487
  29.6 9.8 %collective-permute-start.5 = (f32[128,512]{1,0:T(8,128)S(1)}, f32[128,512]{1,0:T(8,128)S(1)}, u32[]{:S(2)}, u32[]{:S(2)}) collective-permute-start(f32[128,512]{1,0:T(8,128)S(1)} %add_select_fusion.1), channel_id=1, source_target_pairs={{0,8},{4,12},{8,0},{12,4},{16,24},{20,28},{24,16},{28,20},{1,9},{5... | collective-permute-start | bytes 786440 | tf_op jit(solution)/shard_map/ppermute | solution.py:487
  38.9 8.4 %collective-permute-start.11 = (f32[128,512]{1,0:T(8,128)S(1)}, f32[128,512]{1,0:T(8,128)S(1)}, u32[]{:S(2)}, u32[]{:S(2)}) collective-permute-start(f32[128,512]{1,0:T(8,128)S(1)} %add_select_fusion), channel_id=1, source_target_pairs={{0,8},{4,12},{8,0},{12,4},{16,24},{20,28},{24,16},{28,20},{1,9},{5... | collective-permute-start | bytes 786440 | tf_op jit(solution)/shard_map/ppermute | solution.py:487
  39.5 7.8 %collective-permute-start.6 = (f32[128,512]{1,0:T(8,128)S(1)}, f32[128,512]{1,0:T(8,128)S(1)}, u32[]{:S(2)}, u32[]{:S(2)}) collective-permute-start(f32[128,512]{1,0:T(8,128)S(1)} %multiply_add_fusion.14), channel_id=1, source_target_pairs={{8,16},{12,20},{16,8},{20,12},{9,17},{13,21},{17,9},{21,13},{10,18... | collective-permute-start | bytes 786440 | tf_op jit(solution)/shard_map/ppermute | solution.py:487
  40.2 21.1 %collective-permute-start.16 = (f32[128,512]{1,0:T(8,128)S(1)}, f32[128,512]{1,0:T(8,128)S(1)}, u32[]{:S(2)}, u32[]{:S(2)}) collective-permute-start(f32[128,512]{1,0:T(8,128)S(1)} %get-tuple-element.166), channel_id=1, source_target_pairs={{0,4},{4,0},{8,12},{12,8},{16,20},{20,16},{24,28},{28,24},{1,5},{5... | collective-permute-start | bytes 786440 | tf_op jit(solution)/shard_map/ppermute | solution.py:487
  42.5 22.3 %collective-permute-start.14 = (f32[128,512]{1,0:T(8,128)S(1)}, f32[128,512]{1,0:T(8,128)S(1)}, u32[]{:S(2)}, u32[]{:S(2)}) collective-permute-start(f32[128,512]{1,0:T(8,128)S(1)} %get-tuple-element.168), channel_id=1, source_target_pairs={{0,4},{4,0},{8,12},{12,8},{16,20},{20,16},{24,28},{28,24},{1,5},{5... | collective-permute-start | bytes 786440 | tf_op jit(solution)/shard_map/ppermute | solution.py:487
  47.3 8.8 %collective-permute-start.7 = (f32[128,512]{1,0:T(8,128)S(1)}, f32[128,512]{1,0:T(8,128)S(1)}, u32[]{:S(2)}, u32[]{:S(2)}) collective-permute-start(f32[128,512]{1,0:T(8,128)S(1)} %add_add_fusion.1), channel_id=1, source_target_pairs={{0,8},{4,12},{8,0},{12,4},{16,24},{20,28},{24,16},{28,20},{1,9},{5... | collective-permute-start | bytes 786440 | tf_op jit(solution)/shard_map/ppermute | solution.py:487
  51.9 5.9 %collective-permute-start.12 = (f32[128,512]{1,0:T(8,128)S(1)}, f32[128,512]{1,0:T(8,128)S(1)}, u32[]{:S(2)}, u32[]{:S(2)}) collective-permute-start(f32[128,512]{1,0:T(8,128)S(1)} %get-tuple-element.175), channel_id=1, source_target_pairs={{8,16},{12,20},{16,8},{20,12},{9,17},{13,21},{17,9},{21,13},{10,18... | collective-permute-start | bytes 786440 | tf_op jit(solution)/shard_map/ppermute | solution.py:487
  52.8 12.0 %collective-permute-start.15 = (f32[128,512]{1,0:T(8,128)S(1)}, f32[128,512]{1,0:T(8,128)S(1)}, u32[]{:S(2)}, u32[]{:S(2)}) collective-permute-start(f32[128,512]{1,0:T(8,128)S(1)} %get-tuple-element.176), channel_id=1, source_target_pairs={{0,4},{4,0},{8,12},{12,8},{16,20},{20,16},{24,28},{28,24},{1,5},{5... | collective-permute-start | bytes 786440 | tf_op jit(solution)/shard_map/ppermute | solution.py:487
  56.4 7.2 %collective-permute-start.17 = (f32[128,512]{1,0:T(8,128)S(1)}, f32[128,512]{1,0:T(8,128)S(1)}, u32[]{:S(2)}, u32[]{:S(2)}) collective-permute-start(f32[128,512]{1,0:T(8,128)S(1)} %get-tuple-element.178), channel_id=1, source_target_pairs={{0,4},{4,0},{8,12},{12,8},{16,20},{20,16},{24,28},{28,24},{1,5},{5... | collective-permute-start | bytes 786440 | tf_op jit(solution)/shard_map/ppermute | solution.py:487
  57.9 8.0 %collective-permute-start.13 = (f32[128,512]{1,0:T(8,128)S(1)}, f32[128,512]{1,0:T(8,128)S(1)}, u32[]{:S(2)}, u32[]{:S(2)}) collective-permute-start(f32[128,512]{1,0:T(8,128)S(1)} %add_add_fusion), channel_id=1, source_target_pairs={{0,8},{4,12},{8,0},{12,4},{16,24},{20,28},{24,16},{28,20},{1,9},{5... | collective-permute-start | bytes 786440 | tf_op jit(solution)/shard_map/ppermute | solution.py:487
  67.2 4.0 %collective-permute-start.18 = (f32[2,64,128]{2,1,0:T(8,128)S(1)}, f32[2,64,128]{2,1,0:T(8,128)S(1)}, u32[]{:S(2)}, u32[]{:S(2)}) collective-permute-start(f32[2,64,128]{2,1,0:T(8,128)S(1)} %get-tuple-element.172), channel_id=1, source_target_pairs={{0,1},{1,0},{2,3},{3,2},{4,5},{5,4},{6,7},{7,6},{8,9},{9,8},{10,11... | collective-permute-start | bytes 196616 | tf_op jit(solution)/shard_map/ppermute | solution.py:633
  67.3 4.5 %collective-permute-start.19 = (f32[2,64,128]{2,1,0:T(8,128)S(1)}, f32[2,64,128]{2,1,0:T(8,128)S(1)}, u32[]{:S(2)}, u32[]{:S(2)}) collective-permute-start(f32[2,64,128]{2,1,0:T(8,128)S(1)} %get-tuple-element.173), channel_id=1, source_target_pairs={{0,2},{1,3},{2,0},{3,1},{4,6},{5,7},{6,4},{7,5},{8,10},{9,11},{10,... | collective-permute-start | bytes 196616 | tf_op jit(solution)/shard_map/ppermute | solution.py:633
  68.9 4.0 %collective-permute-start.20 = (f32[2,64,128]{2,1,0:T(8,128)S(1)}, f32[2,64,128]{2,1,0:T(8,128)S(1)}, u32[]{:S(2)}, u32[]{:S(2)}) collective-permute-start(f32[2,64,128]{2,1,0:T(8,128)S(1)} %get-tuple-element.174), channel_id=1, source_target_pairs={{0,3},{1,2},{2,1},{3,0},{4,7},{5,6},{6,5},{7,4},{8,11},{9,10},{10,... | collective-permute-start | bytes 196616 | tf_op jit(solution)/shard_map/ppermute | solution.py:633
  (11 other events, 54.1 us)

commit v5 on v4

--- a/solution.py
+++ b/solution.py
@@ -277,8 +277,10 @@
     gc_out_ref[...] = gc_ref[...] + dot(dys, state_low, NT)
     outer = dot(b_ref[...], adjoint_low)
     gx_ref[...] = (dx_ref[...] + over_lanes(into_ref[chunk]) * outer).astype(BF16)
-    change_ref[...] = per_head(dys.astype(F32) * dot(c_ref[...], state_low))
-    earlier_ref[...] = per_head(xs.astype(F32) * outer)
+    spread = spread_matrix(HEADS).astype(BF16)
+    change = dys.astype(F32) * dot(c_ref[...], state_low)
+    change_ref[...] = dot(spread, change.astype(BF16), NT)
+    earlier_ref[...] = dot(spread, (xs.astype(F32) * outer).astype(BF16), NT)
     later_ref[...] = per_head(total_ref[:, lanes] * state_in * adjoint_in)
 
 

time: 74.8 us -> 74.3 us (level)
  transfers between devices with their start and end apart: 21 -> 21, of which waited for: 8 -> 8; matrix products, arithmetic and copies ran while one was open for 7% -> 7% of each run, Pallas kernels for 14% -> 13%
where the time goes in v5:
time: 74.3 us; the launch traced here: 73.1 us
  starting transfers between devices  32.9 us (44%)
  waiting for transfers between devices  17.1 us (23%)
  Pallas kernels  16 us (22%)
  other arithmetic  5.95 us (8%)
  between operations  1.04 us (1%)
    ppermute x18, starting transfers between devices, permute(): return lax.ppermute(value, 'ctx', links)  30.9 us
    ppermute x18, waiting for transfers between devices, permute(): return lax.ppermute(value, 'ctx', links)  15.4 us
    pallas_call x4, Pallas kernels, intra(): pl.pallas_call(intra_kernel, grid=(1,), in_specs=[pl.BlockSpec((HEADS, to...  6.39 us
    pallas_call x1, Pallas kernels, local_states(): pl.pallas_call(functools.partial(local_kernel, groups), in_specs=[hbm] *...  5.58 us
    pallas_call x4, Pallas kernels, inter(): pl.pallas_call(functools.partial(inter_kernel, chunk), in_specs=vmem(len(...  3.09 us
    ppermute x3, starting transfers between devices, shards(): parts.append(lax.ppermute(piece(rank ^ step), 'head', links))  1.93 us
    ppermute x3, waiting for transfers between devices, shards(): parts.append(lax.ppermute(piece(rank ^ step), 'head', links))  1.69 us
  transfers between devices with their start and end apart: 21, of which 8 were waited for; matrix products, arithmetic and copies ran while one was open for 7% of the time, Pallas kernels for 13%

profile of v5, /device:TPU:0, one launch (start us, length us, event | category | flops | bytes accessed | tf_op | source)
XLA Modules:
  0.0 73.1 jit_solution(11075000690987712398)
XLA Ops:
  0.6 5.6 %local_states.1 = (f32[32,256]{1,0:T(8,128)}, f32[4,256,8]{2,1,0:T(8,128)}, f32[4,256,8]{2,1,0:T(8,128)}, f32[4,256,8]{2,1,0:T(8,128)}, f32[1,2048]{1,0:T(1,128)...) custom-call(f32[32,256]{1,0:T(8,128)} %decay_in.1, ...), custom_call_target="tpu_custom_call" | custom-call | flops 268435456 | bytes 6291456 | tf_op jit(solution)/shard_map/local_states/pallas_call | solution.py:323
  7.0 5.8 %collective-permute-start = (f32[1,2048]{1,0:T(1,128)}, f32[1,2048]{1,0:T(1,128)S(1)}, u32[]{:S(2)}, u32[]{:S(2)}) collective-permute-start(f32[1,2048]{1,0:T(1,128)} %get-tuple-element.76.total_ref), channel_id=1, source_target_pairs={{0,4},{4,0},{8,12},{12,8},{16,20},{20,16},{24,28},{28,24},{1,5},{5... | collective-permute-start | bytes 24584 | tf_op jit(solution)/shard_map/ppermute | solution.py:489
  12.8 1.6 %collective-permute-start.2 = (f32[128,512]{1,0:T(8,128)}, f32[128,512]{1,0:T(8,128)S(1)}, u32[]{:S(2)}, u32[]{:S(2)}) collective-permute-start(f32[128,512]{1,0:T(8,128)} %get-tuple-element.77), channel_id=1, source_target_pairs={{0,8},{4,12},{8,0},{12,4},{16,24},{20,28},{24,16},{28,20},{1,9},{5... | collective-permute-start | bytes 786440 | tf_op jit(solution)/shard_map/ppermute | solution.py:489
  16.3 2.1 %collective-permute-start.10 = (f32[256,512]{1,0:T(8,128)}, f32[256,512]{1,0:T(8,128)S(1)}, u32[]{:S(2)}, u32[]{:S(2)}) collective-permute-start(f32[256,512]{1,0:T(8,128)} %get-tuple-element.91), channel_id=1, source_target_pairs={{0,4},{4,0},{8,12},{12,8},{16,20},{20,16},{24,28},{28,24},{1,5},{5... | collective-permute-start | bytes 1572872 | tf_op jit(solution)/shard_map/ppermute | solution.py:489
  18.4 2.2 %collective-permute-done.2 = f32[128,512]{1,0:T(8,128)S(1)} collective-permute-done((f32[128,512]{1,0:T(8,128)}, f32[128,512]{1,0:T(8,128)S(1)}, u32[]{:S(2)}, u32[]{:S(2)}) %collective-permute-start.2) | collective-permute-done | bytes 262176 | tf_op jit(solution)/shard_map/ppermute | solution.py:489
  20.5 1.6 %collective-permute-start.8 = (f32[128,512]{1,0:T(8,128)}, f32[128,512]{1,0:T(8,128)S(1)}, u32[]{:S(2)}, u32[]{:S(2)}) collective-permute-start(f32[128,512]{1,0:T(8,128)} %get-tuple-element.88), channel_id=1, source_target_pairs={{0,8},{4,12},{8,0},{12,4},{16,24},{20,28},{24,16},{28,20},{1,9},{5... | collective-permute-start | bytes 786440 | tf_op jit(solution)/shard_map/ppermute | solution.py:489
  22.1 1.1 %multiply_add_fusion.17 = (f32[128,512]{1,0:T(8,128)S(1)}, f32[128,512]{1,0:T(8,128)S(1)}) fusion(f32[128,512]{1,0:T(8,128)} %get-tuple-element.77, f32[128,512]{1,0:T(8,128)S(1)} %collective-permute-done.2, f32[512]{0:T(512)S(1)} %bitcast.56, f32[]{:T(128)S(6)} %select_n.242, f32[512]{0:T(512)S(1)} %bitcast.57), kind=kLoop, calls=%fused_computation.30 | loop fusion | flops 327680 | bytes 1052676 | tf_op jit(solution)/shard_map/add | solution.py:556
  23.9 3.4 %collective-permute-done.8 = f32[128,512]{1,0:T(8,128)S(1)} collective-permute-done((f32[128,512]{1,0:T(8,128)}, f32[128,512]{1,0:T(8,128)S(1)}, u32[]{:S(2)}, u32[]{:S(2)}) %collective-permute-start.8) | collective-permute-done | bytes 262176 | tf_op jit(solution)/shard_map/ppermute | solution.py:489
  28.2 1.3 %collective-permute-done.4 = f32[256,512]{1,0:T(8,128)S(1)} collective-permute-done((f32[256,512]{1,0:T(8,128)}, f32[256,512]{1,0:T(8,128)S(1)}, u32[]{:S(2)}, u32[]{:S(2)}) %collective-permute-start.4) | collective-permute-done | bytes 524320 | tf_op jit(solution)/shard_map/ppermute | solution.py:489
  29.6 3.4 %collective-permute-start.5 = (f32[128,512]{1,0:T(8,128)S(1)}, f32[128,512]{1,0:T(8,128)S(1)}, u32[]{:S(2)}, u32[]{:S(2)}) collective-permute-start(f32[128,512]{1,0:T(8,128)S(1)} %add_select_fusion.1), channel_id=1, source_target_pairs={{0,8},{4,12},{8,0},{12,4},{16,24},{20,28},{24,16},{28,20},{1,9},{5... | collective-permute-start | bytes 786440 | tf_op jit(solution)/shard_map/ppermute | solution.py:489
  33.0 5.7 %collective-permute-done.10 = f32[256,512]{1,0:T(8,128)S(1)} collective-permute-done((f32[256,512]{1,0:T(8,128)}, f32[256,512]{1,0:T(8,128)S(1)}, u32[]{:S(2)}, u32[]{:S(2)}) %collective-permute-start.10) | collective-permute-done | bytes 524320 | tf_op jit(solution)/shard_map/ppermute | solution.py:489
  40.9 1.6 %intra.4 = (f32[256,512]{1,0:T(8,128)S(1)}, bf16[256,512]{1,0:T(8,128)(2,1)S(1)}, bf16[256,512]{1,0:T(8,128)(2,1)S(1)}, f32[8,256]{1,0:T(8,128)S(1)}, f32[256,128]{1,0:T(8,128)S(1)}, /*index=5*/f32[256,128]{1,0:T(8,128)S(1)}) custom-call(f32[32,256]{1,0:T(8,128)S(1)} %copy-done.7, f32[4,256,8]{2,1,0:T(8,128)S(1)} %copy-done.3, f32[4,256,8]{2,1,0:T(8,128)S(1)} %copy-done, ...), custom_call_target="tpu_custom_call" | custom-call | flops 134217728 | bytes 1048576 | tf_op jit(solution)/shard_map/intra/pallas_call | solution.py:353
  42.5 1.6 %collective-permute-start.14 = (f32[128,512]{1,0:T(8,128)S(1)}, f32[128,512]{1,0:T(8,128)S(1)}, u32[]{:S(2)}, u32[]{:S(2)}) collective-permute-start(f32[128,512]{1,0:T(8,128)S(1)} %get-tuple-element.168), channel_id=1, source_target_pairs={{0,4},{4,0},{8,12},{12,8},{16,20},{20,16},{24,28},{28,24},{1,5},{5... | collective-permute-start | bytes 786440 | tf_op jit(solution)/shard_map/ppermute | solution.py:489
  44.0 1.6 %intra.5 = (f32[256,512]{1,0:T(8,128)S(1)}, bf16[256,512]{1,0:T(8,128)(2,1)S(1)}, bf16[256,512]{1,0:T(8,128)(2,1)S(1)}, f32[8,256]{1,0:T(8,128)S(1)}, f32[256,128]{1,0:T(8,128)S(1)}, /*index=5*/f32[256,128]{1,0:T(8,128)S(1)}) custom-call(f32[32,256]{1,0:T(8,128)S(1)} %copy-done.7, f32[4,256,8]{2,1,0:T(8,128)S(1)} %copy-done.3, f32[4,256,8]{2,1,0:T(8,128)S(1)} %copy-done, ...), custom_call_target="tpu_custom_call" | custom-call | flops 134217728 | bytes 1048576 | tf_op jit(solution)/shard_map/intra/pallas_call | solution.py:353
  45.6 1.6 %intra.6 = (f32[256,512]{1,0:T(8,128)S(1)}, bf16[256,512]{1,0:T(8,128)(2,1)S(1)}, bf16[256,512]{1,0:T(8,128)(2,1)S(1)}, f32[8,256]{1,0:T(8,128)S(1)}, f32[256,128]{1,0:T(8,128)S(1)}, /*index=5*/f32[256,128]{1,0:T(8,128)S(1)}) custom-call(f32[32,256]{1,0:T(8,128)S(1)} %copy-done.7, f32[4,256,8]{2,1,0:T(8,128)S(1)} %copy-done.3, f32[4,256,8]{2,1,0:T(8,128)S(1)} %copy-done, ...), custom_call_target="tpu_custom_call" | custom-call | flops 134217728 | bytes 1048576 | tf_op jit(solution)/shard_map/intra/pallas_call | solution.py:353
  47.3 4.4 %collective-permute-start.7 = (f32[128,512]{1,0:T(8,128)S(1)}, f32[128,512]{1,0:T(8,128)S(1)}, u32[]{:S(2)}, u32[]{:S(2)}) collective-permute-start(f32[128,512]{1,0:T(8,128)S(1)} %add_add_fusion.1), channel_id=1, source_target_pairs={{0,8},{4,12},{8,0},{12,4},{16,24},{20,28},{24,16},{28,20},{1,9},{5... | collective-permute-start | bytes 786440 | tf_op jit(solution)/shard_map/ppermute | solution.py:489
  52.8 1.4 %collective-permute-start.15 = (f32[128,512]{1,0:T(8,128)S(1)}, f32[128,512]{1,0:T(8,128)S(1)}, u32[]{:S(2)}, u32[]{:S(2)}) collective-permute-start(f32[128,512]{1,0:T(8,128)S(1)} %get-tuple-element.176), channel_id=1, source_target_pairs={{0,4},{4,0},{8,12},{12,8},{16,20},{20,16},{24,28},{28,24},{1,5},{5... | collective-permute-start | bytes 786440 | tf_op jit(solution)/shard_map/ppermute | solution.py:489
  54.2 1.6 %intra.7 = (f32[256,512]{1,0:T(8,128)S(1)}, bf16[256,512]{1,0:T(8,128)(2,1)S(1)}, bf16[256,512]{1,0:T(8,128)(2,1)S(1)}, f32[8,256]{1,0:T(8,128)S(1)}, f32[256,128]{1,0:T(8,128)S(1)}, /*index=5*/f32[256,128]{1,0:T(8,128)S(1)}) custom-call(f32[32,256]{1,0:T(8,128)S(1)} %copy-done.7, f32[4,256,8]{2,1,0:T(8,128)S(1)} %copy-done.3, f32[4,256,8]{2,1,0:T(8,128)S(1)} %copy-done, ...), custom_call_target="tpu_custom_call" | custom-call | flops 134217728 | bytes 1048576 | tf_op jit(solution)/shard_map/intra/pallas_call | solution.py:353
  56.4 1.4 %collective-permute-start.17 = (f32[128,512]{1,0:T(8,128)S(1)}, f32[128,512]{1,0:T(8,128)S(1)}, u32[]{:S(2)}, u32[]{:S(2)}) collective-permute-start(f32[128,512]{1,0:T(8,128)S(1)} %get-tuple-element.178), channel_id=1, source_target_pairs={{0,4},{4,0},{8,12},{12,8},{16,20},{20,16},{24,28},{28,24},{1,5},{5... | collective-permute-start | bytes 786440 | tf_op jit(solution)/shard_map/ppermute | solution.py:489
  57.9 2.4 %collective-permute-start.13 = (f32[128,512]{1,0:T(8,128)S(1)}, f32[128,512]{1,0:T(8,128)S(1)}, u32[]{:S(2)}, u32[]{:S(2)}) collective-permute-start(f32[128,512]{1,0:T(8,128)S(1)} %add_add_fusion), channel_id=1, source_target_pairs={{0,8},{4,12},{8,0},{12,4},{16,24},{20,28},{24,16},{28,20},{1,9},{5... | collective-permute-start | bytes 786440 | tf_op jit(solution)/shard_map/ppermute | solution.py:489
  61.1 2.5 %collective-permute-done.17 = f32[128,512]{1,0:T(8,128)S(1)} collective-permute-done((f32[128,512]{1,0:T(8,128)S(1)}, f32[128,512]{1,0:T(8,128)S(1)}, u32[]{:S(2)}, u32[]{:S(2)}) %collective-permute-start.17) | collective-permute-done | bytes 262176 | tf_op jit(solution)/shard_map/ppermute | solution.py:489
  66.8 1.6 %collective-permute-start.19 = (f32[2,64,128]{2,1,0:T(8,128)S(1)}, f32[2,64,128]{2,1,0:T(8,128)S(1)}, u32[]{:S(2)}, u32[]{:S(2)}) collective-permute-start(f32[2,64,128]{2,1,0:T(8,128)S(1)} %get-tuple-element.173), channel_id=1, source_target_pairs={{0,2},{1,3},{2,0},{3,1},{4,6},{5,7},{6,4},{7,5},{8,10},{9,11},{10,... | collective-permute-start | bytes 196616 | tf_op jit(solution)/shard_map/ppermute | solution.py:635
  68.6 1.1 %pad_maximum_fusion = bf16[256,2048]{1,0:T(8,128)(2,1)} fusion(bf16[256,512]{1,0:T(8,128)(2,1)S(1)} %get-tuple-element.127, bf16[256,512]{1,0:T(8,128)(2,1)S(1)} %get-tuple-element.126, bf16[256,512]{1,0:T(8,128)(2,1)S(1)} %get-tuple-element.125, bf16[256,512]{1,0:T(8,128)(2,1)S(1)} %get-tuple-element.103), kind=kLoop, calls=%fused_computation | loop fusion | flops 4194304 | bytes 2097152 | tf_op jit(solution)/shard_map/concatenate | solution.py:621
  71.3 1.1 %collective-permute-done.20 = f32[2,64,128]{2,1,0:T(8,128)S(1)} collective-permute-done((f32[2,64,128]{2,1,0:T(8,128)S(1)}, f32[2,64,128]{2,1,0:T(8,128)S(1)}, u32[]{:S(2)}, u32[]{:S(2)}) %collective-permute-start.20) | collective-permute-done | bytes 65568 | tf_op jit(solution)/shard_map/ppermute | solution.py:635
  (85 shorter events, 14.4 us)
Async XLA Ops:
  6.2 21.1 %copy-start.13 = (f32[128,512]{1,0:T(8,128)S(1)}, f32[128,512]{1,0:T(8,128)}, u32[]{:S(2)}) copy-start(f32[128,512]{1,0:T(8,128)} %get-tuple-element.88) | copy-start | bytes 786436
  6.2 8.5 %collective-permute-start.1 = (f32[1,2048]{1,0:T(1,128)}, f32[1,2048]{1,0:T(1,128)S(1)}, u32[]{:S(2)}, u32[]{:S(2)}) collective-permute-start(f32[1,2048]{1,0:T(1,128)} %get-tuple-element.76.total_ref), channel_id=1, source_target_pairs={{4,8},{12,16},{20,24},{8,4},{16,12},{24,20},{5,9},{13,17},{21,25},... | collective-permute-start | bytes 24584 | tf_op jit(solution)/shard_map/ppermute | solution.py:489
  7.0 7.7 %collective-permute-start = (f32[1,2048]{1,0:T(1,128)}, f32[1,2048]{1,0:T(1,128)S(1)}, u32[]{:S(2)}, u32[]{:S(2)}) collective-permute-start(f32[1,2048]{1,0:T(1,128)} %get-tuple-element.76.total_ref), channel_id=1, source_target_pairs={{0,4},{4,0},{8,12},{12,8},{16,20},{20,16},{24,28},{28,24},{1,5},{5... | collective-permute-start | bytes 24584 | tf_op jit(solution)/shard_map/ppermute | solution.py:489
  12.8 7.7 %collective-permute-start.2 = (f32[128,512]{1,0:T(8,128)}, f32[128,512]{1,0:T(8,128)S(1)}, u32[]{:S(2)}, u32[]{:S(2)}) collective-permute-start(f32[128,512]{1,0:T(8,128)} %get-tuple-element.77), channel_id=1, source_target_pairs={{0,8},{4,12},{8,0},{12,4},{16,24},{20,28},{24,16},{28,20},{1,9},{5... | collective-permute-start | bytes 786440 | tf_op jit(solution)/shard_map/ppermute | solution.py:489
  14.4 15.1 %collective-permute-start.4 = (f32[256,512]{1,0:T(8,128)}, f32[256,512]{1,0:T(8,128)S(1)}, u32[]{:S(2)}, u32[]{:S(2)}) collective-permute-start(f32[256,512]{1,0:T(8,128)} %get-tuple-element.79), channel_id=1, source_target_pairs={{0,4},{4,0},{8,12},{12,8},{16,20},{20,16},{24,28},{28,24},{1,5},{5... | collective-permute-start | bytes 1572872 | tf_op jit(solution)/shard_map/ppermute | solution.py:489
  16.3 22.4 %collective-permute-start.10 = (f32[256,512]{1,0:T(8,128)}, f32[256,512]{1,0:T(8,128)S(1)}, u32[]{:S(2)}, u32[]{:S(2)}) collective-permute-start(f32[256,512]{1,0:T(8,128)} %get-tuple-element.91), channel_id=1, source_target_pairs={{0,4},{4,0},{8,12},{12,8},{16,20},{20,16},{24,28},{28,24},{1,5},{5... | collective-permute-start | bytes 1572872 | tf_op jit(solution)/shard_map/ppermute | solution.py:489
  20.5 6.8 %collective-permute-start.8 = (f32[128,512]{1,0:T(8,128)}, f32[128,512]{1,0:T(8,128)S(1)}, u32[]{:S(2)}, u32[]{:S(2)}) collective-permute-start(f32[128,512]{1,0:T(8,128)} %get-tuple-element.88), channel_id=1, source_target_pairs={{0,8},{4,12},{8,0},{12,4},{16,24},{20,28},{24,16},{28,20},{1,9},{5... | collective-permute-start | bytes 786440 | tf_op jit(solution)/shard_map/ppermute | solution.py:489
  23.2 5.0 %collective-permute-start.3 = (f32[128,512]{1,0:T(8,128)S(1)}, f32[128,512]{1,0:T(8,128)S(1)}, u32[]{:S(2)}, u32[]{:S(2)}) collective-permute-start(f32[128,512]{1,0:T(8,128)S(1)} %get-tuple-element.165), channel_id=1, source_target_pairs={{8,16},{12,20},{16,8},{20,12},{9,17},{13,21},{17,9},{21,13},{10,18... | collective-permute-start | bytes 786440 | tf_op jit(solution)/shard_map/ppermute | solution.py:489
  27.3 11.4 %copy-start.9 = (f32[256,512]{1,0:T(8,128)S(1)}, f32[256,512]{1,0:T(8,128)}, u32[]{:S(2)}) copy-start(f32[256,512]{1,0:T(8,128)} %get-tuple-element.91) | copy-start | bytes 1572868
  27.3 11.4 %copy-start.11 = (f32[128,512]{1,0:T(8,128)S(1)}, f32[128,512]{1,0:T(8,128)}, u32[]{:S(2)}) copy-start(f32[128,512]{1,0:T(8,128)} %get-tuple-element.89) | copy-start | bytes 786436
  27.4 11.3 %collective-permute-start.9 = (f32[128,512]{1,0:T(8,128)S(1)}, f32[128,512]{1,0:T(8,128)S(1)}, u32[]{:S(2)}, u32[]{:S(2)}) collective-permute-start(f32[128,512]{1,0:T(8,128)S(1)} %get-tuple-element.167), channel_id=1, source_target_pairs={{8,16},{12,20},{16,8},{20,12},{9,17},{13,21},{17,9},{21,13},{10,18... | collective-permute-start | bytes 786440 | tf_op jit(solution)/shard_map/ppermute | solution.py:489
  29.6 9.8 %collective-permute-start.5 = (f32[128,512]{1,0:T(8,128)S(1)}, f32[128,512]{1,0:T(8,128)S(1)}, u32[]{:S(2)}, u32[]{:S(2)}) collective-permute-start(f32[128,512]{1,0:T(8,128)S(1)} %add_select_fusion.1), channel_id=1, source_target_pairs={{0,8},{4,12},{8,0},{12,4},{16,24},{20,28},{24,16},{28,20},{1,9},{5... | collective-permute-start | bytes 786440 | tf_op jit(solution)/shard_map/ppermute | solution.py:489
  38.9 8.4 %collective-permute-start.11 = (f32[128,512]{1,0:T(8,128)S(1)}, f32[128,512]{1,0:T(8,128)S(1)}, u32[]{:S(2)}, u32[]{:S(2)}) collective-permute-start(f32[128,512]{1,0:T(8,128)S(1)} %add_select_fusion), channel_id=1, source_target_pairs={{0,8},{4,12},{8,0},{12,4},{16,24},{20,28},{24,16},{28,20},{1,9},{5... | collective-permute-start | bytes 786440 | tf_op jit(solution)/shard_map/ppermute | solution.py:489
  39.5 7.8 %collective-permute-start.6 = (f32[128,512]{1,0:T(8,128)S(1)}, f32[128,512]{1,0:T(8,128)S(1)}, u32[]{:S(2)}, u32[]{:S(2)}) collective-permute-start(f32[128,512]{1,0:T(8,128)S(1)} %multiply_add_fusion.14), channel_id=1, source_target_pairs={{8,16},{12,20},{16,8},{20,12},{9,17},{13,21},{17,9},{21,13},{10,18... | collective-permute-start | bytes 786440 | tf_op jit(solution)/shard_map/ppermute | solution.py:489
  40.2 21.0 %collective-permute-start.16 = (f32[128,512]{1,0:T(8,128)S(1)}, f32[128,512]{1,0:T(8,128)S(1)}, u32[]{:S(2)}, u32[]{:S(2)}) collective-permute-start(f32[128,512]{1,0:T(8,128)S(1)} %get-tuple-element.166), channel_id=1, source_target_pairs={{0,4},{4,0},{8,12},{12,8},{16,20},{20,16},{24,28},{28,24},{1,5},{5... | collective-permute-start | bytes 786440 | tf_op jit(solution)/shard_map/ppermute | solution.py:489
  42.5 22.1 %collective-permute-start.14 = (f32[128,512]{1,0:T(8,128)S(1)}, f32[128,512]{1,0:T(8,128)S(1)}, u32[]{:S(2)}, u32[]{:S(2)}) collective-permute-start(f32[128,512]{1,0:T(8,128)S(1)} %get-tuple-element.168), channel_id=1, source_target_pairs={{0,4},{4,0},{8,12},{12,8},{16,20},{20,16},{24,28},{28,24},{1,5},{5... | collective-permute-start | bytes 786440 | tf_op jit(solution)/shard_map/ppermute | solution.py:489
  47.3 8.8 %collective-permute-start.7 = (f32[128,512]{1,0:T(8,128)S(1)}, f32[128,512]{1,0:T(8,128)S(1)}, u32[]{:S(2)}, u32[]{:S(2)}) collective-permute-start(f32[128,512]{1,0:T(8,128)S(1)} %add_add_fusion.1), channel_id=1, source_target_pairs={{0,8},{4,12},{8,0},{12,4},{16,24},{20,28},{24,16},{28,20},{1,9},{5... | collective-permute-start | bytes 786440 | tf_op jit(solution)/shard_map/ppermute | solution.py:489
  51.9 5.9 %collective-permute-start.12 = (f32[128,512]{1,0:T(8,128)S(1)}, f32[128,512]{1,0:T(8,128)S(1)}, u32[]{:S(2)}, u32[]{:S(2)}) collective-permute-start(f32[128,512]{1,0:T(8,128)S(1)} %get-tuple-element.175), channel_id=1, source_target_pairs={{8,16},{12,20},{16,8},{20,12},{9,17},{13,21},{17,9},{21,13},{10,18... | collective-permute-start | bytes 786440 | tf_op jit(solution)/shard_map/ppermute | solution.py:489
  52.8 11.8 %collective-permute-start.15 = (f32[128,512]{1,0:T(8,128)S(1)}, f32[128,512]{1,0:T(8,128)S(1)}, u32[]{:S(2)}, u32[]{:S(2)}) collective-permute-start(f32[128,512]{1,0:T(8,128)S(1)} %get-tuple-element.176), channel_id=1, source_target_pairs={{0,4},{4,0},{8,12},{12,8},{16,20},{20,16},{24,28},{28,24},{1,5},{5... | collective-permute-start | bytes 786440 | tf_op jit(solution)/shard_map/ppermute | solution.py:489
  56.4 7.2 %collective-permute-start.17 = (f32[128,512]{1,0:T(8,128)S(1)}, f32[128,512]{1,0:T(8,128)S(1)}, u32[]{:S(2)}, u32[]{:S(2)}) collective-permute-start(f32[128,512]{1,0:T(8,128)S(1)} %get-tuple-element.178), channel_id=1, source_target_pairs={{0,4},{4,0},{8,12},{12,8},{16,20},{20,16},{24,28},{28,24},{1,5},{5... | collective-permute-start | bytes 786440 | tf_op jit(solution)/shard_map/ppermute | solution.py:489
  57.9 7.7 %collective-permute-start.13 = (f32[128,512]{1,0:T(8,128)S(1)}, f32[128,512]{1,0:T(8,128)S(1)}, u32[]{:S(2)}, u32[]{:S(2)}) collective-permute-start(f32[128,512]{1,0:T(8,128)S(1)} %add_add_fusion), channel_id=1, source_target_pairs={{0,8},{4,12},{8,0},{12,4},{16,24},{20,28},{24,16},{28,20},{1,9},{5... | collective-permute-start | bytes 786440 | tf_op jit(solution)/shard_map/ppermute | solution.py:489
  66.7 4.0 %collective-permute-start.18 = (f32[2,64,128]{2,1,0:T(8,128)S(1)}, f32[2,64,128]{2,1,0:T(8,128)S(1)}, u32[]{:S(2)}, u32[]{:S(2)}) collective-permute-start(f32[2,64,128]{2,1,0:T(8,128)S(1)} %get-tuple-element.172), channel_id=1, source_target_pairs={{0,1},{1,0},{2,3},{3,2},{4,5},{5,4},{6,7},{7,6},{8,9},{9,8},{10,11... | collective-permute-start | bytes 196616 | tf_op jit(solution)/shard_map/ppermute | solution.py:635
  66.8 4.5 %collective-permute-start.19 = (f32[2,64,128]{2,1,0:T(8,128)S(1)}, f32[2,64,128]{2,1,0:T(8,128)S(1)}, u32[]{:S(2)}, u32[]{:S(2)}) collective-permute-start(f32[2,64,128]{2,1,0:T(8,128)S(1)} %get-tuple-element.173), channel_id=1, source_target_pairs={{0,2},{1,3},{2,0},{3,1},{4,6},{5,7},{6,4},{7,5},{8,10},{9,11},{10,... | collective-permute-start | bytes 196616 | tf_op jit(solution)/shard_map/ppermute | solution.py:635
  68.4 4.0 %collective-permute-start.20 = (f32[2,64,128]{2,1,0:T(8,128)S(1)}, f32[2,64,128]{2,1,0:T(8,128)S(1)}, u32[]{:S(2)}, u32[]{:S(2)}) collective-permute-start(f32[2,64,128]{2,1,0:T(8,128)S(1)} %get-tuple-element.174), channel_id=1, source_target_pairs={{0,3},{1,2},{2,1},{3,0},{4,7},{5,6},{6,5},{7,4},{8,11},{9,10},{10,... | collective-permute-start | bytes 196616 | tf_op jit(solution)/shard_map/ppermute | solution.py:635
  (11 other events, 54.1 us)
